TPU v7x, 1024 devices: a whole 4x8x16 slice. The times are simulated.
1024 devices in a mesh: exp: 32 (over x, y), seq: 32 (over z, core).
Axes of the slice: x: 4, y: 8, z: 16, core: 2. Of those that a mesh axis runs over, the one named last changes fastest.
Arguments:
- output_gradient: bfloat16 [4096, 4096], P('exp', 'seq'), may hold values from -6 to 6
- routed_expert_index: int32 [4096, 8], P('exp'), may hold values from 0 to 127, all different within a row; in each aligned block of 128 rows (0 to 127, 128 to 255, ...) at most 12 rows name the same one
- combine: bfloat16 [4096, 8], P('exp'), may hold values from 0.049804688 to 0.5
- token_task_index: int32 [4096], P('exp'), may hold values from 0 to 7
- saved_gate_input: bfloat16 [128, 32, 12, 1536], P('exp', None, None, 'seq'), may hold values from -6 to 6
- saved_up_input: bfloat16 [128, 32, 12, 1536], P('exp', None, None, 'seq'), may hold values from -6 to 6
- down_weight: bfloat16 [128, 1536, 4096], P('exp', None, 'seq'), may hold values from -0.15625 to 0.15625
- adapter_first_factor: bfloat16 [128, 8, 1536, 64], P('exp', None, 'seq'), may hold values from -0.15625 to 0.15625
- adapter_second_factor: bfloat16 [128, 8, 64, 4096], P('exp', None, None, 'seq'), may hold values from -0.1875 to 0.1875
Outputs:
- grad_gate_pre: bfloat16 [128, 32, 12, 1536], P('exp', None, None, 'seq')
- grad_up_pre: bfloat16 [128, 32, 12, 1536], P('exp', None, None, 'seq')
- grad_lora_a: bfloat16 [128, 8, 1536, 64], P('exp', None, 'seq')
- grad_lora_b: bfloat16 [128, 8, 64, 4096], P('exp', None, None, 'seq')
- grad_combine: float32 [4096, 8], P('exp')
Inputs may be any that keep to these rules, and one draw needn't show every extreme that they name: `routed_expert_index`: each token names 8 different experts; among the tokens of one exp index (aligned blocks of 128 tokens) no expert is named more than 12 times, a bound that some block reaches.
All inputs are finite; a program needn't handle non-finite values.
Results may differ from a plain program's by a relative error of at most 0.015.
Values may be sent and summed in bfloat16 or wider, within the bound.
No kernel may reach another device: no remote copies, remote signals or barrier semaphores. Data moves between devices by JAX's collectives and lax.ppermute only.
A program may use at most 128 MiB of HBM per device.

v0:
```python
import jax
import jax.numpy as jnp
from jax import lax
from jax.sharding import PartitionSpec as P


def on_device(
    output_gradient,
    routed_expert_index,
    combine,
    token_task_index,
    saved_gate_input,
    saved_up_input,
    down_weight,
    adapter_first_factor,
    adapter_second_factor,
):
    exp_width = lax.axis_size("exp")
    exp_local, source_count, most_rows, ff_piece = saved_gate_input.shape
    tok_count, top_count = routed_expert_index.shape
    task_row_count = adapter_first_factor.shape[1]
    expert_count = exp_local * exp_width
    per_expert = source_count * most_rows
    total_slots = exp_local * per_expert
    flat_ids = routed_expert_index.reshape(-1)
    onehot = (flat_ids[:, None] == jnp.arange(expert_count, dtype=jnp.int32)[None, :]).astype(
        jnp.int32
    )
    before = jnp.cumsum(onehot, axis=0) - onehot
    place_rank = jnp.sum(before * onehot, axis=1)
    slot_of = flat_ids % exp_local * per_expert + flat_ids // exp_local * most_rows + place_rank
    picker = slot_of[None, :] == jnp.arange(total_slots, dtype=jnp.int32)[:, None]
    picker_half = picker.astype(jnp.bfloat16)
    token_rows = jnp.repeat(output_gradient, top_count, axis=0)
    send_rows = jnp.dot(picker_half, token_rows, preferred_element_type=jnp.float32).astype(
        jnp.bfloat16
    )
    send_rows = send_rows.reshape(exp_local, source_count, most_rows, -1)
    send_gate = jnp.dot(
        picker_half, combine.reshape(-1), preferred_element_type=jnp.float32
    ).astype(jnp.bfloat16)
    task_rep = jnp.repeat(token_task_index, top_count).astype(jnp.bfloat16)
    send_task = jnp.dot(picker_half, task_rep, preferred_element_type=jnp.float32).astype(
        jnp.bfloat16
    )
    recv_rows, recv_gate, recv_task = (
        lax.all_to_all(send_rows, "exp", split_axis=1, concat_axis=1, tiled=True),
        lax.all_to_all(
            send_gate.reshape(exp_local, source_count, most_rows),
            "exp",
            split_axis=1,
            concat_axis=1,
            tiled=True,
        ),
        lax.all_to_all(
            send_task.reshape(exp_local, source_count, most_rows),
            "exp",
            split_axis=1,
            concat_axis=1,
            tiled=True,
        ),
    )
    input_row_block = recv_rows.reshape(exp_local, per_expert, -1)
    gate_activated = recv_gate.reshape(exp_local, per_expert).astype(jnp.float32)
    task_in = recv_task.reshape(exp_local, per_expert).astype(jnp.int32)
    task_mask = (task_in[..., None] == jnp.arange(task_row_count, dtype=jnp.int32)).astype(
        jnp.float32
    )
    gate_f = saved_gate_input.reshape(exp_local, per_expert, ff_piece).astype(jnp.float32)
    up_f = saved_up_input.reshape(exp_local, per_expert, ff_piece).astype(jnp.float32)
    sigmoid_gate = jax.nn.sigmoid(gate_f)
    activation = gate_f * sigmoid_gate
    hidden_state = (activation * up_f).astype(jnp.bfloat16)
    latent_rows_full = jnp.einsum(
        "ujy,upyg->ujpg", hidden_state, adapter_first_factor, preferred_element_type=jnp.float32
    )
    lat_part = jnp.sum(latent_rows_full * task_mask[..., None], axis=2)
    query_latent_full = jnp.einsum(
        "akg,amqg->akmq", input_row_block, adapter_second_factor, preferred_element_type=jnp.float32
    )
    ql_part = jnp.sum(query_latent_full * task_mask[..., None], axis=2)
    back_hidden = lax.psum_scatter(
        jnp.einsum(
            "efd,esd->fes", down_weight, input_row_block, preferred_element_type=jnp.float32
        ),
        "seq",
        scatter_dimension=0,
        tiled=True,
    )
    back_hidden = jnp.transpose(back_hidden, (1, 2, 0))
    output_part = jnp.einsum(
        "esf,efd->esd",
        lax.all_gather(hidden_state, "seq", axis=2, tiled=True),
        down_weight,
        preferred_element_type=jnp.float32,
    )
    weight_part = jnp.sum(output_part * input_row_block.astype(jnp.float32), axis=2)
    lat_sum, ql_sum, weight_sum = lax.psum((lat_part, ql_part, weight_part), "seq")
    latent = lat_sum.astype(jnp.bfloat16)
    down_weight_gradient = weight_sum + jnp.sum(latent.astype(jnp.float32) * ql_sum, axis=2)
    scaled_lat = (gate_activated[..., None] * ql_sum).astype(jnp.bfloat16)
    spread_update = (task_mask[..., None] * scaled_lat.astype(jnp.float32)[:, :, None, :]).astype(
        jnp.bfloat16
    )
    hidden_grad = gate_activated[..., None] * back_hidden + jnp.einsum(
        "unqk,uqjk->unj", spread_update, adapter_first_factor, preferred_element_type=jnp.float32
    )
    gate_input_gradient = (
        hidden_grad * up_f * sigmoid_gate * (1.0 + gate_f * (1.0 - sigmoid_gate))
    ).astype(jnp.bfloat16)
    up_input_gradient = (hidden_grad * activation).astype(jnp.bfloat16)
    first_factor_gradient = jnp.einsum(
        "estr,esf->etfr", spread_update, hidden_state, preferred_element_type=jnp.float32
    ).astype(jnp.bfloat16)
    weighted_lat = (gate_activated[..., None] * latent.astype(jnp.float32)).astype(jnp.bfloat16)
    spread_z = (task_mask[..., None] * weighted_lat.astype(jnp.float32)[:, :, None, :]).astype(
        jnp.bfloat16
    )
    second_factor_gradient = jnp.einsum(
        "estr,esd->etrd", spread_z, input_row_block, preferred_element_type=jnp.float32
    ).astype(jnp.bfloat16)
    returned_vals = lax.all_to_all(
        down_weight_gradient.reshape(exp_local, source_count, most_rows),
        "exp",
        split_axis=1,
        concat_axis=1,
        tiled=True,
    )
    grad_combine = jnp.dot(
        picker.T.astype(jnp.float32), returned_vals.reshape(-1), precision=lax.Precision.HIGHEST
    )
    grad_combine = grad_combine.reshape(tok_count, top_count)
    shape_out = (exp_local, source_count, most_rows, ff_piece)
    return (
        gate_input_gradient.reshape(shape_out),
        up_input_gradient.reshape(shape_out),
        first_factor_gradient,
        second_factor_gradient,
        grad_combine,
    )


def solution(mesh):
    placed = (
        P("exp", "seq"),
        P("exp", None),
        P("exp", None),
        P("exp"),
        P("exp", None, None, "seq"),
        P("exp", None, None, "seq"),
        P("exp", None, "seq"),
        P("exp", None, "seq", None),
        P("exp", None, None, "seq"),
    )
    return jax.shard_map(
        on_device,
        mesh=mesh,
        in_specs=placed,
        out_specs=(
            P("exp", None, None, "seq"),
            P("exp", None, None, "seq"),
            P("exp", None, "seq", None),
            P("exp", None, None, "seq"),
            P("exp", None),
        ),
        check_vma=False,
    )
```

profile of v0, /device:TPU:1, one launch (start us, length us, event | category | flops | bytes accessed | tf_op | source)
XLA Modules:
  0.0 543.8 jit_solution(639675109831967419)
XLA Ops:
  7.2 0.9 copy.91
  8.1 0.1 eq.81
  8.2 0.1 reshape.169
  8.3 0.1 copy.93
  8.4 0.2 fusion.37
  8.7 0.1 copy.94
  8.8 0.4 fusion.36
  9.3 0.1 reshape.187
  9.4 1.2 fusion.34
  10.5 0.1 reshape.176
  10.7 0.6 copy.103
  11.3 10.5 %all-to-all-start.2 = ((bf16[4,32,12]{2,0,1:T(4,128)(2,1)}), bf16[4,32,12]{2,0,1:T(4,128)(2,1)S(1)}, u32[]{:S(2)}, u32[]{:S(2)}) async-start(bf16[4,32,12]{2,0,1:T(4,128)(2,1)} %copy.103), calls=%async_computation.2 | async-start | bytes 65536 | tf_op jit(solution)/shard_map/all_to_all | solution.py:55
  21.8 1.2 fusion.12
  23.1 1.1 copy.99
  24.2 6.4 %all-to-all-done.2 = bf16[4,32,12]{2,0,1:T(4,128)(2,1)S(1)} async-done(((bf16[4,32,12]{2,0,1:T(4,128)(2,1)}), bf16[4,32,12]{2,0,1:T(4,128)(2,1)S(1)}, u32[]{:S(2)}, u32[]{:S(2)}) %all-to-all-start.2) | async-done | bytes 3104 | tf_op jit(solution)/shard_map/all_to_all | solution.py:55
  30.6 3.9 all-to-all-start.1
  34.5 0.1 copy.104
  34.7 0.1 copy.105
  34.8 0.1 reshape.182
  34.9 9.8 %all-to-all-done.1 = bf16[4,32,12,128]{3,0,2,1:T(4,128)(2,1)S(1)} async-done(((bf16[4,32,12,128]{3,0,2,1:T(4,128)(2,1)}), bf16[4,32,12,128]{3,0,2,1:T(4,128)(2,1)S(1)}, u32[]{:S(2)}, u32[]{:S(2)}) %all-to-all-start.1) | async-done | bytes 393248 | tf_op jit(solution)/shard_map/all_to_all | solution.py:47
  44.7 0.3 copy.124
  45.0 5.1 convolution_bitcast_fusion
  50.1 12.0 %copy.101 = f32[1536,4,384]{2,1,0:T(4,128)} copy(f32[1536,4,384]{0,2,1:T(8,128)} %convolution_bitcast_fusion) | data formatting | bytes 18874368 | tf_op jit(solution)/shard_map/efd,esd->fes/transpose | solution.py:83
  62.1 1.3 multiply_reduce_fusion.1
  63.5 0.7 copy-done.6
  64.1 0.1 copy.95
  64.3 0.1 reshape.185
  64.4 1.2 fusion.33
  65.5 0.1 reshape.172
  65.6 0.6 copy.96
  66.3 5.2 all-to-all-start
  71.5 0.2 all-gather.2.cloned.1.call-start
  71.7 1.3 copy.107
  73.0 0.3 copy.108
  73.3 1.3 copy.109
  74.6 1.0 copy.110
  75.6 1.3 dynamic-slice
  77.5 2.7 all-to-all-done
  80.2 0.1 copy.97
  80.4 0.1 copy.98
  80.5 0.1 reshape.181
  80.6 235.5 %all-reduce.6.cloned.1.call-done = (f32[4,384,64]{1,2,0:T(8,128)}, f32[1536,4,384]{2,1,0:T(4,128)}) async-done(((f32[4,384,64]{1,2,0:T(8,128)}, f32[1536,4,384]{2,1,0:T(4,128)}), (f32[4,384,64]{1,2,0:T(8,128)}, f32[1536,4,384]{2,1,0:T(4,128)})) %all-reduce.6.cloned.1.call-update) | async-done | bytes 9830416 | tf_op jit(solution)/shard_map/psum | solution.py:98
  316.1 1.0 fusion.46
  317.1 1.0 constant_dynamic-slice_fusion
  318.1 2.3 multiply_convert_fusion.16
  320.4 0.7 copy.121
  321.3 0.7 fusion.53
  322.0 1.6 multiply_reduce_fusion
  323.6 1.2 copy.112
  324.8 0.8 copy.127
  325.6 1.1 copy.114
  326.8 0.8 copy.128
  327.6 2.8 fusion.27
  330.4 69.1 %all-gather.2.cloned.1.call-done = bf16[4,384,1536]{1,0,2:T(4,128)(2,1)} async-done(((bf16[4,384,48]{1,0,2:T(4,128)(2,1)}), bf16[4,384,1536]{1,0,2:T(4,128)(2,1)}) %all-gather.2.cloned.1.call-update) | async-done | bytes 4718608 | tf_op jit(solution)/shard_map/all_gather | solution.py:93
  399.5 3.5 fusion.28
  403.0 93.3 %all-reduce.7 = (bf16[4,384,64]{1,2,0:T(8,128)(2,1)S(1)}, f32[4,384]{1,0:T(4,128)S(1)}) all-reduce(f32[4,384,64]{1,2,0:T(8,128)S(1)} %multiply_reduce_fusion, f32[4,384]{1,0:T(4,128)S(1)} %fusion.28), channel_id=1, replica_groups=mesh['exp'=32,'seq'=32] {'seq'}, use_global_device_ids=true, to_apply=%region_7.8 | all-reduce | flops 99840 | bytes 602112 | tf_op jit(solution)/shard_map/psum | solution.py:98
  496.4 0.1 reshape.179
  496.6 0.7 copy.125
  497.2 9.5 %all-to-all-start.3 = ((f32[4,32,12]{2,0,1:T(4,128)}), f32[4,32,12]{2,0,1:T(4,128)S(1)}, u32[]{:S(2)}, u32[]{:S(2)}) async-start(f32[4,32,12]{2,0,1:T(4,128)} %copy.125), calls=%async_computation.3 | async-start | bytes 131072 | tf_op jit(solution)/shard_map/all_to_all | solution.py:122
  506.7 2.2 fusion.22
  508.9 6.5 %all-to-all-done.3 = f32[4,32,12]{2,0,1:T(4,128)S(1)} async-done(((f32[4,32,12]{2,0,1:T(4,128)}), f32[4,32,12]{2,0,1:T(4,128)S(1)}, u32[]{:S(2)}, u32[]{:S(2)}) %all-to-all-start.3) | async-done | bytes 6176 | tf_op jit(solution)/shard_map/all_to_all | solution.py:122
  515.4 0.1 reshape.193
  515.5 20.8 %fusion.4 = f32[1,128,8]{2,0,1:T(1,128)S(1)} fusion(f32[1536,1,1]{0,1,2:T(1,128)S(1)} %reshape.193, s32[128,8]{1,0:T(8,128)S(1)} %copy-done.3), kind=kOutput, calls=%fused_computation.6 | convolution fusion | flops 20447232 | bytes 14336 | tf_op jit(solution)/shard_map/dot_general | solution.py:129
  536.3 0.7 copy.134
  (36 shorter events, 0.6 us)
Async XLA Ops:
  7.2 37.8 %copy-start = (bf16[4,1536,128]{2,1,0:T(8,128)(2,1)S(1)}, bf16[4,1536,128]{2,1,0:T(8,128)(2,1)}, u32[]{:S(2)}) copy-start(bf16[4,1536,128]{2,1,0:T(8,128)(2,1)} %param.15) | copy-start | bytes 4718596
  7.2 2.0 copy-start.9
  7.2 14.6 %copy-start.8 = (bf16[128,128]{1,0:T(8,128)(2,1)S(1)}, bf16[128,128]{1,0:T(8,128)(2,1)}, u32[]{:S(2)}) copy-start(bf16[128,128]{1,0:T(8,128)(2,1)} %param.9) | copy-start | bytes 98308
  11.3 19.3 %all-to-all-start.2 = ((bf16[4,32,12]{2,0,1:T(4,128)(2,1)}), bf16[4,32,12]{2,0,1:T(4,128)(2,1)S(1)}, u32[]{:S(2)}, u32[]{:S(2)}) async-start(bf16[4,32,12]{2,0,1:T(4,128)(2,1)} %copy.103), calls=%async_computation.2 | async-start | bytes 65536 | tf_op jit(solution)/shard_map/all_to_all | solution.py:55
  30.6 14.1 %all-to-all-start.1 = ((bf16[4,32,12,128]{3,0,2,1:T(4,128)(2,1)}), bf16[4,32,12,128]{3,0,2,1:T(4,128)(2,1)S(1)}, u32[]{:S(2)}, u32[]{:S(2)}) async-start(bf16[4,32,12,128]{3,0,2,1:T(4,128)(2,1)} %copy.99), calls=%async_computation.1 | async-start | bytes 786432 | tf_op jit(solution)/shard_map/all_to_all | solution.py:47
  34.5 281.6 %all-reduce.6.cloned.1.call-start = ((), (), s32[]{:S(2)}) async-start(), calls=%async_computation.5 | async-start | bytes 19660800 | tf_op jit(solution)/shard_map/psum | solution.py:98
  34.9 27.2 %copy-start.4 = (f32[4,384,8]{1,2,0:T(8,128)}, f32[4,384,8]{1,2,0:T(8,128)S(1)}, u32[]{:S(2)}) copy-start(f32[4,384,8]{1,2,0:T(8,128)S(1)} %fusion.59) | copy-start | bytes 147460
  50.1 12.0 %copy-start.7 = (bf16[4,8,64,128]{3,2,1,0:T(8,128)(2,1)S(1)}, bf16[4,8,64,128]{3,2,1,0:T(8,128)(2,1)}, u32[]{:S(2)}) copy-start(bf16[4,8,64,128]{3,2,1,0:T(8,128)(2,1)} %param.17) | copy-start | bytes 1572868
  63.5 0.7 copy-start.6
  66.3 14.0 %all-to-all-start = ((bf16[4,32,12]{2,0,1:T(4,128)(2,1)}), bf16[4,32,12]{2,0,1:T(4,128)(2,1)S(1)}, u32[]{:S(2)}, u32[]{:S(2)}) async-start(bf16[4,32,12]{2,0,1:T(4,128)(2,1)} %copy.96), calls=%async_computation | async-start | bytes 65536 | tf_op jit(solution)/shard_map/all_to_all | solution.py:48
  71.5 328.0 %all-gather.2.cloned.1.call-start = ((), (), s32[]{:S(2)}) async-start(), calls=%async_computation.4 | async-start | bytes 4866048 | tf_op jit(solution)/shard_map/all_gather | solution.py:93
  75.6 246.4 %copy-start.5 = (f32[4,384,8]{1,2,0:T(8,128)S(1)}, f32[4,384,8]{1,2,0:T(8,128)}, u32[]{:S(2)}) copy-start(f32[4,384,8]{1,2,0:T(8,128)} %copy-done.4) | copy-start | bytes 147460
  320.4 3.2 copy-start.2
  330.4 165.9 %copy-start.1 = (f32[4,384,64]{1,2,0:T(8,128)S(1)}, f32[4,384,64]{1,2,0:T(8,128)}, u32[]{:S(2)}) copy-start(f32[4,384,64]{1,2,0:T(8,128)} %get-tuple-element.27) | copy-start | bytes 1179652
  403.0 112.5 %copy-start.3 = (s32[128,8]{1,0:T(8,128)S(1)}, s32[128,8]{1,0:T(8,128)}, u32[]{:S(2)}) copy-start(s32[128,8]{1,0:T(8,128)} %fusion.53) | copy-start | bytes 12292
  497.2 18.1 %all-to-all-start.3 = ((f32[4,32,12]{2,0,1:T(4,128)}), f32[4,32,12]{2,0,1:T(4,128)S(1)}, u32[]{:S(2)}, u32[]{:S(2)}) async-start(f32[4,32,12]{2,0,1:T(4,128)} %copy.125), calls=%async_computation.3 | async-start | bytes 131072 | tf_op jit(solution)/shard_map/all_to_all | solution.py:122
Sparse Core Ops, SparseCore 0:
  63.6 252.4 all-reduce.5
  321.3 78.1 all-gather.1
where the time goes:
time: 548 us; the launch traced here: 544 us
  waiting for transfers between devices  330 us (60%)
  blocking collectives  93.3 us (17%)
  matrix products  43.1 us (8%)
  local copies, waits for them, and re-layouts  30.5 us (6%)
  starting transfers between devices  29.3 us (5%)
  between operations  15 us (3%)
    psum x1, waiting for transfers between devices, on_device(): lax.psum((lat_part, ql_part, weight_part), 'seq')  236 us
    psum x1, blocking collectives, on_device(): lax.psum((lat_part, ql_part, weight_part), 'seq')  93.3 us
    all_gather x1, waiting for transfers between devices, on_device(): lax.all_gather(hidden_state, 'seq', axis=2, tiled=True)  69.1 us
    dot_general x1, matrix products, on_device(): jnp.dot(picker.T.astype(jnp.float32), returned_vals.reshape(-1), precisio...  20.8 us
    transpose x1, local copies, waits for them, and re-layouts, on_device(): jnp.einsum('efd,esd->fes', down_weight, input_row_block, preferred_elemen...  12 us
  transfers between devices with their start and end apart: 6, of which 6 were waited for; matrix products, arithmetic and copies ran while one was open for 4% of the time, Pallas kernels for 0%

commit v1 on v0

v1 whole, which is shorter than its diff:
```python
import jax
import jax.numpy as jnp
from jax import lax
from jax.experimental import pallas as pl
from jax.experimental.pallas import tpu as pltpu
from jax.sharding import Mesh
from jax.sharding import PartitionSpec as P

BF = jnp.bfloat16
F32 = jnp.float32


def back_partial(core, weight, weight_peer, rows, rows_peer):
    exp_local, z_width, _, piece, width = weight.shape
    slots = rows.shape[1]

    def kernel(core_ref, w_ref, wp_ref, x_ref, xp_ref, out_ref):
        nums = (((1,), (1,)), ((), ()))
        own = w_ref[0, :, 0].reshape(z_width * piece, width)
        peer = wp_ref[0].reshape(z_width * piece, width)
        total = lax.dot_general(own, x_ref[0], nums, preferred_element_type=F32)
        total += lax.dot_general(peer, xp_ref[0], nums, preferred_element_type=F32)
        out_ref[:, 0] = total.astype(BF).reshape(z_width, piece, slots)

    return pl.pallas_call(
        kernel,
        out_shape=jax.ShapeDtypeStruct((z_width, exp_local, piece, slots), BF),
        grid_spec=pltpu.PrefetchScalarGridSpec(
            num_scalar_prefetch=1,
            grid=(exp_local,),
            in_specs=[
                pl.BlockSpec((1, z_width, 1, piece, width), lambda e, c: (e, 0, c[0], 0, 0)),
                pl.BlockSpec((1, z_width, piece, width), lambda e, c: (e, 0, 0, 0)),
                pl.BlockSpec((1, slots, width), lambda e, c: (e, 0, 0)),
                pl.BlockSpec((1, slots, width), lambda e, c: (e, 0, 0)),
            ],
            out_specs=pl.BlockSpec((z_width, 1, piece, slots), lambda e, c: (0, e, 0, 0)),
        ),
        name="back_partial",
    )(core.reshape(1), weight, weight_peer, rows, rows_peer)


def on_device(
    output_gradient,
    routed_expert_index,
    combine,
    token_task_index,
    saved_gate_input,
    saved_up_input,
    down_weight,
    adapter_first_factor,
    adapter_second_factor,
):
    exp_width = lax.axis_size("exp")
    z_width = lax.axis_size("z")
    core = lax.axis_index("core")
    z_index = lax.axis_index("z")
    exp_local, source_count, most, piece = saved_gate_input.shape
    tok_count, top = routed_expert_index.shape
    width = output_gradient.shape[1]
    task_count, rank = adapter_first_factor.shape[1], adapter_first_factor.shape[3]
    expert_count = exp_local * exp_width
    per_expert = source_count * most
    total_slots = exp_local * per_expert
    swap = [(0, 1), (1, 0)]

    weight = down_weight.reshape(exp_local, z_width, 2, piece, width)
    weight_peer = lax.ppermute(
        lax.dynamic_index_in_dim(weight, 1 - core, axis=2, keepdims=False), "core", swap
    )

    ids = routed_expert_index.T
    experts = jnp.arange(expert_count, dtype=jnp.int32)
    tokens = jnp.arange(tok_count, dtype=jnp.int32)
    names = ids[:, None, :] == experts[None, :, None]
    named = jnp.any(names, axis=0)
    gates = jnp.sum(jnp.where(names, combine.T[:, None, :].astype(F32), 0.0), axis=0)
    earlier = (tokens[:, None] < tokens[None, :]).astype(BF)
    place = jnp.dot(named.astype(BF), earlier, preferred_element_type=F32)
    place_or = jnp.where(named, place, -1.0).astype(BF)
    row_of = jnp.arange(expert_count * most, dtype=jnp.int32)
    spread = (row_of[:, None] // most == experts[None, :]).astype(BF)
    picked = jnp.dot(spread, place_or, preferred_element_type=F32) == (
        (row_of % most).astype(F32)[:, None]
    )
    send_rows = jnp.dot(picked.astype(BF), output_gradient, preferred_element_type=F32).astype(BF)
    slab = exp_local * most
    extra = -(exp_local + 1) % 8
    send = jnp.concatenate(
        [
            send_rows.reshape(exp_width, slab, width),
            gates.astype(BF).reshape(exp_width, exp_local, tok_count),
            jnp.broadcast_to(token_task_index.astype(BF), (exp_width, 1, tok_count)),
            jnp.zeros((exp_width, extra, tok_count), BF),
        ],
        axis=1,
    )
    received = lax.all_to_all(send, "exp", split_axis=0, concat_axis=0, tiled=True)

    rows = received[:, :slab].transpose(1, 0, 2).reshape(exp_local, per_expert, width)
    rows_peer = lax.ppermute(rows, "core", swap)
    gate_rows = received[:, slab : slab + exp_local].transpose(1, 0, 2)
    used = gate_rows > 0
    place_in = jnp.dot(
        used.astype(BF).reshape(exp_local * source_count, tok_count),
        earlier,
        preferred_element_type=F32,
    ).reshape(exp_local, source_count, tok_count)
    holds = used[:, None] & (
        place_in[:, None] == jnp.arange(most, dtype=jnp.int32).astype(F32)[:, None, None]
    )
    gate_slot = jnp.sum(jnp.where(holds, gate_rows.astype(F32)[:, None], 0.0), axis=3).reshape(
        exp_local, per_expert
    )
    task_rows = received[:, slab + exp_local].astype(F32)
    task_slot = jnp.sum(
        jnp.where(holds, task_rows, 0.0), axis=3
    ).reshape(exp_local, per_expert)
    task_mask = (
        task_slot[..., None] == jnp.arange(task_count, dtype=jnp.int32).astype(F32)
    ).astype(F32)

    partial = back_partial(core.astype(jnp.int32), weight, weight_peer, rows, rows_peer)
    back = lax.psum_scatter(partial, "z", scatter_dimension=0, tiled=True)[0]

    gate_f = saved_gate_input.swapaxes(1, 2).reshape(exp_local, per_expert, piece).astype(F32)
    up_f = saved_up_input.swapaxes(1, 2).reshape(exp_local, per_expert, piece).astype(F32)
    sig = jax.nn.sigmoid(gate_f)
    act = gate_f * sig
    hidden = (act * up_f).astype(BF)

    lat_all = jnp.einsum(
        "ujy,upyg->ujpg", hidden, adapter_first_factor, preferred_element_type=F32
    )
    lat_part = jnp.sum(lat_all * task_mask[..., None], axis=2)
    ql_all = jnp.einsum("akg,amqg->akmq", rows, adapter_second_factor, preferred_element_type=F32)
    ql_part = jnp.sum(ql_all * task_mask[..., None], axis=2)
    both = jnp.concatenate([lat_part, ql_part], axis=2).reshape(2, total_slots // 2, 2 * rank)
    theirs = lax.dynamic_index_in_dim(both, 1 - core, axis=0, keepdims=False)
    mine = lax.dynamic_index_in_dim(both, core, axis=0, keepdims=False)
    mine = mine + lax.ppermute(theirs.astype(BF), "core", swap).astype(F32)
    mine = mine.astype(BF).reshape(z_width, -1, 2 * rank)
    mine = lax.all_to_all(mine, "z", split_axis=0, concat_axis=0, tiled=True)
    mine = jnp.sum(mine.astype(F32), axis=0).astype(BF)
    half = lax.all_gather(mine, "z", axis=0, tiled=True)
    other = lax.ppermute(half, "core", swap)
    full = jnp.where(
        core == 0, jnp.concatenate([half, other]), jnp.concatenate([other, half])
    ).reshape(exp_local, per_expert, 2 * rank)
    back, full = lax.optimization_barrier((back, full))
    latent, query = full[..., :rank], full[..., rank:]
    query_f = query.astype(F32)

    scaled = (gate_slot[..., None] * query_f).astype(BF)
    spread_update = (task_mask[..., None] * scaled.astype(F32)[:, :, None, :]).astype(BF)
    weighted = (gate_slot[..., None] * latent.astype(F32)).astype(BF)
    spread_z = (task_mask[..., None] * weighted.astype(F32)[:, :, None, :]).astype(BF)
    first_grad = jnp.einsum(
        "estr,esf->etfr", spread_update, hidden, preferred_element_type=F32
    ).astype(BF)
    second_grad = jnp.einsum(
        "estr,esd->etrd", spread_z, rows, preferred_element_type=F32
    ).astype(BF)
    inner = jnp.sum(latent.astype(F32) * query_f, axis=2)
    update_part = jnp.einsum(
        "unqk,uqjk->unj", spread_update, adapter_first_factor, preferred_element_type=F32
    )

    back_f = jnp.swapaxes(back.astype(F32), 1, 2)
    first_device = (z_index == 0) & (core == 0)
    pair_part = jnp.sum(hidden.astype(F32) * back_f, axis=2) + jnp.where(first_device, inner, 0.0)
    dh = gate_slot[..., None] * back_f + update_part
    gate_grad = (dh * up_f * sig * (1.0 + gate_f * (1.0 - sig))).astype(BF)
    up_grad = (dh * act).astype(BF)

    returned = lax.all_to_all(
        pair_part.reshape(exp_local, most, source_count).transpose(2, 0, 1),
        "exp",
        split_axis=0,
        concat_axis=0,
        tiled=True,
    ).reshape(expert_count, most)
    finder = names.transpose(1, 0, 2).reshape(expert_count, top * tok_count).astype(BF)
    place_pick = jnp.sum(jnp.where(names, place[None], 0.0), axis=1).reshape(1, top * tok_count)
    found = jnp.dot(returned.astype(BF).T, finder, preferred_element_type=F32)
    found = jnp.sum(
        jnp.where(jnp.arange(most, dtype=jnp.int32).astype(F32)[:, None] == place_pick, found, 0.0),
        axis=0,
    ).reshape(top, tok_count)
    copies = jnp.broadcast_to(found.astype(BF), (z_width * 2, top, tok_count))
    pieces = lax.all_to_all(copies, ("z", "core"), split_axis=0, concat_axis=0, tiled=True)
    grad_combine = jnp.sum(pieces.astype(F32), axis=0).T
    shape_out = (exp_local, most, source_count, piece)
    return (
        gate_grad.reshape(shape_out).swapaxes(1, 2),
        up_grad.reshape(shape_out).swapaxes(1, 2),
        first_grad,
        second_grad,
        grad_combine,
    )


def solution(mesh):
    exp_width, seq_width = mesh.shape["exp"], mesh.shape["seq"]
    split = Mesh(mesh.devices.reshape(exp_width, seq_width // 2, 2), ("exp", "z", "core"))
    seq = ("z", "core")
    placed = (
        P("exp", seq),
        P("exp", None),
        P("exp", None),
        P("exp"),
        P("exp", None, None, seq),
        P("exp", None, None, seq),
        P("exp", None, seq),
        P("exp", None, seq, None),
        P("exp", None, None, seq),
    )
    return jax.shard_map(
        on_device,
        mesh=split,
        in_specs=placed,
        out_specs=(
            P("exp", None, None, seq),
            P("exp", None, None, seq),
            P("exp", None, seq, None),
            P("exp", None, None, seq),
            P("exp", None),
        ),
        check_vma=False,
    )
```

time: 548 us -> 192 us (0.35)
  waiting for transfers between devices: 330 us -> 21.1 us
  starting transfers between devices: 29.3 us -> 71.8 us
  blocking collectives: 93.3 us -> 55.7 us
  matrix products: 43.1 us -> 8.79 us
  local copies, waits for them, and re-layouts: 30.5 us -> 7.41 us
    psum x1 -> x0, waiting for transfers between devices: 236 us -> none  [on_device(): lax.psum((lat_part, ql_part, weight_part), 'seq')]
    psum x1 -> x0, blocking collectives: 93.3 us -> none  [on_device(): lax.psum((lat_part, ql_part, weight_part), 'seq')]
    all_gather x1 -> x0, waiting for transfers between devices: 69.1 us -> none  [on_device(): lax.all_gather(hidden_state, 'seq', axis=2, tiled=True)]
    dot_general x10 -> x8, matrix products: 40.8 us -> 7.28 us  [the longest x1 1.85 us: on_device(): jnp.einsum('estr,esf->etfr', spread_update, hidden, preferred_element_typ...]
    all_to_all x0 -> x1, blocking collectives: none -> 31.9 us  [on_device(): mine = lax.all_to_all(mine, 'z', split_axis=0, concat_axis=0, tiled=True)]
    ppermute x0 -> x4, starting transfers between devices: none -> 31.8 us  [the longest x1 10.6 us: on_device(): rows_peer = lax.ppermute(rows, 'core', swap)]
    all_gather x0 -> x1, blocking collectives: none -> 23.9 us  [on_device(): half = lax.all_gather(mine, 'z', axis=0, tiled=True)]
    transpose x1 -> x3, local copies, waits for them, and re-layouts: 12 us -> 0.87 us  [the longest x1 0.74 us: on_device(): pair_part.reshape(exp_local, most, source_count).transpose(2, 0, 1)]
  transfers between devices with their start and end apart: 6 -> 8, of which waited for: 6 -> 7; matrix products, arithmetic and copies ran while one was open for 4% -> 6% of each run, Pallas kernels for 0% -> 0%
where the time goes in v1:
time: 192 us; the launch traced here: 191 us
  starting transfers between devices  71.8 us (37%)
  blocking collectives  55.7 us (29%)
  waiting for transfers between devices  21.1 us (11%)
  between operations  14.4 us (8%)
  matrix products  8.79 us (5%)
  local copies, waits for them, and re-layouts  7.41 us (4%)
  other arithmetic  6.89 us (4%)
  Pallas kernels  5 us (3%)
    all_to_all x1, blocking collectives, on_device(): mine = lax.all_to_all(mine, 'z', split_axis=0, concat_axis=0, tiled=True)  31.9 us
    all_gather x1, blocking collectives, on_device(): half = lax.all_gather(mine, 'z', axis=0, tiled=True)  23.9 us
    all_to_all x1, starting transfers between devices, on_device(): lax.all_to_all(copies, ('z', 'core'), split_axis=0, concat_axis=0, tiled=...  20 us
    all_to_all x1, waiting for transfers between devices, on_device(): lax.all_to_all(copies, ('z', 'core'), split_axis=0, concat_axis=0, tiled=...  11.7 us
    ppermute x1, starting transfers between devices, on_device(): rows_peer = lax.ppermute(rows, 'core', swap)  10.6 us
    all_to_all x1, starting transfers between devices, on_device(): lax.all_to_all(send, 'exp', split_axis=0, concat_axis=0, tiled=True)  10.5 us
    ppermute x1, starting transfers between devices, on_device(): other = lax.ppermute(half, 'core', swap)  9.51 us
    ppermute x1, starting transfers between devices, on_device(): lax.ppermute(lax.dynamic_index_in_dim(weight, 1 - core, axis=2, keepdims=...  9.43 us
  transfers between devices with their start and end apart: 8, of which 7 were waited for; matrix products, arithmetic and copies ran while one was open for 6% of the time, Pallas kernels for 0%

profile of v1, /device:TPU:1, one launch (start us, length us, event | category | flops | bytes accessed | tf_op | source)
XLA Modules:
  0.0 191.1 jit_solution(16150363282222159870)
XLA Ops:
  7.2 0.0 copy-start
  7.2 0.8 convert_element_type.177
  8.0 0.8 fusion.15
  8.8 0.1 fusion.32
  8.9 0.7 convert_bitcast_fusion.1
  9.6 0.8 select_reduce_fusion.2
  10.4 0.1 pad.9.clone
  10.5 1.3 convolution_convert_fusion
  11.8 0.9 maximum_maximum_fusion
  12.8 10.5 %all-to-all-start = ((bf16[32,56,128]{2,1,0:T(8,128)(2,1)}), bf16[32,56,128]{2,1,0:T(8,128)(2,1)S(1)}, u32[]{:S(2)}, u32[]{:S(2)}) async-start(bf16[32,56,128]{2,1,0:T(8,128)(2,1)} %maximum_maximum_fusion), calls=%async_computation | async-start | bytes 917504 | tf_op jit(solution)/shard_map/all_to_all | solution.py:98
  23.3 0.0 reduce-scatter.2.cloned.1.call-start
  23.4 0.9 dynamic-slice_bitcast_fusion
  24.3 9.4 %collective-permute-start = (bf16[4,16,48,128]{3,2,1,0:T(8,128)(2,1)}, bf16[4,16,48,128]{3,2,1,0:T(8,128)(2,1)S(1)}, u32[]{:S(2)}, u32[]{:S(2)}) collective-permute-start(bf16[4,16,48,128]{3,2,1,0:T(8,128)(2,1)} %dynamic-slice_bitcast_fusion), channel_id=1, source_target_pairs={{0,1},{1,0},{2,3},{3,2},{4,5},{5,4},{6,7},{7,6},{8,9},{9,8},{10,11... | collective-permute-start | bytes 2359304 | tf_op jit(solution)/shard_map/ppermute | solution.py:68
  33.7 0.4 all-to-all-done
  34.1 0.1 copy.70
  34.2 0.0 copy-start.2
  34.3 10.6 %collective-permute-start.1 = (bf16[4,384,128]{2,1,0:T(8,128)(2,1)S(1)}, bf16[4,384,128]{2,1,0:T(8,128)(2,1)S(1)}, u32[]{:S(2)}, u32[]{:S(2)}) collective-permute-start(bf16[4,384,128]{2,1,0:T(8,128)(2,1)S(1)} %bitcast.92), channel_id=1, source_target_pairs={{0,1},{1,0},{2,3},{3,2},{4,5},{5,4},{6,7},{7,6},{8,9},{9,8},{10,11... | collective-permute-start | bytes 1179656 | tf_op jit(solution)/shard_map/ppermute | solution.py:101
  44.9 1.3 collective-permute-done.1.xp_ref
  46.2 0.7 copy-done.7
  46.9 5.0 %back_partial.1 = bf16[16,4,48,384]{3,2,1,0:T(8,128)(2,1)} custom-call(s32[1]{0:T(128)} %bitcast.8.core_ref, bf16[4,16,2,48,128]{4,3,2,1,0:T(8,128)(2,1)} %bitcast.86, bf16[4,16,48,128]{3,2,1,0:T(8,128)(2,1)} %copy-done.4, bf16[4,384,128]{2,1,0:T(8,128)(2,1)} %bitcast.93, bf16[4,384,128]{2,1,0:T(8,128)(2,1)} %copy-done.7), custom_call_target="tpu_custom_call" | custom-call | tf_op jit(solution)/shard_map/back_partial/pallas_call | solution.py:25
  51.9 0.0 reduce-scatter.2.cloned.1.call-update
  52.0 1.0 copy-done.8
  52.9 0.1 convert_element_type.220
  53.0 0.2 copy.72
  53.3 0.1 convert_element_type.221
  53.4 0.0 copy-start.3
  53.4 0.2 copy.73
  53.7 0.1 multiply_convert_fusion.17
  53.8 0.1 fusion.33
  54.0 0.6 select_reduce_fusion
  54.6 0.1 eq.112
  54.7 0.1 compare_convert_fusion
  54.7 1.6 multiply_reduce_fusion.1
  56.4 0.6 multiply_reduce_fusion
  57.0 0.1 pad_maximum_fusion
  57.1 0.0 copy-start.6
  57.1 0.3 copy.74
  57.4 2.3 %collective-permute-start.2 = (bf16[768,128]{1,0:T(8,128)(2,1)S(1)}, bf16[768,128]{1,0:T(8,128)(2,1)S(1)}, u32[]{:S(2)}, u32[]{:S(2)}) collective-permute-start(bf16[768,128]{1,0:T(8,128)(2,1)S(1)} %fusion.26), channel_id=1, source_target_pairs={{0,1},{1,0},{2,3},{3,2},{4,5},{5,4},{6,7},{7,6},{8,9},{9,8},{10,11... | collective-permute-start | bytes 589832 | tf_op jit(solution)/shard_map/ppermute | solution.py:141
  59.7 1.0 collective-permute-done.2
  60.8 31.9 %all_to_all.20 = bf16[16,48,128]{2,1,0:T(8,128)(2,1)S(1)} all-to-all(bf16[16,48,128]{2,1,0:T(8,128)(2,1)S(1)} %bitcast.97), channel_id=1, replica_groups=mesh['exp'=32,'z'=16,'core'=2] {'z'}, dimensions={0} | all-to-all | bytes 393216 | tf_op jit(solution)/shard_map/all_to_all | solution.py:143
  92.7 23.9 %all_gather.3 = bf16[768,128]{1,0:T(8,128)(2,1)S(1)} all-gather(bf16[48,128]{1,0:T(8,128)(2,1)S(1)} %reduce_sum.107), channel_id=1, replica_groups=mesh['exp'=32,'z'=16,'core'=2] {'z'}, dimensions={0}, use_global_device_ids=true | all-gather | bytes 208896 | tf_op jit(solution)/shard_map/all_gather | solution.py:145
  116.5 9.5 %collective-permute-start.3 = (bf16[768,128]{1,0:T(8,128)(2,1)S(1)}, bf16[768,128]{1,0:T(8,128)(2,1)S(1)}, u32[]{:S(2)}, u32[]{:S(2)}) collective-permute-start(bf16[768,128]{1,0:T(8,128)(2,1)S(1)} %all_gather.3), channel_id=1, source_target_pairs={{0,1},{1,0},{2,3},{3,2},{4,5},{5,4},{6,7},{7,6},{8,9},{9,8},{10,11... | collective-permute-start | bytes 589832 | tf_op jit(solution)/shard_map/ppermute | solution.py:146
  126.1 0.1 mul.87
  126.2 1.0 collective-permute-done.3
  127.1 0.1 maximum_select_fusion
  127.2 0.6 reduce-scatter.2.cloned.1.call-done
  127.8 0.2 copy.75
  128.1 1.0 fusion.23
  129.0 0.1 fusion.27
  129.1 0.0 copy-start.10
  129.1 1.5 multiply_convert_fusion.15
  130.7 0.1 add.55
  130.8 0.7 copy.81
  131.5 9.4 %all-to-all-start.2 = ((bf16[32,4,12]{2,1,0:T(4,128)(2,1)}), bf16[32,4,12]{2,1,0:T(4,128)(2,1)S(1)}, u32[]{:S(2)}, u32[]{:S(2)}) async-start(bf16[32,4,12]{2,1,0:T(4,128)(2,1)} %copy.81), calls=%async_computation.3 | async-start | bytes 65536 | tf_op jit(solution)/shard_map/all_to_all | solution.py:176
  140.9 1.9 fusion.11
  142.8 0.9 copy.78
  143.7 0.9 copy.79
  144.6 5.1 %all-to-all-done.2 = bf16[32,4,12]{2,1,0:T(4,128)(2,1)S(1)} async-done(((bf16[32,4,12]{2,1,0:T(4,128)(2,1)}), bf16[32,4,12]{2,1,0:T(4,128)(2,1)S(1)}, u32[]{:S(2)}, u32[]{:S(2)}) %all-to-all-start.2) | async-done | bytes 3104 | tf_op jit(solution)/shard_map/all_to_all | solution.py:176
  149.7 0.2 fusion.14
  149.9 0.6 broadcast_in_dim.91
  150.5 20.0 %all-to-all-start.3 = ((bf16[32,8,128]{2,1,0:T(8,128)(2,1)}), bf16[32,8,128]{2,1,0:T(8,128)(2,1)S(1)}, u32[]{:S(2)}, u32[]{:S(2)}) async-start(bf16[32,8,128]{2,1,0:T(8,128)(2,1)} %broadcast_in_dim.91), calls=%async_computation.4 | async-start | bytes 131072 | tf_op jit(solution)/shard_map/all_to_all | solution.py:191
  170.6 1.4 fusion.9
  172.0 11.7 %all-to-all-done.3 = bf16[32,8,128]{2,1,0:T(8,128)(2,1)S(1)} async-done(((bf16[32,8,128]{2,1,0:T(8,128)(2,1)}), bf16[32,8,128]{2,1,0:T(8,128)(2,1)S(1)}, u32[]{:S(2)}, u32[]{:S(2)}) %all-to-all-start.3) | async-done | bytes 65568 | tf_op jit(solution)/shard_map/all_to_all | solution.py:191
  183.7 0.6 convert_reduce_fusion
  (30 shorter events, 0.3 us)
Async XLA Ops:
  7.2 49.2 %copy-start = (bf16[4,8,64,128]{3,2,1,0:T(8,128)(2,1)S(1)}, bf16[4,8,64,128]{3,2,1,0:T(8,128)(2,1)}, u32[]{:S(2)}) copy-start(bf16[4,8,64,128]{3,2,1,0:T(8,128)(2,1)} %param.17) | copy-start | bytes 1572868
  7.2 16.2 %copy-start.1 = (bf16[4,1536,128]{2,1,0:T(8,128)(2,1)S(1)}, bf16[4,1536,128]{2,1,0:T(8,128)(2,1)}, u32[]{:S(2)}) copy-start(bf16[4,1536,128]{2,1,0:T(8,128)(2,1)} %param.15) | copy-start | bytes 4718596
  12.8 21.3 %all-to-all-start = ((bf16[32,56,128]{2,1,0:T(8,128)(2,1)}), bf16[32,56,128]{2,1,0:T(8,128)(2,1)S(1)}, u32[]{:S(2)}, u32[]{:S(2)}) async-start(bf16[32,56,128]{2,1,0:T(8,128)(2,1)} %maximum_maximum_fusion), calls=%async_computation | async-start | bytes 917504 | tf_op jit(solution)/shard_map/all_to_all | solution.py:98
  23.3 104.5 %reduce-scatter.2.cloned.1.call-start = ((), (), s32[]{:S(2)}) async-start(), calls=%async_computation.5 | async-start | bytes 2506752 | tf_op jit(solution)/shard_map/reduce_scatter | solution.py:124
  24.3 20.6 %collective-permute-start = (bf16[4,16,48,128]{3,2,1,0:T(8,128)(2,1)}, bf16[4,16,48,128]{3,2,1,0:T(8,128)(2,1)S(1)}, u32[]{:S(2)}, u32[]{:S(2)}) collective-permute-start(bf16[4,16,48,128]{3,2,1,0:T(8,128)(2,1)} %dynamic-slice_bitcast_fusion), channel_id=1, source_target_pairs={{0,1},{1,0},{2,3},{3,2},{4,5},{5,4},{6,7},{7,6},{8,9},{9,8},{10,11... | collective-permute-start | bytes 2359304 | tf_op jit(solution)/shard_map/ppermute | solution.py:68
  34.2 11.9 %copy-start.2 = (bf16[48,32,128]{2,1,0:T(8,128)(2,1)}, bf16[48,32,128]{2,1,0:T(8,128)(2,1)S(1)}, u32[]{:S(2)}) copy-start(bf16[48,32,128]{2,1,0:T(8,128)(2,1)S(1)} %copy.70) | copy-start | bytes 1179652
  34.3 11.9 %collective-permute-start.1 = (bf16[4,384,128]{2,1,0:T(8,128)(2,1)S(1)}, bf16[4,384,128]{2,1,0:T(8,128)(2,1)S(1)}, u32[]{:S(2)}, u32[]{:S(2)}) collective-permute-start(bf16[4,384,128]{2,1,0:T(8,128)(2,1)S(1)} %bitcast.92), channel_id=1, source_target_pairs={{0,1},{1,0},{2,3},{3,2},{4,5},{5,4},{6,7},{7,6},{8,9},{9,8},{10,11... | collective-permute-start | bytes 1179656 | tf_op jit(solution)/shard_map/ppermute | solution.py:101
  44.9 1.3 copy-start.4
  46.2 0.7 copy-start.7
  51.9 1.0 copy-start.8
  51.9 1.3 copy-start.9
  53.4 3.0 %copy-start.3 = (bf16[48,32,128]{2,1,0:T(8,128)(2,1)S(1)}, bf16[48,32,128]{2,1,0:T(8,128)(2,1)}, u32[]{:S(2)}) copy-start(bf16[48,32,128]{2,1,0:T(8,128)(2,1)} %copy-done.2) | copy-start | bytes 1179652
  53.8 2.6 %copy-start.5 = (bf16[4,384,48]{1,2,0:T(8,128)(2,1)}, bf16[4,384,48]{1,2,0:T(8,128)(2,1)S(1)}, u32[]{:S(2)}) copy-start(bf16[4,384,48]{1,2,0:T(8,128)(2,1)S(1)} %multiply_convert_fusion.17) | copy-start | bytes 442372
  57.1 71.0 %copy-start.6 = (bf16[4,384,48]{1,2,0:T(8,128)(2,1)S(1)}, bf16[4,384,48]{1,2,0:T(8,128)(2,1)}, u32[]{:S(2)}) copy-start(bf16[4,384,48]{1,2,0:T(8,128)(2,1)} %copy-done.5) | copy-start | bytes 442372
  57.4 3.3 %collective-permute-start.2 = (bf16[768,128]{1,0:T(8,128)(2,1)S(1)}, bf16[768,128]{1,0:T(8,128)(2,1)S(1)}, u32[]{:S(2)}, u32[]{:S(2)}) collective-permute-start(bf16[768,128]{1,0:T(8,128)(2,1)S(1)} %fusion.26), channel_id=1, source_target_pairs={{0,1},{1,0},{2,3},{3,2},{4,5},{5,4},{6,7},{7,6},{8,9},{9,8},{10,11... | collective-permute-start | bytes 589832 | tf_op jit(solution)/shard_map/ppermute | solution.py:141
  116.5 10.6 %collective-permute-start.3 = (bf16[768,128]{1,0:T(8,128)(2,1)S(1)}, bf16[768,128]{1,0:T(8,128)(2,1)S(1)}, u32[]{:S(2)}, u32[]{:S(2)}) collective-permute-start(bf16[768,128]{1,0:T(8,128)(2,1)S(1)} %all_gather.3), channel_id=1, source_target_pairs={{0,1},{1,0},{2,3},{3,2},{4,5},{5,4},{6,7},{7,6},{8,9},{9,8},{10,11... | collective-permute-start | bytes 589832 | tf_op jit(solution)/shard_map/ppermute | solution.py:146
  129.1 20.6 %copy-start.10 = (s32[128,8]{0,1:T(8,128)S(1)}, s32[128,8]{0,1:T(8,128)}, u32[]{:S(2)}) copy-start(s32[128,8]{0,1:T(8,128)} %param.10) | copy-start | bytes 12292
  131.5 18.2 %all-to-all-start.2 = ((bf16[32,4,12]{2,1,0:T(4,128)(2,1)}), bf16[32,4,12]{2,1,0:T(4,128)(2,1)S(1)}, u32[]{:S(2)}, u32[]{:S(2)}) async-start(bf16[32,4,12]{2,1,0:T(4,128)(2,1)} %copy.81), calls=%async_computation.3 | async-start | bytes 65536 | tf_op jit(solution)/shard_map/all_to_all | solution.py:176
  150.5 33.1 %all-to-all-start.3 = ((bf16[32,8,128]{2,1,0:T(8,128)(2,1)}), bf16[32,8,128]{2,1,0:T(8,128)(2,1)S(1)}, u32[]{:S(2)}, u32[]{:S(2)}) async-start(bf16[32,8,128]{2,1,0:T(8,128)(2,1)} %broadcast_in_dim.91), calls=%async_computation.4 | async-start | bytes 131072 | tf_op jit(solution)/shard_map/all_to_all | solution.py:191
Sparse Core Ops, SparseCore 0:
  52.1 75.6 reduce-scatter.1

commit v2 on v1

v2 whole, which is shorter than its diff:
```python
import jax
import jax.numpy as jnp
from jax import lax
from jax.experimental import pallas as pl
from jax.experimental.pallas import tpu as pltpu
from jax.sharding import Mesh
from jax.sharding import PartitionSpec as P

BF = jnp.bfloat16
F32 = jnp.float32


def partial_sums(core, task_row, hidden, first, second, weight, weight_peer, rows, rows_peer):
    exp_local, z_width, _, piece, width = weight.shape
    slots = rows.shape[1]
    task_count, rank = first.shape[1], first.shape[3]
    more = 2 * rank // z_width

    def kernel(core_ref, t_ref, h_ref, a_ref, b_ref, w_ref, wp_ref, x_ref, xp_ref, out_ref):
        nums = (((1,), (1,)), ((), ()))
        x = x_ref[0]
        own = w_ref[0, :, 0].reshape(z_width * piece, width)
        peer = wp_ref[0].reshape(z_width * piece, width)
        total = lax.dot_general(own, x, nums, preferred_element_type=F32)
        total += lax.dot_general(peer, xp_ref[0], nums, preferred_element_type=F32)
        out_ref[:, :piece] = total.astype(BF).reshape(z_width, piece, slots)
        ql_all = lax.dot_general(
            b_ref[0].reshape(task_count * rank, width), x, nums, preferred_element_type=F32
        )
        lat = jnp.zeros((rank, slots), F32)
        ql = jnp.zeros((rank, slots), F32)
        for t in range(task_count):
            keep = t_ref[0] == float(t)
            part = lax.dot_general(
                a_ref[0, t], h_ref[0], (((0,), (0,)), ((), ())), preferred_element_type=F32
            )
            lat += jnp.where(keep, part, 0.0)
            ql += jnp.where(keep, ql_all[t * rank : (t + 1) * rank], 0.0)
        out_ref[: z_width // 2, piece:] = lat.astype(BF).reshape(z_width // 2, more, slots)
        out_ref[z_width // 2 :, piece:] = ql.astype(BF).reshape(z_width // 2, more, slots)

    return pl.pallas_call(
        kernel,
        out_shape=jax.ShapeDtypeStruct((z_width, piece + more, exp_local * slots), BF),
        grid_spec=pltpu.PrefetchScalarGridSpec(
            num_scalar_prefetch=1,
            grid=(exp_local,),
            in_specs=[
                pl.BlockSpec((1, 1, slots), lambda e, c: (e, 0, 0)),
                pl.BlockSpec((1, piece, slots), lambda e, c: (e, 0, 0)),
                pl.BlockSpec((1, task_count, piece, rank), lambda e, c: (e, 0, 0, 0)),
                pl.BlockSpec((1, task_count, rank, width), lambda e, c: (e, 0, 0, 0)),
                pl.BlockSpec((1, z_width, 1, piece, width), lambda e, c: (e, 0, c[0], 0, 0)),
                pl.BlockSpec((1, z_width, piece, width), lambda e, c: (e, 0, 0, 0)),
                pl.BlockSpec((1, slots, width), lambda e, c: (e, 0, 0)),
                pl.BlockSpec((1, slots, width), lambda e, c: (e, 0, 0)),
            ],
            out_specs=pl.BlockSpec((z_width, piece + more, slots), lambda e, c: (0, 0, e)),
        ),
        name="partial_sums",
    )(core.reshape(1), task_row, hidden, first, second, weight, weight_peer, rows, rows_peer)


def on_device(
    output_gradient,
    routed_expert_index,
    combine,
    token_task_index,
    saved_gate_input,
    saved_up_input,
    down_weight,
    adapter_first_factor,
    adapter_second_factor,
):
    exp_width = lax.axis_size("exp")
    z_width = lax.axis_size("z")
    core = lax.axis_index("core")
    exp_local, source_count, most, piece = saved_gate_input.shape
    tok_count, top = routed_expert_index.shape
    width = output_gradient.shape[1]
    task_count, rank = adapter_first_factor.shape[1], adapter_first_factor.shape[3]
    expert_count = exp_local * exp_width
    per_expert = source_count * most
    total_slots = exp_local * per_expert
    swap = [(0, 1), (1, 0)]

    weight = down_weight.reshape(exp_local, z_width, 2, piece, width)
    weight_peer = lax.ppermute(
        lax.dynamic_index_in_dim(weight, 1 - core, axis=2, keepdims=False), "core", swap
    )

    ids = routed_expert_index.T
    experts = jnp.arange(expert_count, dtype=jnp.int32)
    tokens = jnp.arange(tok_count, dtype=jnp.int32)
    names = ids[:, None, :] == experts[None, :, None]
    named = jnp.any(names, axis=0)
    gates = jnp.sum(jnp.where(names, combine.T[:, None, :].astype(F32), 0.0), axis=0)
    earlier = (tokens[:, None] < tokens[None, :]).astype(BF)
    place = jnp.dot(named.astype(BF), earlier, preferred_element_type=F32)
    place_or = jnp.where(named, place, -1.0).astype(BF)
    row_of = jnp.arange(expert_count * most, dtype=jnp.int32)
    spread = (row_of[:, None] // most == experts[None, :]).astype(BF)
    picked = jnp.dot(spread, place_or, preferred_element_type=F32) == (
        (row_of % most).astype(F32)[:, None]
    )
    send_rows = jnp.dot(picked.astype(BF), output_gradient, preferred_element_type=F32).astype(BF)
    slab = exp_local * most
    extra = -(exp_local + 1) % 8
    send = jnp.concatenate(
        [
            send_rows.reshape(exp_width, slab, width),
            gates.astype(BF).reshape(exp_width, exp_local, tok_count),
            jnp.broadcast_to(token_task_index.astype(BF), (exp_width, 1, tok_count)),
            jnp.zeros((exp_width, extra, tok_count), BF),
        ],
        axis=1,
    )
    received = lax.all_to_all(send, "exp", split_axis=0, concat_axis=0, tiled=True)

    rows = received[:, :slab].transpose(1, 0, 2).reshape(exp_local, per_expert, width)
    rows_peer = lax.ppermute(rows, "core", swap)
    gate_rows = received[:, slab : slab + exp_local].transpose(1, 0, 2)
    used = gate_rows > 0
    place_in = jnp.dot(
        used.astype(BF).reshape(exp_local * source_count, tok_count),
        earlier,
        preferred_element_type=F32,
    ).reshape(exp_local, source_count, tok_count)
    holds = used[:, None] & (
        place_in[:, None] == jnp.arange(most, dtype=jnp.int32).astype(F32)[:, None, None]
    )
    gate_slot = jnp.sum(jnp.where(holds, gate_rows.astype(F32)[:, None], 0.0), axis=3).reshape(
        exp_local, per_expert
    )
    task_rows = received[:, slab + exp_local].astype(F32)
    task_slot = jnp.sum(
        jnp.where(holds, task_rows, 0.0), axis=3
    ).reshape(exp_local, per_expert)
    task_mask = (
        task_slot[:, None] == jnp.arange(task_count, dtype=jnp.int32).astype(F32)[:, None]
    ).astype(F32)

    gate_f = saved_gate_input.transpose(0, 3, 2, 1).reshape(exp_local, piece, per_expert)
    up_f = saved_up_input.transpose(0, 3, 2, 1).reshape(exp_local, piece, per_expert)
    gate_f, up_f = gate_f.astype(F32), up_f.astype(F32)
    sig = jax.nn.sigmoid(gate_f)
    act = gate_f * sig
    hidden = (act * up_f).astype(BF)

    partial = partial_sums(
        core.astype(jnp.int32),
        task_slot[:, None],
        hidden,
        adapter_first_factor,
        adapter_second_factor,
        weight,
        weight_peer,
        rows,
        rows_peer,
    )
    summed = lax.psum_scatter(partial, "z", scatter_dimension=0, tiled=True)[0]
    back = summed[:piece].astype(F32).reshape(piece, exp_local, per_expert).transpose(1, 0, 2)

    pair_part = jnp.sum(hidden.astype(F32) * back, axis=1).reshape(1, total_slots)
    small = jnp.concatenate([summed[piece:], pair_part.astype(BF)])
    small = small.astype(F32) + lax.ppermute(small, "core", swap).astype(F32)
    everything = lax.all_gather(small.astype(BF), "z", axis=0, tiled=False)
    more = 2 * rank // z_width
    split = (rank, exp_local, per_expert)
    latent = everything[: z_width // 2, :more].reshape(split).astype(F32)
    query = everything[z_width // 2 :, :more].reshape(split).astype(F32)
    pair_sum = jnp.sum(everything[:, more].astype(F32), axis=0).reshape(exp_local, per_expert)
    weight_grad = pair_sum + jnp.sum(latent * query, axis=0)

    returned = lax.all_to_all(
        weight_grad.astype(BF).reshape(exp_local, most, source_count).transpose(2, 0, 1),
        "exp",
        split_axis=0,
        concat_axis=0,
        tiled=True,
    ).reshape(expert_count, most)

    scaled = (gate_slot * query).astype(BF)
    spread_update = (
        task_mask.transpose(1, 0, 2)[:, None] * scaled.astype(F32)[None]
    ).astype(BF)
    weighted = (gate_slot * latent).astype(BF)
    spread_z = (task_mask.transpose(1, 0, 2)[:, None] * weighted.astype(F32)[None]).astype(BF)
    first_grad = jnp.einsum(
        "tres,efs->etfr", spread_update, hidden, preferred_element_type=F32
    ).astype(BF)
    second_grad = jnp.einsum(
        "tres,esd->etrd", spread_z, rows, preferred_element_type=F32
    ).astype(BF)
    update_part = jnp.einsum(
        "tres,etfr->efs", spread_update, adapter_first_factor, preferred_element_type=F32
    )
    dh = gate_slot[:, None] * back + update_part
    gate_grad = (dh * up_f * sig * (1.0 + gate_f * (1.0 - sig))).astype(BF)
    up_grad = (dh * act).astype(BF)

    finder = names.transpose(1, 0, 2).reshape(expert_count, top * tok_count).astype(BF)
    place_pick = jnp.sum(jnp.where(names, place[None], 0.0), axis=1).reshape(1, top * tok_count)
    found = jnp.dot(returned.T, finder, preferred_element_type=F32)
    found = jnp.sum(
        jnp.where(jnp.arange(most, dtype=jnp.int32).astype(F32)[:, None] == place_pick, found, 0.0),
        axis=0,
    )
    grad_combine = found.reshape(top, tok_count).T
    shape_out = (exp_local, piece, most, source_count)
    return (
        gate_grad.reshape(shape_out).transpose(0, 3, 2, 1),
        up_grad.reshape(shape_out).transpose(0, 3, 2, 1),
        first_grad,
        second_grad,
        grad_combine,
    )


def solution(mesh):
    exp_width, seq_width = mesh.shape["exp"], mesh.shape["seq"]
    split = Mesh(mesh.devices.reshape(exp_width, seq_width // 2, 2), ("exp", "z", "core"))
    seq = ("z", "core")
    placed = (
        P("exp", seq),
        P("exp", None),
        P("exp", None),
        P("exp"),
        P("exp", None, None, seq),
        P("exp", None, None, seq),
        P("exp", None, seq),
        P("exp", None, seq, None),
        P("exp", None, None, seq),
    )
    return jax.shard_map(
        on_device,
        mesh=split,
        in_specs=placed,
        out_specs=(
            P("exp", None, None, seq),
            P("exp", None, None, seq),
            P("exp", None, seq, None),
            P("exp", None, None, seq),
            P("exp", None),
        ),
        check_vma=False,
    )
```

time: 192 us -> 196 us (1.021)
  the two profiles are of different devices: /device:TPU:1 before, /device:TPU:8 now
where the time goes in v2:
time: 196 us; the launch traced here: 195 us
  waiting for transfers between devices  90.9 us (46%)
  starting transfers between devices  32.2 us (16%)
  blocking collectives  31.7 us (16%)
  between operations  14.4 us (7%)
  other arithmetic  7.99 us (4%)
  local copies, waits for them, and re-layouts  6.71 us (3%)
  Pallas kernels  5.79 us (3%)
  matrix products  5.36 us (3%)
    reduce_scatter x1, waiting for transfers between devices, on_device(): summed = lax.psum_scatter(partial, 'z', scatter_dimension=0, tiled=True)[0]  78.6 us
    all_gather x1, blocking collectives, on_device(): everything = lax.all_gather(small.astype(BF), 'z', axis=0, tiled=False)  31.7 us
    all_to_all x1, starting transfers between devices, on_device(): lax.all_to_all(send, 'exp', split_axis=0, concat_axis=0, tiled=True)  16.6 us
    all_to_all x1, starting transfers between devices, on_device(): lax.all_to_all(weight_grad.astype(BF).reshape(exp_local, most, source_cou...  9.8 us
    all_to_all x1, waiting for transfers between devices, on_device(): lax.all_to_all(send, 'exp', split_axis=0, concat_axis=0, tiled=True)  8.48 us
    pallas_call x1, Pallas kernels, partial_sums(): pl.pallas_call(kernel, out_shape=jax.ShapeDtypeStruct((z_width, piece + m...  5.79 us
  transfers between devices with their start and end apart: 6, of which 5 were waited for; matrix products, arithmetic and copies ran while one was open for 5% of the time, Pallas kernels for 0%

profile of v2, /device:TPU:8, one launch (start us, length us, event | category | flops | bytes accessed | tf_op | source)
XLA Modules:
  0.0 195.1 jit_solution(422625941486659642)
XLA Ops:
  7.2 0.0 copy-start
  7.2 0.0 copy-start.1
  7.2 0.8 convert_element_type.222
  8.0 0.7 convert_bitcast_fusion.1
  8.7 0.8 fusion.15
  9.5 0.1 fusion.27
  9.6 0.1 pad.5.clone
  9.7 0.8 select_reduce_fusion.2
  10.5 0.6 convolution_convert_fusion
  11.1 0.9 maximum_maximum_fusion
  12.0 16.6 %all-to-all-start = ((bf16[32,56,128]{2,1,0:T(8,128)(2,1)}), bf16[32,56,128]{2,1,0:T(8,128)(2,1)S(1)}, u32[]{:S(2)}, u32[]{:S(2)}) async-start(bf16[32,56,128]{2,1,0:T(8,128)(2,1)} %maximum_maximum_fusion), calls=%async_computation | async-start | bytes 917504 | tf_op jit(solution)/shard_map/all_to_all | solution.py:118
  28.7 0.0 reduce-scatter.2.cloned.1.call-start
  28.7 0.0 copy-done.1
  28.7 0.1 dynamic-slice_bitcast_fusion
  28.8 1.9 collective-permute-start
  30.8 0.1 convert_element_type.271
  30.8 0.2 copy.51
  31.1 1.1 convert_element_type.272
  32.2 0.2 copy.52
  32.4 0.8 multiply_convert_fusion.19.h_ref
  33.2 8.5 %all-to-all-done = bf16[32,56,128]{2,1,0:T(8,128)(2,1)S(1)} async-done(((bf16[32,56,128]{2,1,0:T(8,128)(2,1)}), bf16[32,56,128]{2,1,0:T(8,128)(2,1)S(1)}, u32[]{:S(2)}, u32[]{:S(2)}) %all-to-all-start) | async-done | bytes 458784 | tf_op jit(solution)/shard_map/all_to_all | solution.py:118
  41.7 0.1 copy.53
  41.8 0.0 copy-start.2
  41.9 1.9 collective-permute-start.1
  43.8 0.1 fusion.28
  44.0 0.6 select_reduce_fusion.1
  44.6 0.7 broadcast_in_dim_reshape.3.t_ref
  45.3 0.0 collective-permute-done.wp_ref
  45.3 0.2 collective-permute-done.1.xp_ref
  45.5 0.7 copy-done.5
  46.2 0.1 copy-done.7
  46.3 5.8 %partial_sums.1 = bf16[16,56,1536]{2,1,0:T(8,128)(2,1)} custom-call(s32[1]{0:T(128)} %bitcast.7.core_ref, f32[4,1,384]{2,1,0:T(1,128)} %broadcast_in_dim_reshape.3.t_ref, bf16[4,48,384]{2,1,0:T(8,128)(2,1)} %multiply_convert_fusion.19.h_ref, bf16[4,8,48,64]{3,2,1,0:T(8,128)(2,1)} %a_ref.1, bf16[4,8,64,128]{3,2,1,0:T(8,128)(2,1)} %b_ref.1, ...), custom_call_target="tpu_custom_call" | custom-call | tf_op jit(solution)/shard_map/partial_sums/pallas_call | solution.py:42
  52.1 0.0 reduce-scatter.2.cloned.1.call-update
  52.1 0.1 eq.105
  52.2 78.6 %reduce-scatter.2.cloned.1.call-done = bf16[1,56,1536]{2,1,0:T(8,128)(2,1)} async-done(((bf16[16,56,1536]{2,1,0:T(8,128)(2,1)}), bf16[1,56,1536]{2,1,0:T(8,128)(2,1)}) %reduce-scatter.2.cloned.1.call-update) | async-done | bytes 172048 | tf_op jit(solution)/shard_map/reduce_scatter | solution.py:161
  130.8 0.9 slice_convert_fusion.2
  131.7 0.1 reshape.173
  131.9 0.1 fusion.19
  131.9 0.7 slice_bitcast_fusion.1
  132.7 1.9 collective-permute-start.2
  134.6 0.1 compare_convert_fusion
  134.7 0.1 mul.84
  134.8 1.0 collective-permute-done.2
  135.8 31.7 %all-gather.1 = bf16[16,9,1536]{2,1,0:T(8,128)(2,1)S(1)} all-gather(bf16[1,9,1536]{2,1,0:T(8,128)(2,1)S(1)} %fusion.30), channel_id=2, replica_groups=mesh['exp'=32,'z'=16,'core'=2] {'z'}, dimensions={0}, use_global_device_ids=true | all-gather | bytes 470016 | tf_op jit(solution)/shard_map/all_gather | solution.py:167
  167.6 0.1 multiply_reduce_fusion
  167.6 0.1 fusion.25
  167.7 0.0 copy-start.6
  167.8 0.1 slice_convert_fusion
  167.8 0.1 reshape.172
  168.0 0.1 convert_element_type.263
  168.1 0.7 copy.62
  168.8 9.8 %all-to-all-start.1 = ((bf16[32,4,12]{2,1,0:T(4,128)(2,1)}), bf16[32,4,12]{2,1,0:T(4,128)(2,1)S(1)}, u32[]{:S(2)}, u32[]{:S(2)}) async-start(bf16[32,4,12]{2,1,0:T(4,128)(2,1)} %copy.62), calls=%async_computation.2 | async-start | bytes 65536 | tf_op jit(solution)/shard_map/all_to_all | solution.py:175
  178.6 0.1 reshape.171
  178.8 0.1 fusion.23
  178.9 0.0 copy-start.3
  179.0 0.5 multiply_convert_fusion.17
  179.5 0.0 copy-start.9
  179.5 0.4 copy-done.3
  179.9 1.4 fusion.9
  181.3 1.9 fusion.11
  183.1 0.9 copy.60
  184.0 0.9 copy.59
  185.0 2.5 %all-to-all-done.1 = bf16[32,4,12]{2,1,0:T(4,128)(2,1)S(1)} async-done(((bf16[32,4,12]{2,1,0:T(4,128)(2,1)}), bf16[32,4,12]{2,1,0:T(4,128)(2,1)S(1)}, u32[]{:S(2)}, u32[]{:S(2)}) %all-to-all-start.1) | async-done | bytes 3104 | tf_op jit(solution)/shard_map/all_to_all | solution.py:175
  187.4 0.8 fusion.14
  (26 shorter events, 0.2 us)
Async XLA Ops:
  7.2 3.3 %copy-start = (bf16[128,128]{1,0:T(8,128)(2,1)S(1)}, bf16[128,128]{1,0:T(8,128)(2,1)}, u32[]{:S(2)}) copy-start(bf16[128,128]{1,0:T(8,128)(2,1)} %param.9) | copy-start | bytes 98308
  7.2 21.6 %copy-start.1 = (bf16[4,1536,128]{2,1,0:T(8,128)(2,1)S(1)}, bf16[4,1536,128]{2,1,0:T(8,128)(2,1)}, u32[]{:S(2)}) copy-start(bf16[4,1536,128]{2,1,0:T(8,128)(2,1)} %param.15) | copy-start | bytes 4718596
  7.2 23.6 %copy-start.8 = (bf16[4,32,12,48]{3,1,2,0:T(8,128)(2,1)S(1)}, bf16[4,32,12,48]{3,1,2,0:T(8,128)(2,1)}, u32[]{:S(2)}) copy-start(bf16[4,32,12,48]{3,1,2,0:T(8,128)(2,1)} %param.13) | copy-start | bytes 442372
  12.0 29.6 %all-to-all-start = ((bf16[32,56,128]{2,1,0:T(8,128)(2,1)}), bf16[32,56,128]{2,1,0:T(8,128)(2,1)S(1)}, u32[]{:S(2)}, u32[]{:S(2)}) async-start(bf16[32,56,128]{2,1,0:T(8,128)(2,1)} %maximum_maximum_fusion), calls=%async_computation | async-start | bytes 917504 | tf_op jit(solution)/shard_map/all_to_all | solution.py:118
  28.7 102.1 %reduce-scatter.2.cloned.1.call-start = ((), (), s32[]{:S(2)}) async-start(), calls=%async_computation.3 | async-start | bytes 2924544 | tf_op jit(solution)/shard_map/reduce_scatter | solution.py:161
  28.8 16.4 %collective-permute-start = (bf16[4,16,48,128]{3,2,1,0:T(8,128)(2,1)S(1)}, bf16[4,16,48,128]{3,2,1,0:T(8,128)(2,1)S(1)}, u32[]{:S(2)}, u32[]{:S(2)}) collective-permute-start(bf16[4,16,48,128]{3,2,1,0:T(8,128)(2,1)S(1)} %dynamic-slice_bitcast_fusion), channel_id=1, source_target_pairs={{0,1},{1,0},{2,3},{3,2},{4,5},{5,4},{6,7},{7,6},{8,9},{9,8},{10,11... | collective-permute-start | bytes 2359304 | tf_op jit(solution)/shard_map/ppermute | solution.py:88
  41.8 3.7 %copy-start.2 = (bf16[48,32,128]{2,1,0:T(8,128)(2,1)}, bf16[48,32,128]{2,1,0:T(8,128)(2,1)S(1)}, u32[]{:S(2)}) copy-start(bf16[48,32,128]{2,1,0:T(8,128)(2,1)S(1)} %copy.53) | copy-start | bytes 1179652
  41.9 3.6 %collective-permute-start.1 = (bf16[4,384,128]{2,1,0:T(8,128)(2,1)S(1)}, bf16[4,384,128]{2,1,0:T(8,128)(2,1)S(1)}, u32[]{:S(2)}, u32[]{:S(2)}) collective-permute-start(bf16[4,384,128]{2,1,0:T(8,128)(2,1)S(1)} %bitcast.84), channel_id=1, source_target_pairs={{0,1},{1,0},{2,3},{3,2},{4,5},{5,4},{6,7},{7,6},{8,9},{9,8},{10,11... | collective-permute-start | bytes 1179656 | tf_op jit(solution)/shard_map/ppermute | solution.py:121
  45.3 0.9 copy-start.5
  45.5 0.8 copy-start.7
  52.1 79.8 %copy-start.4 = (bf16[4,48,384]{2,1,0:T(8,128)(2,1)S(1)}, bf16[4,48,384]{2,1,0:T(8,128)(2,1)}, u32[]{:S(2)}) copy-start(bf16[4,48,384]{2,1,0:T(8,128)(2,1)} %multiply_convert_fusion.19.h_ref) | copy-start | bytes 442372
  132.7 3.1 %collective-permute-start.2 = (bf16[9,1536]{1,0:T(8,128)(2,1)S(1)}, bf16[9,1536]{1,0:T(8,128)(2,1)S(1)}, u32[]{:S(2)}, u32[]{:S(2)}) collective-permute-start(bf16[9,1536]{1,0:T(8,128)(2,1)S(1)} %pad_maximum_fusion), channel_id=1, source_target_pairs={{0,1},{1,0},{2,3},{3,2},{4,5},{5,4},{6,7},{7,6},{8,9},{9,8},{10,11... | collective-permute-start | bytes 82952 | tf_op jit(solution)/shard_map/ppermute | solution.py:166
  167.7 11.2 %copy-start.6 = (bf16[4,8,48,64]{3,2,1,0:T(8,128)(2,1)S(1)}, bf16[4,8,48,64]{3,2,1,0:T(8,128)(2,1)}, u32[]{:S(2)}) copy-start(bf16[4,8,48,64]{3,2,1,0:T(8,128)(2,1)} %a_ref.1) | copy-start | bytes 589828
  168.8 18.6 %all-to-all-start.1 = ((bf16[32,4,12]{2,1,0:T(4,128)(2,1)}), bf16[32,4,12]{2,1,0:T(4,128)(2,1)S(1)}, u32[]{:S(2)}, u32[]{:S(2)}) async-start(bf16[32,4,12]{2,1,0:T(4,128)(2,1)} %copy.62), calls=%async_computation.2 | async-start | bytes 65536 | tf_op jit(solution)/shard_map/all_to_all | solution.py:175
  178.9 1.0 copy-start.3
  179.5 8.0 %copy-start.9 = (s32[128,8]{0,1:T(8,128)S(1)}, s32[128,8]{0,1:T(8,128)}, u32[]{:S(2)}) copy-start(s32[128,8]{0,1:T(8,128)} %param.10) | copy-start | bytes 12292
Sparse Core Ops, SparseCore 0:
  52.2 78.5 reduce-scatter.1

commit v3 on v2

--- a/solution.py
+++ b/solution.py
@@ -8,6 +8,7 @@
 
 BF = jnp.bfloat16
 F32 = jnp.float32
+PAD = 7
 
 
 def partial_sums(core, task_row, hidden, first, second, weight, weight_peer, rows, rows_peer):
@@ -15,15 +16,15 @@
     slots = rows.shape[1]
     task_count, rank = first.shape[1], first.shape[3]
     more = 2 * rank // z_width
-
-    def kernel(core_ref, t_ref, h_ref, a_ref, b_ref, w_ref, wp_ref, x_ref, xp_ref, out_ref):
+    chunk = piece + more + PAD
+
+    def kernel(core_ref, t_ref, h_ref, a_ref, b_ref, w_ref, wp_ref, x_ref, xp_ref, out_ref, f32_ref):
         nums = (((1,), (1,)), ((), ()))
         x = x_ref[0]
         own = w_ref[0, :, 0].reshape(z_width * piece, width)
         peer = wp_ref[0].reshape(z_width * piece, width)
         total = lax.dot_general(own, x, nums, preferred_element_type=F32)
         total += lax.dot_general(peer, xp_ref[0], nums, preferred_element_type=F32)
-        out_ref[:, :piece] = total.astype(BF).reshape(z_width, piece, slots)
         ql_all = lax.dot_general(
             b_ref[0].reshape(task_count * rank, width), x, nums, preferred_element_type=F32
         )
@@ -36,12 +37,18 @@
             )
             lat += jnp.where(keep, part, 0.0)
             ql += jnp.where(keep, ql_all[t * rank : (t + 1) * rank], 0.0)
-        out_ref[: z_width // 2, piece:] = lat.astype(BF).reshape(z_width // 2, more, slots)
-        out_ref[z_width // 2 :, piece:] = ql.astype(BF).reshape(z_width // 2, more, slots)
+        small = jnp.concatenate([lat, ql])
+        empty = jnp.zeros((PAD, slots), F32)
+        for z in range(z_width):
+            at = z * chunk
+            f32_ref[at : at + piece] = total[z * piece : (z + 1) * piece]
+            f32_ref[at + piece : at + piece + more] = small[z * more : (z + 1) * more]
+            f32_ref[at + piece + more : at + chunk] = empty
+        out_ref[...] = f32_ref[...].astype(BF)
 
     return pl.pallas_call(
         kernel,
-        out_shape=jax.ShapeDtypeStruct((z_width, piece + more, exp_local * slots), BF),
+        out_shape=jax.ShapeDtypeStruct((z_width * chunk, exp_local * slots), BF),
         grid_spec=pltpu.PrefetchScalarGridSpec(
             num_scalar_prefetch=1,
             grid=(exp_local,),
@@ -55,7 +62,8 @@
                 pl.BlockSpec((1, slots, width), lambda e, c: (e, 0, 0)),
                 pl.BlockSpec((1, slots, width), lambda e, c: (e, 0, 0)),
             ],
-            out_specs=pl.BlockSpec((z_width, piece + more, slots), lambda e, c: (0, 0, e)),
+            out_specs=pl.BlockSpec((z_width * chunk, slots), lambda e, c: (0, e)),
+            scratch_shapes=[pltpu.VMEM((z_width * chunk, slots), F32)],
         ),
         name="partial_sums",
     )(core.reshape(1), task_row, hidden, first, second, weight, weight_peer, rows, rows_peer)
@@ -158,14 +166,17 @@
         rows,
         rows_peer,
     )
-    summed = lax.psum_scatter(partial, "z", scatter_dimension=0, tiled=True)[0]
+    summed = lax.psum_scatter(partial, "z", scatter_dimension=0, tiled=True)
+    summed = lax.optimization_barrier(summed)
     back = summed[:piece].astype(F32).reshape(piece, exp_local, per_expert).transpose(1, 0, 2)
 
     pair_part = jnp.sum(hidden.astype(F32) * back, axis=1).reshape(1, total_slots)
-    small = jnp.concatenate([summed[piece:], pair_part.astype(BF)])
+    more = 2 * rank // z_width
+    small = jnp.concatenate([summed[piece : piece + more], pair_part.astype(BF)])
+    small = small.reshape(-1, 128)
     small = small.astype(F32) + lax.ppermute(small, "core", swap).astype(F32)
     everything = lax.all_gather(small.astype(BF), "z", axis=0, tiled=False)
-    more = 2 * rank // z_width
+    everything = everything.reshape(z_width, more + 1, total_slots)
     split = (rank, exp_local, per_expert)
     latent = everything[: z_width // 2, :more].reshape(split).astype(F32)
     query = everything[z_width // 2 :, :more].reshape(split).astype(F32)

time: 196 us -> 155 us (0.79)
  waiting for transfers between devices: 90.9 us -> 12.5 us
  blocking collectives: 31.7 us -> 84.3 us
  between operations: 14.4 us -> 1.73 us
  starting transfers between devices: 32.2 us -> 29.8 us
  local copies, waits for them, and re-layouts: 6.71 us -> 8.82 us
    reduce_scatter x1 -> x0, waiting for transfers between devices: 78.6 us -> none  [on_device(): summed = lax.psum_scatter(partial, 'z', scatter_dimension=0, tiled=True)[0]]
    unnamed x0 -> x1, blocking collectives: none -> 53.7 us
    all_to_all x1, starting transfers between devices: 9.8 us -> 4.86 us  [on_device(): lax.all_to_all(weight_grad.astype(BF).reshape(exp_local, most, source_cou...]
    unnamed x0 -> x1, starting transfers between devices: none -> 2.53 us
  transfers between devices with their start and end apart: 6 -> 6, of which waited for: 5 -> 4; matrix products, arithmetic and copies ran while one was open for 5% -> 7% of each run, Pallas kernels for 0% -> 0%
where the time goes in v3:
time: 155 us
  blocking collectives  84.3 us (54%)
  starting transfers between devices  29.8 us (19%)
  waiting for transfers between devices  12.5 us (8%)
  local copies, waits for them, and re-layouts  8.82 us (6%)
  other arithmetic  6.07 us (4%)
  Pallas kernels  6.03 us (4%)
  matrix products  5.35 us (3%)
  between operations  1.73 us (1%)
    unnamed x1, blocking collectives  53.7 us
    all_gather x1, blocking collectives, on_device(): everything = lax.all_gather(small.astype(BF), 'z', axis=0, tiled=False)  30.6 us
    all_to_all x1, starting transfers between devices, on_device(): lax.all_to_all(send, 'exp', split_axis=0, concat_axis=0, tiled=True)  16.6 us
    all_to_all x1, waiting for transfers between devices, on_device(): lax.all_to_all(send, 'exp', split_axis=0, concat_axis=0, tiled=True)  8.67 us
    pallas_call x1, Pallas kernels, partial_sums(): pl.pallas_call(kernel, out_shape=jax.ShapeDtypeStruct((z_width * chunk, e...  6.03 us
    all_to_all x1, starting transfers between devices, on_device(): lax.all_to_all(weight_grad.astype(BF).reshape(exp_local, most, source_cou...  4.86 us
  transfers between devices with their start and end apart: 6, of which 4 were waited for; matrix products, arithmetic and copies ran while one was open for 7% of the time, Pallas kernels for 0%

profile of v3, /device:TPU:8, one launch (start us, length us, event | category | flops | bytes accessed | tf_op | source)
XLA Modules:
  0.0 154.6 jit_solution(3661246769562373742)
XLA Ops:
  0.6 0.0 copy-start
  0.6 0.0 copy-start.1
  0.7 0.8 convert_element_type.218
  1.5 0.7 convert_bitcast_fusion.1
  2.2 0.8 fusion.16
  2.9 0.1 fusion.30
  3.1 0.1 pad.5.clone
  3.1 0.8 select_reduce_fusion.2
  4.0 0.0 copy-start.7
  4.0 0.6 convolution_convert_fusion
  4.6 0.9 maximum_maximum_fusion
  5.5 16.6 %all-to-all-start = ((bf16[32,56,128]{2,1,0:T(8,128)(2,1)}), bf16[32,56,128]{2,1,0:T(8,128)(2,1)S(1)}, u32[]{:S(2)}, u32[]{:S(2)}) async-start(bf16[32,56,128]{2,1,0:T(8,128)(2,1)} %maximum_maximum_fusion), calls=%async_computation | async-start | bytes 917504 | tf_op jit(solution)/shard_map/all_to_all | solution.py:126
  22.2 0.9 dynamic-slice_bitcast_fusion
  23.1 1.9 %collective-permute-start = (bf16[4,16,48,128]{3,2,1,0:T(8,128)(2,1)}, bf16[4,16,48,128]{3,2,1,0:T(8,128)(2,1)S(1)}, u32[]{:S(2)}, u32[]{:S(2)}) collective-permute-start(bf16[4,16,48,128]{3,2,1,0:T(8,128)(2,1)} %dynamic-slice_bitcast_fusion), channel_id=1, source_target_pairs={{0,1},{1,0},{2,3},{3,2},{4,5},{5,4},{6,7},{7,6},{8,9},{9,8},{10,11... | collective-permute-start | bytes 2359304 | tf_op jit(solution)/shard_map/ppermute | solution.py:96
  25.0 0.1 convert_element_type.266
  25.1 0.2 copy.49
  25.4 0.1 convert_element_type.267
  25.5 0.2 copy.50
  25.7 0.8 multiply_convert_fusion.19.h_ref
  26.5 8.7 %all-to-all-done = bf16[32,56,128]{2,1,0:T(8,128)(2,1)S(1)} async-done(((bf16[32,56,128]{2,1,0:T(8,128)(2,1)}), bf16[32,56,128]{2,1,0:T(8,128)(2,1)S(1)}, u32[]{:S(2)}, u32[]{:S(2)}) %all-to-all-start) | async-done | bytes 458784 | tf_op jit(solution)/shard_map/all_to_all | solution.py:126
  35.2 0.1 copy.51
  35.3 0.0 copy-start.2
  35.4 1.9 %collective-permute-start.1 = (bf16[4,384,128]{2,1,0:T(8,128)(2,1)S(1)}, bf16[4,384,128]{2,1,0:T(8,128)(2,1)S(1)}, u32[]{:S(2)}, u32[]{:S(2)}) collective-permute-start(bf16[4,384,128]{2,1,0:T(8,128)(2,1)S(1)} %bitcast.99), channel_id=1, source_target_pairs={{0,1},{1,0},{2,3},{3,2},{4,5},{5,4},{6,7},{7,6},{8,9},{9,8},{10,11... | collective-permute-start | bytes 1179656 | tf_op jit(solution)/shard_map/ppermute | solution.py:129
  37.3 0.1 fusion.31
  37.5 0.6 select_reduce_fusion.1
  38.1 0.7 broadcast_in_dim_reshape.3.t_ref
  38.7 0.2 collective-permute-done.1.xp_ref
  39.0 0.7 copy-done.5
  39.6 0.1 copy-done.9
  39.7 6.0 %partial_sums.1 = bf16[1008,1536]{1,0:T(8,128)(2,1)} custom-call(s32[1]{0:T(128)} %bitcast.7.core_ref, f32[4,1,384]{2,1,0:T(1,128)} %broadcast_in_dim_reshape.3.t_ref, bf16[4,48,384]{2,1,0:T(8,128)(2,1)} %multiply_convert_fusion.19.h_ref, bf16[4,8,48,64]{3,2,1,0:T(8,128)(2,1)} %a_ref.1, bf16[4,8,64,128]{3,2,1,0:T(8,128)(2,1)} %b_ref.1, ...), custom_call_target="tpu_custom_call" | custom-call | tf_op jit(solution)/shard_map/partial_sums/pallas_call | solution.py:49
  45.8 53.7 %fusion = bf16[64,1536]{1,0:T(8,128)(2,1)S(1)} fusion(bf16[1008,1536]{1,0:T(8,128)(2,1)} %partial_sums.1), kind=kCustom, calls=%all-reduce-scatter | all-reduce-scatter fusion | flops 1572865 | bytes 3297280
  99.5 2.5 %collective-permute-start.3 = (bf16[15,1536]{1,0:T(8,128)(2,1)S(1)}, bf16[15,1536]{1,0:T(8,128)(2,1)S(1)}, u32[]{:S(2)}, u32[]{:S(2)}) collective-permute-start(bf16[15,1536]{1,0:T(8,128)(2,1)S(1)} %slice.40), channel_id=1, source_target_pairs={{0,2},{2,4},{4,6},{6,8},{8,10},{10,12},{12,14},{14,16},{16,18},{18... | collective-permute-start | bytes 138248
  102.0 1.3 dynamic-slice.4
  103.9 0.1 eq.105
  104.0 0.3 concatenate.8
  104.3 0.1 constant_dynamic-slice_fusion
  104.4 0.1 fusion.22
  104.5 0.1 reshape.169
  104.6 1.9 %collective-permute-start.2 = (bf16[108,128]{1,0:T(8,128)(2,1)S(1)}, bf16[108,128]{1,0:T(8,128)(2,1)S(1)}, u32[]{:S(2)}, u32[]{:S(2)}) collective-permute-start(bf16[108,128]{1,0:T(8,128)(2,1)S(1)} %reshape.169), channel_id=1, source_target_pairs={{0,1},{1,0},{2,3},{3,2},{4,5},{5,4},{6,7},{7,6},{8,9},{9,8},{10,11... | collective-permute-start | bytes 82952 | tf_op jit(solution)/shard_map/ppermute | solution.py:177
  106.5 0.1 compare_convert_fusion
  106.6 0.1 mul.84
  106.7 1.0 collective-permute-done.2
  107.7 30.6 %all-gather.1 = bf16[16,108,128]{2,1,0:T(8,128)(2,1)S(1)} all-gather(bf16[1,108,128]{2,1,0:T(8,128)(2,1)S(1)} %fusion.35), channel_id=2, replica_groups=mesh['exp'=32,'z'=16,'core'=2] {'z'}, dimensions={0}, use_global_device_ids=true | all-gather | bytes 470016 | tf_op jit(solution)/shard_map/all_gather | solution.py:178
  138.4 0.5 reshape.170
  138.9 0.1 fusion.28
  139.0 0.1 multiply_reduce_fusion
  139.0 0.0 copy-start.8
  139.1 0.1 slice_convert_fusion
  139.1 0.1 reshape.179
  139.3 0.1 convert_element_type.258
  139.4 0.7 copy.60
  140.1 4.9 %all-to-all-start.1 = ((bf16[32,4,12]{2,1,0:T(4,128)(2,1)}), bf16[32,4,12]{2,1,0:T(4,128)(2,1)S(1)}, u32[]{:S(2)}, u32[]{:S(2)}) async-start(bf16[32,4,12]{2,1,0:T(4,128)(2,1)} %copy.60), calls=%async_computation.1 | async-start | bytes 65536 | tf_op jit(solution)/shard_map/all_to_all | solution.py:186
  145.0 0.1 reshape.178
  145.1 0.0 copy-start.3
  145.1 0.1 fusion.26
  145.4 0.5 multiply_convert_fusion.17
  145.8 0.0 copy-start.10
  145.9 0.3 copy-done.3
  146.1 1.4 fusion.10
  147.5 1.9 %fusion.12 = bf16[4,8,48,64]{3,2,1,0:T(8,128)(2,1)} fusion(f32[64,4,384]{2,0,1:T(8,128)S(1)} %copy.54, f32[8,4,384]{2,0,1:T(8,128)S(1)} %compare_convert_fusion, bf16[4,48,384]{2,1,0:T(8,128)(2,1)S(1)} %copy-done.4), kind=kOutput, calls=%fused_computation.15 | convolution fusion | flops 77168640 | bytes 786432 | tf_op jit(solution)/shard_map/tres,efs->etfr/dot_general | solution.py:200
  149.3 0.9 copy.58
  150.3 0.9 copy.57
  151.2 2.6 %all-to-all-done.1 = bf16[32,4,12]{2,1,0:T(4,128)(2,1)S(1)} async-done(((bf16[32,4,12]{2,1,0:T(4,128)(2,1)}), bf16[32,4,12]{2,1,0:T(4,128)(2,1)S(1)}, u32[]{:S(2)}, u32[]{:S(2)}) %all-to-all-start.1) | async-done | bytes 3104 | tf_op jit(solution)/shard_map/all_to_all | solution.py:186
  153.8 0.8 fusion.15
  (33 shorter events, 0.3 us)
Async XLA Ops:
  0.6 3.3 %copy-start = (bf16[128,128]{1,0:T(8,128)(2,1)S(1)}, bf16[128,128]{1,0:T(8,128)(2,1)}, u32[]{:S(2)}) copy-start(bf16[128,128]{1,0:T(8,128)(2,1)} %param.9) | copy-start | bytes 98308
  0.6 21.5 %copy-start.1 = (bf16[4,1536,128]{2,1,0:T(8,128)(2,1)S(1)}, bf16[4,1536,128]{2,1,0:T(8,128)(2,1)}, u32[]{:S(2)}) copy-start(bf16[4,1536,128]{2,1,0:T(8,128)(2,1)} %param.15) | copy-start | bytes 4718596
  0.7 24.4 %copy-start.6 = (bf16[4,32,12,48]{3,1,2,0:T(8,128)(2,1)S(1)}, bf16[4,32,12,48]{3,1,2,0:T(8,128)(2,1)}, u32[]{:S(2)}) copy-start(bf16[4,32,12,48]{3,1,2,0:T(8,128)(2,1)} %param.13) | copy-start | bytes 442372
  4.0 21.4 %copy-start.7 = (bf16[4,32,12,48]{3,1,2,0:T(8,128)(2,1)S(1)}, bf16[4,32,12,48]{3,1,2,0:T(8,128)(2,1)}, u32[]{:S(2)}) copy-start(bf16[4,32,12,48]{3,1,2,0:T(8,128)(2,1)} %param.14) | copy-start | bytes 442372
  5.5 29.6 %all-to-all-start = ((bf16[32,56,128]{2,1,0:T(8,128)(2,1)}), bf16[32,56,128]{2,1,0:T(8,128)(2,1)S(1)}, u32[]{:S(2)}, u32[]{:S(2)}) async-start(bf16[32,56,128]{2,1,0:T(8,128)(2,1)} %maximum_maximum_fusion), calls=%async_computation | async-start | bytes 917504 | tf_op jit(solution)/shard_map/all_to_all | solution.py:126
  23.1 15.6 %collective-permute-start = (bf16[4,16,48,128]{3,2,1,0:T(8,128)(2,1)}, bf16[4,16,48,128]{3,2,1,0:T(8,128)(2,1)S(1)}, u32[]{:S(2)}, u32[]{:S(2)}) collective-permute-start(bf16[4,16,48,128]{3,2,1,0:T(8,128)(2,1)} %dynamic-slice_bitcast_fusion), channel_id=1, source_target_pairs={{0,1},{1,0},{2,3},{3,2},{4,5},{5,4},{6,7},{7,6},{8,9},{9,8},{10,11... | collective-permute-start | bytes 2359304 | tf_op jit(solution)/shard_map/ppermute | solution.py:96
  35.3 3.7 %copy-start.2 = (bf16[48,32,128]{2,1,0:T(8,128)(2,1)}, bf16[48,32,128]{2,1,0:T(8,128)(2,1)S(1)}, u32[]{:S(2)}) copy-start(bf16[48,32,128]{2,1,0:T(8,128)(2,1)S(1)} %copy.51) | copy-start | bytes 1179652
  35.4 3.6 %collective-permute-start.1 = (bf16[4,384,128]{2,1,0:T(8,128)(2,1)S(1)}, bf16[4,384,128]{2,1,0:T(8,128)(2,1)S(1)}, u32[]{:S(2)}, u32[]{:S(2)}) collective-permute-start(bf16[4,384,128]{2,1,0:T(8,128)(2,1)S(1)} %bitcast.99), channel_id=1, source_target_pairs={{0,1},{1,0},{2,3},{3,2},{4,5},{5,4},{6,7},{7,6},{8,9},{9,8},{10,11... | collective-permute-start | bytes 1179656 | tf_op jit(solution)/shard_map/ppermute | solution.py:129
  38.7 0.9 copy-start.5
  39.0 0.8 copy-start.9
  45.8 58.7 %copy-start.4 = (bf16[4,48,384]{2,1,0:T(8,128)(2,1)S(1)}, bf16[4,48,384]{2,1,0:T(8,128)(2,1)}, u32[]{:S(2)}) copy-start(bf16[4,48,384]{2,1,0:T(8,128)(2,1)} %multiply_convert_fusion.19.h_ref) | copy-start | bytes 442372
  99.5 4.6 %collective-permute-start.3 = (bf16[15,1536]{1,0:T(8,128)(2,1)S(1)}, bf16[15,1536]{1,0:T(8,128)(2,1)S(1)}, u32[]{:S(2)}, u32[]{:S(2)}) collective-permute-start(bf16[15,1536]{1,0:T(8,128)(2,1)S(1)} %slice.40), channel_id=1, source_target_pairs={{0,2},{2,4},{4,6},{6,8},{8,10},{10,12},{12,14},{14,16},{16,18},{18... | collective-permute-start | bytes 138248
  104.6 3.1 %collective-permute-start.2 = (bf16[108,128]{1,0:T(8,128)(2,1)S(1)}, bf16[108,128]{1,0:T(8,128)(2,1)S(1)}, u32[]{:S(2)}, u32[]{:S(2)}) collective-permute-start(bf16[108,128]{1,0:T(8,128)(2,1)S(1)} %reshape.169), channel_id=1, source_target_pairs={{0,1},{1,0},{2,3},{3,2},{4,5},{5,4},{6,7},{7,6},{8,9},{9,8},{10,11... | collective-permute-start | bytes 82952 | tf_op jit(solution)/shard_map/ppermute | solution.py:177
  139.0 6.3 %copy-start.8 = (bf16[4,8,48,64]{3,2,1,0:T(8,128)(2,1)S(1)}, bf16[4,8,48,64]{3,2,1,0:T(8,128)(2,1)}, u32[]{:S(2)}) copy-start(bf16[4,8,48,64]{3,2,1,0:T(8,128)(2,1)} %a_ref.1) | copy-start | bytes 589828
  140.1 13.7 %all-to-all-start.1 = ((bf16[32,4,12]{2,1,0:T(4,128)(2,1)}), bf16[32,4,12]{2,1,0:T(4,128)(2,1)S(1)}, u32[]{:S(2)}, u32[]{:S(2)}) async-start(bf16[32,4,12]{2,1,0:T(4,128)(2,1)} %copy.60), calls=%async_computation.1 | async-start | bytes 65536 | tf_op jit(solution)/shard_map/all_to_all | solution.py:186
  145.1 1.0 copy-start.3
  145.8 8.0 %copy-start.10 = (s32[128,8]{0,1:T(8,128)S(1)}, s32[128,8]{0,1:T(8,128)}, u32[]{:S(2)}) copy-start(s32[128,8]{0,1:T(8,128)} %param.10) | copy-start | bytes 12292

commit v4 on v3

--- a/solution.py
+++ b/solution.py
@@ -11,7 +11,7 @@
 PAD = 7
 
 
-def partial_sums(core, task_row, hidden, first, second, weight, weight_peer, rows, rows_peer):
+def partial_sums(core, task_row, hidden, first, second, weight, weight_peer, rows, rows_peer, order):
     exp_local, z_width, _, piece, width = weight.shape
     slots = rows.shape[1]
     task_count, rank = first.shape[1], first.shape[3]
@@ -20,51 +20,41 @@
 
     def kernel(core_ref, t_ref, h_ref, a_ref, b_ref, w_ref, wp_ref, x_ref, xp_ref, out_ref, f32_ref):
         nums = (((1,), (1,)), ((), ()))
-        x = x_ref[0]
-        own = w_ref[0, :, 0].reshape(z_width * piece, width)
-        peer = wp_ref[0].reshape(z_width * piece, width)
-        total = lax.dot_general(own, x, nums, preferred_element_type=F32)
-        total += lax.dot_general(peer, xp_ref[0], nums, preferred_element_type=F32)
-        ql_all = lax.dot_general(
-            b_ref[0].reshape(task_count * rank, width), x, nums, preferred_element_type=F32
-        )
-        lat = jnp.zeros((rank, slots), F32)
-        ql = jnp.zeros((rank, slots), F32)
-        for t in range(task_count):
-            keep = t_ref[0] == float(t)
-            part = lax.dot_general(
-                a_ref[0, t], h_ref[0], (((0,), (0,)), ((), ())), preferred_element_type=F32
+        core_at = core_ref[0]
+        for z in range(z_width):
+            f32_ref[(z + 1) * chunk - PAD : (z + 1) * chunk] = jnp.zeros((PAD, slots), F32)
+        for e in range(exp_local):
+            x = x_ref[e]
+            own = w_ref[e, :, core_at].reshape(z_width * piece, width)
+            peer = wp_ref[e].reshape(z_width * piece, width)
+            total = lax.dot_general(own, x, nums, preferred_element_type=F32)
+            total += lax.dot_general(peer, xp_ref[e], nums, preferred_element_type=F32)
+            ql_all = lax.dot_general(
+                b_ref[e].reshape(task_count * rank, width), x, nums, preferred_element_type=F32
             )
-            lat += jnp.where(keep, part, 0.0)
-            ql += jnp.where(keep, ql_all[t * rank : (t + 1) * rank], 0.0)
-        small = jnp.concatenate([lat, ql])
-        empty = jnp.zeros((PAD, slots), F32)
-        for z in range(z_width):
-            at = z * chunk
-            f32_ref[at : at + piece] = total[z * piece : (z + 1) * piece]
-            f32_ref[at + piece : at + piece + more] = small[z * more : (z + 1) * more]
-            f32_ref[at + piece + more : at + chunk] = empty
-        out_ref[...] = f32_ref[...].astype(BF)
-
+            lat = jnp.zeros((rank, slots), F32)
+            ql = jnp.zeros((rank, slots), F32)
+            for t in range(task_count):
+                keep = t_ref[e : e + 1] == float(t)
+                part = lax.dot_general(
+                    a_ref[e, t], h_ref[e], (((0,), (0,)), ((), ())), preferred_element_type=F32
+                )
+                lat += jnp.where(keep, part, 0.0)
+                ql += jnp.where(keep, ql_all[t * rank : (t + 1) * rank], 0.0)
+            small = jnp.concatenate([lat, ql])
+            for z in range(z_width):
+                at, line = z * chunk, order[z] * more
+                f32_ref[at : at + piece] = total[z * piece : (z + 1) * piece]
+                f32_ref[at + piece : at + piece + more] = small[line : line + more]
+            out_ref[:, e * slots : (e + 1) * slots] = f32_ref[...].astype(BF)
+
+    vmem = pl.BlockSpec(memory_space=pltpu.VMEM)
     return pl.pallas_call(
         kernel,
         out_shape=jax.ShapeDtypeStruct((z_width * chunk, exp_local * slots), BF),
-        grid_spec=pltpu.PrefetchScalarGridSpec(
-            num_scalar_prefetch=1,
-            grid=(exp_local,),
-            in_specs=[
-                pl.BlockSpec((1, 1, slots), lambda e, c: (e, 0, 0)),
-                pl.BlockSpec((1, piece, slots), lambda e, c: (e, 0, 0)),
-                pl.BlockSpec((1, task_count, piece, rank), lambda e, c: (e, 0, 0, 0)),
-                pl.BlockSpec((1, task_count, rank, width), lambda e, c: (e, 0, 0, 0)),
-                pl.BlockSpec((1, z_width, 1, piece, width), lambda e, c: (e, 0, c[0], 0, 0)),
-                pl.BlockSpec((1, z_width, piece, width), lambda e, c: (e, 0, 0, 0)),
-                pl.BlockSpec((1, slots, width), lambda e, c: (e, 0, 0)),
-                pl.BlockSpec((1, slots, width), lambda e, c: (e, 0, 0)),
-            ],
-            out_specs=pl.BlockSpec((z_width * chunk, slots), lambda e, c: (0, e)),
-            scratch_shapes=[pltpu.VMEM((z_width * chunk, slots), F32)],
-        ),
+        in_specs=[pl.BlockSpec(memory_space=pltpu.SMEM)] + [vmem] * 8,
+        out_specs=vmem,
+        scratch_shapes=[pltpu.VMEM((z_width * chunk, slots), F32)],
         name="partial_sums",
     )(core.reshape(1), task_row, hidden, first, second, weight, weight_peer, rows, rows_peer)
 
@@ -81,7 +71,8 @@
     adapter_second_factor,
 ):
     exp_width = lax.axis_size("exp")
-    z_width = lax.axis_size("z")
+    zh_width, zl_width = lax.axis_size("zh"), lax.axis_size("zl")
+    z_width = zh_width * zl_width
     core = lax.axis_index("core")
     exp_local, source_count, most, piece = saved_gate_input.shape
     tok_count, top = routed_expert_index.shape
@@ -157,7 +148,7 @@
 
     partial = partial_sums(
         core.astype(jnp.int32),
-        task_slot[:, None],
+        task_slot,
         hidden,
         adapter_first_factor,
         adapter_second_factor,
@@ -165,8 +156,9 @@
         weight_peer,
         rows,
         rows_peer,
-    )
-    summed = lax.psum_scatter(partial, "z", scatter_dimension=0, tiled=True)
+        [z % zl_width * zh_width + z // zl_width for z in range(z_width)],
+    )
+    summed = lax.psum_scatter(partial, ("zh", "zl"), scatter_dimension=0, tiled=True)
     summed = lax.optimization_barrier(summed)
     back = summed[:piece].astype(F32).reshape(piece, exp_local, per_expert).transpose(1, 0, 2)
 
@@ -175,7 +167,8 @@
     small = jnp.concatenate([summed[piece : piece + more], pair_part.astype(BF)])
     small = small.reshape(-1, 128)
     small = small.astype(F32) + lax.ppermute(small, "core", swap).astype(F32)
-    everything = lax.all_gather(small.astype(BF), "z", axis=0, tiled=False)
+    everything = lax.all_gather(small.astype(BF), "zh", axis=0, tiled=False)
+    everything = lax.all_gather(everything, "zl", axis=0, tiled=False)
     everything = everything.reshape(z_width, more + 1, total_slots)
     split = (rank, exp_local, per_expert)
     latent = everything[: z_width // 2, :more].reshape(split).astype(F32)
@@ -230,8 +223,10 @@
 
 def solution(mesh):
     exp_width, seq_width = mesh.shape["exp"], mesh.shape["seq"]
-    split = Mesh(mesh.devices.reshape(exp_width, seq_width // 2, 2), ("exp", "z", "core"))
-    seq = ("z", "core")
+    split = Mesh(
+        mesh.devices.reshape(exp_width, 4, seq_width // 8, 2), ("exp", "zh", "zl", "core")
+    )
+    seq = ("zh", "zl", "core")
     placed = (
         P("exp", seq),
         P("exp", None),

time: 155 us -> 158 us (1.019)
  blocking collectives: 84.3 us -> 87.1 us
    all_gather x1 -> x2, blocking collectives: 30.6 us -> 33.5 us  [the longest x1 18.4 us: on_device(): everything = lax.all_gather(small.astype(BF), 'zh', axis=0, tiled=False)]
where the time goes in v4:
time: 158 us
  blocking collectives  87.1 us (55%)
  starting transfers between devices  29.8 us (19%)
  waiting for transfers between devices  12.4 us (8%)
  local copies, waits for them, and re-layouts  8.73 us (6%)
  Pallas kernels  6.65 us (4%)
  other arithmetic  6.07 us (4%)
  matrix products  5.35 us (3%)
  between operations  1.74 us (1%)
    unnamed x1, blocking collectives  53.6 us
    all_gather x1, blocking collectives, on_device(): everything = lax.all_gather(small.astype(BF), 'zh', axis=0, tiled=False)  18.4 us
    all_to_all x1, starting transfers between devices, on_device(): lax.all_to_all(send, 'exp', split_axis=0, concat_axis=0, tiled=True)  16.6 us
    all_gather x1, blocking collectives, on_device(): everything = lax.all_gather(everything, 'zl', axis=0, tiled=False)  15.1 us
    all_to_all x1, waiting for transfers between devices, on_device(): lax.all_to_all(send, 'exp', split_axis=0, concat_axis=0, tiled=True)  8.67 us
    pallas_call x1, Pallas kernels, partial_sums(): pl.pallas_call(kernel, out_shape=jax.ShapeDtypeStruct((z_width * chunk, e...  6.65 us
    all_to_all x1, starting transfers between devices, on_device(): lax.all_to_all(weight_grad.astype(BF).reshape(exp_local, most, source_cou...  4.83 us
  transfers between devices with their start and end apart: 6, of which 4 were waited for; matrix products, arithmetic and copies ran while one was open for 7% of the time, Pallas kernels for 0%

profile of v4, /device:TPU:8, one launch (start us, length us, event | category | flops | bytes accessed | tf_op | source)
XLA Modules:
  0.0 157.8 jit_solution(10349644379965506145)
XLA Ops:
  0.6 0.0 copy-start
  0.6 0.0 copy-start.1
  0.7 0.9 fusion.16
  1.6 0.1 fusion.30
  1.7 0.7 convert_bitcast_fusion.1
  2.4 0.7 convert_element_type.218
  3.1 0.8 select_reduce_fusion.2
  3.9 0.1 pad.5.clone
  4.0 0.6 convolution_convert_fusion
  4.6 0.9 maximum_maximum_fusion
  5.5 16.6 %all-to-all-start = ((bf16[32,56,128]{2,1,0:T(8,128)(2,1)}), bf16[32,56,128]{2,1,0:T(8,128)(2,1)S(1)}, u32[]{:S(2)}, u32[]{:S(2)}) async-start(bf16[32,56,128]{2,1,0:T(8,128)(2,1)} %maximum_maximum_fusion), calls=%async_computation | async-start | bytes 917504 | tf_op jit(solution)/shard_map/all_to_all | solution.py:117
  22.2 0.9 dynamic-slice_bitcast_fusion
  23.1 1.9 %collective-permute-start = (bf16[4,16,48,128]{3,2,1,0:T(8,128)(2,1)}, bf16[4,16,48,128]{3,2,1,0:T(8,128)(2,1)S(1)}, u32[]{:S(2)}, u32[]{:S(2)}) collective-permute-start(bf16[4,16,48,128]{3,2,1,0:T(8,128)(2,1)} %dynamic-slice_bitcast_fusion), channel_id=1, source_target_pairs={{0,1},{1,0},{2,3},{3,2},{4,5},{5,4},{6,7},{7,6},{8,9},{9,8},{10,11... | collective-permute-start | bytes 2359304 | tf_op jit(solution)/shard_map/ppermute | solution.py:87
  25.0 0.1 convert_element_type.266
  25.1 0.2 copy.47
  25.4 0.0 copy-done.7
  25.4 0.1 convert_element_type.267
  25.5 0.2 copy.48
  25.7 0.8 multiply_convert_fusion.19.h_ref
  26.5 8.7 %all-to-all-done = bf16[32,56,128]{2,1,0:T(8,128)(2,1)S(1)} async-done(((bf16[32,56,128]{2,1,0:T(8,128)(2,1)}), bf16[32,56,128]{2,1,0:T(8,128)(2,1)S(1)}, u32[]{:S(2)}, u32[]{:S(2)}) %all-to-all-start) | async-done | bytes 458784 | tf_op jit(solution)/shard_map/all_to_all | solution.py:117
  35.2 0.1 copy.49
  35.3 0.0 copy-start.2
  35.3 1.9 %collective-permute-start.1 = (bf16[4,384,128]{2,1,0:T(8,128)(2,1)S(1)}, bf16[4,384,128]{2,1,0:T(8,128)(2,1)S(1)}, u32[]{:S(2)}, u32[]{:S(2)}) collective-permute-start(bf16[4,384,128]{2,1,0:T(8,128)(2,1)S(1)} %bitcast.99), channel_id=1, source_target_pairs={{0,1},{1,0},{2,3},{3,2},{4,5},{5,4},{6,7},{7,6},{8,9},{9,8},{10,11... | collective-permute-start | bytes 1179656 | tf_op jit(solution)/shard_map/ppermute | solution.py:120
  37.3 0.1 fusion.31
  37.5 0.6 select_reduce_fusion.1
  38.0 0.7 reshape.169.t_ref
  38.7 0.2 collective-permute-done.1.xp_ref
  39.0 0.7 copy-done.5
  39.6 0.1 copy-done.9
  39.7 6.7 %partial_sums.1 = bf16[1008,1536]{1,0:T(8,128)(2,1)} custom-call(s32[1]{0:T(128)} %bitcast.7.core_ref, f32[4,384]{1,0:T(4,128)} %reshape.169.t_ref, bf16[4,48,384]{2,1,0:T(8,128)(2,1)} %multiply_convert_fusion.19.h_ref, bf16[4,8,48,64]{3,2,1,0:T(8,128)(2,1)} %a_ref.1, bf16[4,8,64,128]{3,2,1,0:T(8,128)(2,1)} %b_ref.1, bf16[4,16,2,48,128]{4,3,2,1,0:T(8,128)(2,1)} %bitcast.95, ...), custom_call_target="tpu_custom_call" | custom-call | tf_op jit(solution)/shard_map/partial_sums/pallas_call | solution.py:52
  46.4 53.6 %fusion = bf16[64,1536]{1,0:T(8,128)(2,1)S(1)} fusion(bf16[1008,1536]{1,0:T(8,128)(2,1)} %partial_sums.1), kind=kCustom, calls=%all-reduce-scatter | all-reduce-scatter fusion | flops 1572865 | bytes 3297280
  100.0 2.6 %collective-permute-start.3 = (bf16[15,1536]{1,0:T(8,128)(2,1)S(1)}, bf16[15,1536]{1,0:T(8,128)(2,1)S(1)}, u32[]{:S(2)}, u32[]{:S(2)}) collective-permute-start(bf16[15,1536]{1,0:T(8,128)(2,1)S(1)} %slice.40), channel_id=1, source_target_pairs={{0,2},{2,4},{4,6},{6,8},{8,10},{10,12},{12,14},{14,16},{16,18},{18... | collective-permute-start | bytes 138248
  102.6 1.3 dynamic-slice.4
  104.6 0.3 concatenate.8
  104.9 0.1 constant_dynamic-slice_fusion
  105.0 0.1 fusion.22
  105.1 0.1 reshape.173
  105.1 1.9 %collective-permute-start.2 = (bf16[108,128]{1,0:T(8,128)(2,1)S(1)}, bf16[108,128]{1,0:T(8,128)(2,1)S(1)}, u32[]{:S(2)}, u32[]{:S(2)}) collective-permute-start(bf16[108,128]{1,0:T(8,128)(2,1)S(1)} %reshape.173), channel_id=1, source_target_pairs={{0,1},{1,0},{2,3},{3,2},{4,5},{5,4},{6,7},{7,6},{8,9},{9,8},{10,11... | collective-permute-start | bytes 82952 | tf_op jit(solution)/shard_map/ppermute | solution.py:169
  107.1 0.1 compare_convert_fusion
  107.2 0.1 mul.84
  107.2 1.0 collective-permute-done.2
  108.3 18.4 %all-gather.2 = bf16[4,108,128]{2,1,0:T(8,128)(2,1)S(1)} all-gather(bf16[1,108,128]{2,1,0:T(8,128)(2,1)S(1)} %fusion.35), channel_id=2, replica_groups=mesh['exp'=32,'zh'=4,'zl'=4,'core'=2] {'zh'}, dimensions={0}, use_global_device_ids=true | all-gather | bytes 138240 | tf_op jit(solution)/shard_map/all_gather | solution.py:170
  126.6 15.1 %all-gather.1 = bf16[16,108,128]{2,1,0:T(8,128)(2,1)S(1)} all-gather(bf16[4,108,128]{2,1,0:T(8,128)(2,1)S(1)} %all-gather.2), channel_id=3, replica_groups=mesh['exp'=32,'zh'=4,'zl'=4,'core'=2] {'zl'}, dimensions={0}, use_global_device_ids=true | all-gather | bytes 552960 | tf_op jit(solution)/shard_map/all_gather | solution.py:171
  141.7 0.5 reshape.174
  142.2 0.1 fusion.28
  142.3 0.1 multiply_reduce_fusion
  142.4 0.0 copy-start.8
  142.4 0.1 slice_convert_fusion
  142.5 0.1 convert_element_type.258
  142.6 0.7 copy.57
  143.3 4.8 %all-to-all-start.1 = ((bf16[32,4,12]{2,1,0:T(4,128)(2,1)}), bf16[32,4,12]{2,1,0:T(4,128)(2,1)S(1)}, u32[]{:S(2)}, u32[]{:S(2)}) async-start(bf16[32,4,12]{2,1,0:T(4,128)(2,1)} %copy.57), calls=%async_computation.1 | async-start | bytes 65536 | tf_op jit(solution)/shard_map/all_to_all | solution.py:179
  148.2 0.1 reshape.182
  148.3 0.1 reshape.183
  148.5 0.0 copy-start.3
  148.5 0.1 fusion.26
  148.7 0.5 multiply_convert_fusion.17
  149.2 0.0 copy-start.11
  149.2 0.3 copy-done.3
  149.5 1.4 fusion.10
  150.8 1.8 %fusion.12 = bf16[4,8,48,64]{3,2,1,0:T(8,128)(2,1)} fusion(f32[64,4,384]{2,0,1:T(8,128)S(1)} %copy.51, f32[8,4,384]{2,0,1:T(8,128)S(1)} %compare_convert_fusion, bf16[4,48,384]{2,1,0:T(8,128)(2,1)S(1)} %copy-done.4), kind=kOutput, calls=%fused_computation.15 | convolution fusion | flops 77168640 | bytes 786432 | tf_op jit(solution)/shard_map/tres,efs->etfr/dot_general | solution.py:193
  152.7 0.9 copy.54
  153.6 0.9 copy.55
  154.5 2.5 %all-to-all-done.1 = bf16[32,4,12]{2,1,0:T(4,128)(2,1)S(1)} async-done(((bf16[32,4,12]{2,1,0:T(4,128)(2,1)}), bf16[32,4,12]{2,1,0:T(4,128)(2,1)S(1)}, u32[]{:S(2)}, u32[]{:S(2)}) %all-to-all-start.1) | async-done | bytes 3104 | tf_op jit(solution)/shard_map/all_to_all | solution.py:179
  157.0 0.8 fusion.15
  (35 shorter events, 0.3 us)
Async XLA Ops:
  0.6 3.3 %copy-start = (bf16[128,128]{1,0:T(8,128)(2,1)S(1)}, bf16[128,128]{1,0:T(8,128)(2,1)}, u32[]{:S(2)}) copy-start(bf16[128,128]{1,0:T(8,128)(2,1)} %param.9) | copy-start | bytes 98308
  0.6 21.5 %copy-start.1 = (bf16[4,1536,128]{2,1,0:T(8,128)(2,1)S(1)}, bf16[4,1536,128]{2,1,0:T(8,128)(2,1)}, u32[]{:S(2)}) copy-start(bf16[4,1536,128]{2,1,0:T(8,128)(2,1)} %param.15) | copy-start | bytes 4718596
  0.7 24.4 %copy-start.6 = (bf16[4,32,12,48]{3,1,2,0:T(8,128)(2,1)S(1)}, bf16[4,32,12,48]{3,1,2,0:T(8,128)(2,1)}, u32[]{:S(2)}) copy-start(bf16[4,32,12,48]{3,1,2,0:T(8,128)(2,1)} %param.13) | copy-start | bytes 442372
  3.9 21.4 %copy-start.7 = (bf16[4,32,12,48]{3,1,2,0:T(8,128)(2,1)S(1)}, bf16[4,32,12,48]{3,1,2,0:T(8,128)(2,1)}, u32[]{:S(2)}) copy-start(bf16[4,32,12,48]{3,1,2,0:T(8,128)(2,1)} %param.14) | copy-start | bytes 442372
  5.5 29.6 %all-to-all-start = ((bf16[32,56,128]{2,1,0:T(8,128)(2,1)}), bf16[32,56,128]{2,1,0:T(8,128)(2,1)S(1)}, u32[]{:S(2)}, u32[]{:S(2)}) async-start(bf16[32,56,128]{2,1,0:T(8,128)(2,1)} %maximum_maximum_fusion), calls=%async_computation | async-start | bytes 917504 | tf_op jit(solution)/shard_map/all_to_all | solution.py:117
  23.1 15.6 %collective-permute-start = (bf16[4,16,48,128]{3,2,1,0:T(8,128)(2,1)}, bf16[4,16,48,128]{3,2,1,0:T(8,128)(2,1)S(1)}, u32[]{:S(2)}, u32[]{:S(2)}) collective-permute-start(bf16[4,16,48,128]{3,2,1,0:T(8,128)(2,1)} %dynamic-slice_bitcast_fusion), channel_id=1, source_target_pairs={{0,1},{1,0},{2,3},{3,2},{4,5},{5,4},{6,7},{7,6},{8,9},{9,8},{10,11... | collective-permute-start | bytes 2359304 | tf_op jit(solution)/shard_map/ppermute | solution.py:87
  35.3 3.6 %copy-start.2 = (bf16[48,32,128]{2,1,0:T(8,128)(2,1)}, bf16[48,32,128]{2,1,0:T(8,128)(2,1)S(1)}, u32[]{:S(2)}) copy-start(bf16[48,32,128]{2,1,0:T(8,128)(2,1)S(1)} %copy.49) | copy-start | bytes 1179652
  35.3 3.6 %collective-permute-start.1 = (bf16[4,384,128]{2,1,0:T(8,128)(2,1)S(1)}, bf16[4,384,128]{2,1,0:T(8,128)(2,1)S(1)}, u32[]{:S(2)}, u32[]{:S(2)}) collective-permute-start(bf16[4,384,128]{2,1,0:T(8,128)(2,1)S(1)} %bitcast.99), channel_id=1, source_target_pairs={{0,1},{1,0},{2,3},{3,2},{4,5},{5,4},{6,7},{7,6},{8,9},{9,8},{10,11... | collective-permute-start | bytes 1179656 | tf_op jit(solution)/shard_map/ppermute | solution.py:120
  38.7 0.9 copy-start.5
  39.0 0.8 copy-start.9
  46.4 58.6 %copy-start.4 = (bf16[4,48,384]{2,1,0:T(8,128)(2,1)S(1)}, bf16[4,48,384]{2,1,0:T(8,128)(2,1)}, u32[]{:S(2)}) copy-start(bf16[4,48,384]{2,1,0:T(8,128)(2,1)} %multiply_convert_fusion.19.h_ref) | copy-start | bytes 442372
  46.4 60.7 %copy-start.10 = (f32[4,384]{1,0:T(4,128)S(1)}, f32[4,384]{1,0:T(4,128)}, u32[]{:S(2)}) copy-start(f32[4,384]{1,0:T(4,128)} %reshape.169.t_ref) | copy-start | bytes 18436
  100.0 4.6 %collective-permute-start.3 = (bf16[15,1536]{1,0:T(8,128)(2,1)S(1)}, bf16[15,1536]{1,0:T(8,128)(2,1)S(1)}, u32[]{:S(2)}, u32[]{:S(2)}) collective-permute-start(bf16[15,1536]{1,0:T(8,128)(2,1)S(1)} %slice.40), channel_id=1, source_target_pairs={{0,2},{2,4},{4,6},{6,8},{8,10},{10,12},{12,14},{14,16},{16,18},{18... | collective-permute-start | bytes 138248
  105.1 3.1 %collective-permute-start.2 = (bf16[108,128]{1,0:T(8,128)(2,1)S(1)}, bf16[108,128]{1,0:T(8,128)(2,1)S(1)}, u32[]{:S(2)}, u32[]{:S(2)}) collective-permute-start(bf16[108,128]{1,0:T(8,128)(2,1)S(1)} %reshape.173), channel_id=1, source_target_pairs={{0,1},{1,0},{2,3},{3,2},{4,5},{5,4},{6,7},{7,6},{8,9},{9,8},{10,11... | collective-permute-start | bytes 82952 | tf_op jit(solution)/shard_map/ppermute | solution.py:169
  142.4 6.3 %copy-start.8 = (bf16[4,8,48,64]{3,2,1,0:T(8,128)(2,1)S(1)}, bf16[4,8,48,64]{3,2,1,0:T(8,128)(2,1)}, u32[]{:S(2)}) copy-start(bf16[4,8,48,64]{3,2,1,0:T(8,128)(2,1)} %a_ref.1) | copy-start | bytes 589828
  143.3 13.7 %all-to-all-start.1 = ((bf16[32,4,12]{2,1,0:T(4,128)(2,1)}), bf16[32,4,12]{2,1,0:T(4,128)(2,1)S(1)}, u32[]{:S(2)}, u32[]{:S(2)}) async-start(bf16[32,4,12]{2,1,0:T(4,128)(2,1)} %copy.57), calls=%async_computation.1 | async-start | bytes 65536 | tf_op jit(solution)/shard_map/all_to_all | solution.py:179
  148.5 1.0 copy-start.3
  149.2 7.8 %copy-start.11 = (s32[128,8]{0,1:T(8,128)S(1)}, s32[128,8]{0,1:T(8,128)}, u32[]{:S(2)}) copy-start(s32[128,8]{0,1:T(8,128)} %param.10) | copy-start | bytes 12292

commit v5 on v3

--- a/solution.py
+++ b/solution.py
@@ -14,7 +14,7 @@
 def partial_sums(core, task_row, hidden, first, second, weight, weight_peer, rows, rows_peer):
     exp_local, z_width, _, piece, width = weight.shape
     slots = rows.shape[1]
-    task_count, rank = first.shape[1], first.shape[3]
+    task_count, rank = first.shape[1], first.shape[2]
     more = 2 * rank // z_width
     chunk = piece + more + PAD
 
@@ -23,19 +23,23 @@
         x = x_ref[0]
         own = w_ref[0, :, 0].reshape(z_width * piece, width)
         peer = wp_ref[0].reshape(z_width * piece, width)
-        total = lax.dot_general(own, x, nums, preferred_element_type=F32)
-        total += lax.dot_general(peer, xp_ref[0], nums, preferred_element_type=F32)
+        total = lax.dot_general(
+            jnp.concatenate([own, peer], axis=1),
+            jnp.concatenate([x, xp_ref[0]], axis=1),
+            nums,
+            preferred_element_type=F32,
+        )
         ql_all = lax.dot_general(
             b_ref[0].reshape(task_count * rank, width), x, nums, preferred_element_type=F32
+        )
+        lat_all = jnp.dot(
+            a_ref[0].reshape(task_count * rank, piece), h_ref[0], preferred_element_type=F32
         )
         lat = jnp.zeros((rank, slots), F32)
         ql = jnp.zeros((rank, slots), F32)
         for t in range(task_count):
             keep = t_ref[0] == float(t)
-            part = lax.dot_general(
-                a_ref[0, t], h_ref[0], (((0,), (0,)), ((), ())), preferred_element_type=F32
-            )
-            lat += jnp.where(keep, part, 0.0)
+            lat += jnp.where(keep, lat_all[t * rank : (t + 1) * rank], 0.0)
             ql += jnp.where(keep, ql_all[t * rank : (t + 1) * rank], 0.0)
         small = jnp.concatenate([lat, ql])
         empty = jnp.zeros((PAD, slots), F32)
@@ -55,7 +59,7 @@
             in_specs=[
                 pl.BlockSpec((1, 1, slots), lambda e, c: (e, 0, 0)),
                 pl.BlockSpec((1, piece, slots), lambda e, c: (e, 0, 0)),
-                pl.BlockSpec((1, task_count, piece, rank), lambda e, c: (e, 0, 0, 0)),
+                pl.BlockSpec((1, task_count, rank, piece), lambda e, c: (e, 0, 0, 0)),
                 pl.BlockSpec((1, task_count, rank, width), lambda e, c: (e, 0, 0, 0)),
                 pl.BlockSpec((1, z_width, 1, piece, width), lambda e, c: (e, 0, c[0], 0, 0)),
                 pl.BlockSpec((1, z_width, piece, width), lambda e, c: (e, 0, 0, 0)),
@@ -67,6 +71,52 @@
         ),
         name="partial_sums",
     )(core.reshape(1), task_row, hidden, first, second, weight, weight_peer, rows, rows_peer)
+
+
+def dispatch_slab(ids, gates, tasks, gradient, expert_count, exp_width, most):
+    top, tok_count = ids.shape
+    width = gradient.shape[1]
+    local = expert_count // exp_width
+    slab = local * most
+    lines = slab + local + 1
+    lines += -lines % 8
+
+    def kernel(id_ref, gate_ref, task_ref, grad_ref, out_ref):
+        expert = lax.broadcasted_iota(jnp.int32, (expert_count, tok_count), 0)
+        gate = gate_ref[...].astype(F32)
+        named = jnp.zeros((expert_count, tok_count), F32)
+        weight = jnp.zeros((expert_count, tok_count), F32)
+        for k in range(top):
+            here = id_ref[k : k + 1] == expert
+            named += jnp.where(here, 1.0, 0.0)
+            weight += jnp.where(here, gate[k : k + 1], 0.0)
+        before = lax.broadcasted_iota(jnp.int32, (tok_count, tok_count), 0)
+        after = lax.broadcasted_iota(jnp.int32, (tok_count, tok_count), 1)
+        earlier = jnp.where(before < after, 1.0, 0.0).astype(BF)
+        place = jnp.dot(named.astype(BF), earlier, preferred_element_type=F32)
+        place = jnp.where(named > 0.0, place, -1.0).astype(BF)
+        row = lax.broadcasted_iota(jnp.int32, (expert_count * most, expert_count), 0)
+        col = lax.broadcasted_iota(jnp.int32, (expert_count * most, expert_count), 1)
+        offset = row - col * most
+        spread = jnp.where((offset >= 0) & (offset < most), 1.0, 0.0).astype(BF)
+        column = lax.broadcasted_iota(jnp.int32, (expert_count, 128), 0)
+        place_row = jnp.dot(spread, place, preferred_element_type=F32)
+        first = jnp.dot(spread, column.astype(F32).astype(BF), preferred_element_type=F32)
+        row_at = lax.broadcasted_iota(jnp.int32, (expert_count * most, tok_count), 0).astype(F32)
+        picked = jnp.where(place_row == row_at - first * float(most), 1.0, 0.0).astype(BF)
+        rows = jnp.dot(picked, grad_ref[...], preferred_element_type=F32).astype(BF)
+        out_ref[:, :slab] = rows.reshape(exp_width, slab, width)
+        task = task_ref[...].astype(F32)
+        empty = jnp.zeros((lines - slab - local - 1, tok_count), F32)
+        for g in range(exp_width):
+            tail = [weight[g * local : (g + 1) * local], task, empty]
+            out_ref[g, slab:] = jnp.concatenate(tail).astype(BF)
+
+    return pl.pallas_call(
+        kernel,
+        out_shape=jax.ShapeDtypeStruct((exp_width, lines, width), BF),
+        name="dispatch_slab",
+    )(ids, gates, tasks, gradient)
 
 
 def on_device(
@@ -102,26 +152,17 @@
     tokens = jnp.arange(tok_count, dtype=jnp.int32)
     names = ids[:, None, :] == experts[None, :, None]
     named = jnp.any(names, axis=0)
-    gates = jnp.sum(jnp.where(names, combine.T[:, None, :].astype(F32), 0.0), axis=0)
     earlier = (tokens[:, None] < tokens[None, :]).astype(BF)
     place = jnp.dot(named.astype(BF), earlier, preferred_element_type=F32)
-    place_or = jnp.where(named, place, -1.0).astype(BF)
-    row_of = jnp.arange(expert_count * most, dtype=jnp.int32)
-    spread = (row_of[:, None] // most == experts[None, :]).astype(BF)
-    picked = jnp.dot(spread, place_or, preferred_element_type=F32) == (
-        (row_of % most).astype(F32)[:, None]
-    )
-    send_rows = jnp.dot(picked.astype(BF), output_gradient, preferred_element_type=F32).astype(BF)
     slab = exp_local * most
-    extra = -(exp_local + 1) % 8
-    send = jnp.concatenate(
-        [
-            send_rows.reshape(exp_width, slab, width),
-            gates.astype(BF).reshape(exp_width, exp_local, tok_count),
-            jnp.broadcast_to(token_task_index.astype(BF), (exp_width, 1, tok_count)),
-            jnp.zeros((exp_width, extra, tok_count), BF),
-        ],
-        axis=1,
+    send = dispatch_slab(
+        ids,
+        combine.T,
+        token_task_index[None],
+        output_gradient,
+        expert_count,
+        exp_width,
+        most,
     )
     received = lax.all_to_all(send, "exp", split_axis=0, concat_axis=0, tiled=True)
 
@@ -159,7 +200,7 @@
         core.astype(jnp.int32),
         task_slot[:, None],
         hidden,
-        adapter_first_factor,
+        adapter_first_factor.swapaxes(2, 3),
         adapter_second_factor,
         weight,
         weight_peer,
@@ -173,9 +214,15 @@
     pair_part = jnp.sum(hidden.astype(F32) * back, axis=1).reshape(1, total_slots)
     more = 2 * rank // z_width
     small = jnp.concatenate([summed[piece : piece + more], pair_part.astype(BF)])
-    small = small.reshape(-1, 128)
-    small = small.astype(F32) + lax.ppermute(small, "core", swap).astype(F32)
-    everything = lax.all_gather(small.astype(BF), "z", axis=0, tiled=False)
+    small = small.reshape(2, -1, 128)
+    theirs = lax.dynamic_index_in_dim(small, 1 - core, axis=0, keepdims=False)
+    mine = lax.dynamic_index_in_dim(small, core, axis=0, keepdims=False).astype(F32)
+    mine = (mine + lax.ppermute(theirs, "core", swap).astype(F32)).astype(BF)
+    half = lax.all_gather(mine, "z", axis=0, tiled=False)
+    other = lax.ppermute(half, "core", swap)
+    everything = jnp.where(
+        core == 0, jnp.stack([half, other], axis=1), jnp.stack([other, half], axis=1)
+    )
     everything = everything.reshape(z_width, more + 1, total_slots)
     split = (rank, exp_local, per_expert)
     latent = everything[: z_width // 2, :more].reshape(split).astype(F32)

time: 155 us -> 155 us (level)
  the two profiles are of different devices: /device:TPU:8 before, /device:TPU:1 now
where the time goes in v5:
time: 155 us
  blocking collectives  71.2 us (46%)
  starting transfers between devices  52 us (34%)
  local copies, waits for them, and re-layouts  10 us (6%)
  Pallas kernels  8.23 us (5%)
  matrix products  4.76 us (3%)
  waiting for transfers between devices  4.21 us (3%)
  other arithmetic  2.31 us (1%)
  between operations  1.77 us (1%)
    unnamed x1, blocking collectives  49.3 us
    all_gather x1, blocking collectives, on_device(): half = lax.all_gather(mine, 'z', axis=0, tiled=False)  21.9 us
    all_to_all x1, starting transfers between devices, on_device(): lax.all_to_all(send, 'exp', split_axis=0, concat_axis=0, tiled=True)  10.5 us
    ppermute x1, starting transfers between devices, on_device(): other = lax.ppermute(half, 'core', swap)  9.48 us
    ppermute x1, starting transfers between devices, on_device(): lax.ppermute(lax.dynamic_index_in_dim(weight, 1 - core, axis=2, keepdims=...  9.45 us
    ppermute x1, starting transfers between devices, on_device(): rows_peer = lax.ppermute(rows, 'core', swap)  8.01 us
    ppermute x1, starting transfers between devices, on_device(): mine = (mine + lax.ppermute(theirs, 'core', swap).astype(F32)).astype(BF)  7.7 us
    pallas_call x1, Pallas kernels, partial_sums(): pl.pallas_call(kernel, out_shape=jax.ShapeDtypeStruct((z_width * chunk, e...  5.77 us
  transfers between devices with their start and end apart: 7, of which 3 were waited for; matrix products, arithmetic and copies ran while one was open for 8% of the time, Pallas kernels for 0%

profile of v5, /device:TPU:1, one launch (start us, length us, event | category | flops | bytes accessed | tf_op | source)
XLA Modules:
  0.0 154.5 jit_solution(9466475527275234490)
XLA Ops:
  0.6 0.0 copy-start.4
  0.7 2.5 %dispatch_slab.1 = bf16[32,56,128]{2,1,0:T(8,128)(2,1)} custom-call(s32[8,128]{1,0:T(8,128)} %bitcast.115, bf16[8,128]{1,0:T(8,128)(2,1)} %bitcast.123, s32[1,128]{1,0:T(1,128)} %bitcast.124, bf16[128,128]{1,0:T(8,128)(2,1)} %grad_ref.1), custom_call_target="tpu_custom_call" | custom-call | tf_op jit(solution)/shard_map/dispatch_slab/pallas_call | solution.py:115
  3.1 10.5 %all-to-all-start = ((bf16[32,56,128]{2,1,0:T(8,128)(2,1)}), bf16[32,56,128]{2,1,0:T(8,128)(2,1)S(1)}, u32[]{:S(2)}, u32[]{:S(2)}) async-start(bf16[32,56,128]{2,1,0:T(8,128)(2,1)} %dispatch_slab.1), calls=%async_computation | async-start | bytes 917504 | tf_op jit(solution)/shard_map/all_to_all | solution.py:167
  13.6 1.2 dynamic-slice_bitcast_fusion
  14.9 0.0 copy-start.8
  14.9 9.4 %collective-permute-start = (bf16[4,16,48,128]{3,2,1,0:T(8,128)(2,1)S(1)}, bf16[4,16,48,128]{3,2,1,0:T(8,128)(2,1)}, u32[]{:S(2)}, u32[]{:S(2)}) collective-permute-start(bf16[4,16,48,128]{3,2,1,0:T(8,128)(2,1)S(1)} %dynamic-slice_bitcast_fusion), channel_id=1, source_target_pairs={{0,1},{1,0},{2,3},{3,2},{4,5},{5,4},{6,7},{7,6},{8,9},{9,8},{10,11... | collective-permute-start | bytes 2359304 | tf_op jit(solution)/shard_map/ppermute | solution.py:146
  24.3 1.0 copy.65
  25.4 0.1 convert_element_type.230
  25.4 0.2 copy.63
  25.7 0.0 copy-done.7
  25.7 0.1 convert_element_type.231
  25.8 0.2 copy.64
  26.1 0.1 fusion.16
  26.1 0.1 fusion.26
  26.3 0.8 multiply_convert_fusion.19.h_ref
  27.0 0.0 all-to-all-done
  27.1 0.1 copy.66
  27.2 0.0 copy-start
  27.2 8.0 %collective-permute-start.1 = (bf16[4,384,128]{2,1,0:T(8,128)(2,1)S(1)}, bf16[4,384,128]{2,1,0:T(8,128)(2,1)S(1)}, u32[]{:S(2)}, u32[]{:S(2)}) collective-permute-start(bf16[4,384,128]{2,1,0:T(8,128)(2,1)S(1)} %bitcast.104), channel_id=1, source_target_pairs={{0,1},{1,0},{2,3},{3,2},{4,5},{5,4},{6,7},{7,6},{8,9},{9,8},{10,11... | collective-permute-start | bytes 1179656 | tf_op jit(solution)/shard_map/ppermute | solution.py:170
  35.3 0.1 fusion.28
  35.5 0.6 select_reduce_fusion.1
  36.0 0.7 broadcast_in_dim_reshape.3.t_ref
  36.7 0.0 collective-permute-done.wp_ref
  36.7 0.0 collective-permute-done.1.xp_ref
  36.7 0.7 copy-done.3
  37.5 5.8 %partial_sums.1 = bf16[1008,1536]{1,0:T(8,128)(2,1)} custom-call(s32[1]{0:T(128)} %bitcast.6.core_ref, f32[4,1,384]{2,1,0:T(1,128)} %broadcast_in_dim_reshape.3.t_ref, bf16[4,48,384]{2,1,0:T(8,128)(2,1)} %multiply_convert_fusion.19.h_ref, bf16[4,8,64,48]{3,2,1,0:T(8,128)(2,1)} %bitcast.103, bf16[4,8,64,128]{3,2,1,0:T(8,128)(2,1)} %b_ref.1, ...), custom_call_target="tpu_custom_call" | custom-call | tf_op jit(solution)/shard_map/partial_sums/pallas_call | solution.py:53
  43.2 49.3 %fusion = bf16[64,1536]{1,0:T(8,128)(2,1)S(1)} fusion(bf16[1008,1536]{1,0:T(8,128)(2,1)} %partial_sums.1), kind=kCustom, calls=%all-reduce-scatter | all-reduce-scatter fusion | flops 1572865 | bytes 3297280
  92.5 1.5 collective-permute-start.4
  94.0 0.1 select_reduce_fusion.2
  94.1 1.3 dynamic-slice.4
  96.0 0.0 collective-permute-done.4
  96.0 0.3 concatenate.4
  96.3 0.1 constant_dynamic-slice_fusion
  96.5 0.1 fusion.19
  96.5 0.1 reshape.134
  96.6 7.7 %collective-permute-start.2 = (bf16[54,128]{1,0:T(8,128)(2,1)S(1)}, bf16[54,128]{1,0:T(8,128)(2,1)S(1)}, u32[]{:S(2)}, u32[]{:S(2)}) collective-permute-start(bf16[54,128]{1,0:T(8,128)(2,1)S(1)} %dynamic-slice_bitcast_fusion.1), channel_id=1, source_target_pairs={{0,1},{1,0},{2,3},{3,2},{4,5},{5,4},{6,7},{7,6},{8,9},{9,8},{10,11... | collective-permute-start | bytes 41480 | tf_op jit(solution)/shard_map/ppermute | solution.py:220
  104.4 0.1 eq.77
  104.4 0.1 mul.84
  104.5 0.6 collective-permute-done.2
  105.2 21.9 %all-gather.1 = bf16[16,54,128]{2,1,0:T(8,128)(2,1)S(1)} all-gather(bf16[1,54,128]{2,1,0:T(8,128)(2,1)S(1)} %fusion.31), channel_id=2, replica_groups=mesh['exp'=32,'z'=16,'core'=2] {'z'}, dimensions={0}, use_global_device_ids=true | all-gather | bytes 235008 | tf_op jit(solution)/shard_map/all_gather | solution.py:221
  127.1 9.5 %collective-permute-start.3 = (bf16[16,54,128]{2,1,0:T(8,128)(2,1)S(1)}, bf16[16,54,128]{2,1,0:T(8,128)(2,1)S(1)}, u32[]{:S(2)}, u32[]{:S(2)}) collective-permute-start(bf16[16,54,128]{2,1,0:T(8,128)(2,1)S(1)} %all-gather.1), channel_id=1, source_target_pairs={{0,1},{1,0},{2,3},{3,2},{4,5},{5,4},{6,7},{7,6},{8,9},{9,8},{10,11... | collective-permute-start | bytes 663560 | tf_op jit(solution)/shard_map/ppermute | solution.py:222
  136.6 0.1 compare_convert_fusion
  136.7 1.0 collective-permute-done.3
  137.7 0.1 maximum_select_fusion
  137.8 0.5 select_n.43
  138.3 0.1 fusion.25
  138.4 0.1 multiply_reduce_fusion
  138.5 0.0 copy-start.5
  138.5 0.1 slice_convert_fusion
  138.6 0.1 reshape.144
  138.7 0.1 convert_element_type.222
  138.8 0.7 copy.76
  139.5 5.4 %all-to-all-start.1 = ((bf16[32,4,12]{2,1,0:T(4,128)(2,1)}), bf16[32,4,12]{2,1,0:T(4,128)(2,1)S(1)}, u32[]{:S(2)}, u32[]{:S(2)}) async-start(bf16[32,4,12]{2,1,0:T(4,128)(2,1)} %copy.76), calls=%async_computation.1 | async-start | bytes 65536 | tf_op jit(solution)/shard_map/all_to_all | solution.py:233
  145.0 0.1 reshape.143
  145.1 0.0 copy-start.1
  145.1 0.1 fusion.23
  145.4 0.5 multiply_convert_fusion.17
  145.8 0.3 copy-done.1
  146.1 1.4 fusion.10
  147.5 1.9 %fusion.12 = bf16[4,8,48,64]{3,2,1,0:T(8,128)(2,1)} fusion(f32[64,4,384]{2,0,1:T(8,128)S(1)} %copy.70, f32[8,4,384]{2,0,1:T(8,128)S(1)} %compare_convert_fusion, bf16[4,48,384]{2,1,0:T(8,128)(2,1)S(1)} %copy-done.2), kind=kOutput, calls=%fused_computation.13 | convolution fusion | flops 77168640 | bytes 786432 | tf_op jit(solution)/shard_map/tres,efs->etfr/dot_general | solution.py:247
  149.3 0.9 copy.74
  150.3 0.9 copy.73
  151.2 2.5 %all-to-all-done.1 = bf16[32,4,12]{2,1,0:T(4,128)(2,1)S(1)} async-done(((bf16[32,4,12]{2,1,0:T(4,128)(2,1)}), bf16[32,4,12]{2,1,0:T(4,128)(2,1)S(1)}, u32[]{:S(2)}, u32[]{:S(2)}) %all-to-all-start.1) | async-done | bytes 3104 | tf_op jit(solution)/shard_map/all_to_all | solution.py:233
  153.7 0.8 fusion.15
  (29 shorter events, 0.3 us)
Async XLA Ops:
  0.6 23.7 %copy-start.4 = (bf16[4,8,48,64]{3,2,1,0:T(8,128)(2,1)S(1)}, bf16[4,8,48,64]{3,2,1,0:T(8,128)(2,1)}, u32[]{:S(2)}) copy-start(bf16[4,8,48,64]{3,2,1,0:T(8,128)(2,1)} %param.16) | copy-start | bytes 589828
  0.6 24.7 %copy-start.6 = (bf16[4,32,12,48]{3,1,2,0:T(8,128)(2,1)S(1)}, bf16[4,32,12,48]{3,1,2,0:T(8,128)(2,1)}, u32[]{:S(2)}) copy-start(bf16[4,32,12,48]{3,1,2,0:T(8,128)(2,1)} %param.13) | copy-start | bytes 442372
  0.7 25.0 %copy-start.7 = (bf16[4,32,12,48]{3,1,2,0:T(8,128)(2,1)S(1)}, bf16[4,32,12,48]{3,1,2,0:T(8,128)(2,1)}, u32[]{:S(2)}) copy-start(bf16[4,32,12,48]{3,1,2,0:T(8,128)(2,1)} %param.14) | copy-start | bytes 442372
  3.1 23.9 %all-to-all-start = ((bf16[32,56,128]{2,1,0:T(8,128)(2,1)}), bf16[32,56,128]{2,1,0:T(8,128)(2,1)S(1)}, u32[]{:S(2)}, u32[]{:S(2)}) async-start(bf16[32,56,128]{2,1,0:T(8,128)(2,1)} %dispatch_slab.1), calls=%async_computation | async-start | bytes 917504 | tf_op jit(solution)/shard_map/all_to_all | solution.py:167
  14.9 11.2 %copy-start.8 = (s32[128,8]{0,1:T(8,128)S(1)}, s32[128,8]{0,1:T(8,128)}, u32[]{:S(2)}) copy-start(s32[128,8]{0,1:T(8,128)} %param.10) | copy-start | bytes 12292
  14.9 21.9 %collective-permute-start = (bf16[4,16,48,128]{3,2,1,0:T(8,128)(2,1)S(1)}, bf16[4,16,48,128]{3,2,1,0:T(8,128)(2,1)}, u32[]{:S(2)}, u32[]{:S(2)}) collective-permute-start(bf16[4,16,48,128]{3,2,1,0:T(8,128)(2,1)S(1)} %dynamic-slice_bitcast_fusion), channel_id=1, source_target_pairs={{0,1},{1,0},{2,3},{3,2},{4,5},{5,4},{6,7},{7,6},{8,9},{9,8},{10,11... | collective-permute-start | bytes 2359304 | tf_op jit(solution)/shard_map/ppermute | solution.py:146
  27.2 9.6 %copy-start = (bf16[48,32,128]{2,1,0:T(8,128)(2,1)}, bf16[48,32,128]{2,1,0:T(8,128)(2,1)S(1)}, u32[]{:S(2)}) copy-start(bf16[48,32,128]{2,1,0:T(8,128)(2,1)S(1)} %copy.66) | copy-start | bytes 1179652
  27.2 9.5 %collective-permute-start.1 = (bf16[4,384,128]{2,1,0:T(8,128)(2,1)S(1)}, bf16[4,384,128]{2,1,0:T(8,128)(2,1)S(1)}, u32[]{:S(2)}, u32[]{:S(2)}) collective-permute-start(bf16[4,384,128]{2,1,0:T(8,128)(2,1)S(1)} %bitcast.104), channel_id=1, source_target_pairs={{0,1},{1,0},{2,3},{3,2},{4,5},{5,4},{6,7},{7,6},{8,9},{9,8},{10,11... | collective-permute-start | bytes 1179656 | tf_op jit(solution)/shard_map/ppermute | solution.py:170
  36.7 0.7 copy-start.3
  43.2 53.2 %copy-start.2 = (bf16[4,48,384]{2,1,0:T(8,128)(2,1)S(1)}, bf16[4,48,384]{2,1,0:T(8,128)(2,1)}, u32[]{:S(2)}) copy-start(bf16[4,48,384]{2,1,0:T(8,128)(2,1)} %multiply_convert_fusion.19.h_ref) | copy-start | bytes 442372
  92.5 3.5 %collective-permute-start.4 = (bf16[15,1536]{1,0:T(8,128)(2,1)S(1)}, bf16[15,1536]{1,0:T(8,128)(2,1)S(1)}, u32[]{:S(2)}, u32[]{:S(2)}) collective-permute-start(bf16[15,1536]{1,0:T(8,128)(2,1)S(1)} %slice.40), channel_id=1, source_target_pairs={{0,2},{2,4},{4,6},{6,8},{8,10},{10,12},{12,14},{14,16},{16,18},{18... | collective-permute-start | bytes 138248
  96.6 8.5 %collective-permute-start.2 = (bf16[54,128]{1,0:T(8,128)(2,1)S(1)}, bf16[54,128]{1,0:T(8,128)(2,1)S(1)}, u32[]{:S(2)}, u32[]{:S(2)}) collective-permute-start(bf16[54,128]{1,0:T(8,128)(2,1)S(1)} %dynamic-slice_bitcast_fusion.1), channel_id=1, source_target_pairs={{0,1},{1,0},{2,3},{3,2},{4,5},{5,4},{6,7},{7,6},{8,9},{9,8},{10,11... | collective-permute-start | bytes 41480 | tf_op jit(solution)/shard_map/ppermute | solution.py:220
  127.1 10.6 %collective-permute-start.3 = (bf16[16,54,128]{2,1,0:T(8,128)(2,1)S(1)}, bf16[16,54,128]{2,1,0:T(8,128)(2,1)S(1)}, u32[]{:S(2)}, u32[]{:S(2)}) collective-permute-start(bf16[16,54,128]{2,1,0:T(8,128)(2,1)S(1)} %all-gather.1), channel_id=1, source_target_pairs={{0,1},{1,0},{2,3},{3,2},{4,5},{5,4},{6,7},{7,6},{8,9},{9,8},{10,11... | collective-permute-start | bytes 663560 | tf_op jit(solution)/shard_map/ppermute | solution.py:222
  138.5 6.9 %copy-start.5 = (bf16[4,8,48,64]{3,2,1,0:T(8,128)(2,1)S(1)}, bf16[4,8,48,64]{3,2,1,0:T(8,128)(2,1)}, u32[]{:S(2)}) copy-start(bf16[4,8,48,64]{3,2,1,0:T(8,128)(2,1)} %param.16) | copy-start | bytes 589828
  139.5 14.2 %all-to-all-start.1 = ((bf16[32,4,12]{2,1,0:T(4,128)(2,1)}), bf16[32,4,12]{2,1,0:T(4,128)(2,1)S(1)}, u32[]{:S(2)}, u32[]{:S(2)}) async-start(bf16[32,4,12]{2,1,0:T(4,128)(2,1)} %copy.76), calls=%async_computation.1 | async-start | bytes 65536 | tf_op jit(solution)/shard_map/all_to_all | solution.py:233
  145.1 1.0 copy-start.1

commit v6 on v5

--- a/solution.py
+++ b/solution.py
@@ -119,6 +119,32 @@
     )(ids, gates, tasks, gradient)
 
 
+def gather_ring(value, axis):
+    width = lax.axis_size(axis)
+    step = 4
+
+    def ahead(array, shift):
+        return lax.ppermute(array, axis, [((i + shift) % width, i) for i in range(width)])
+
+    four = jnp.stack([value, *(ahead(value, step * a) for a in range(1, width // step))])
+    parts = [four, ahead(four, 1), ahead(four, 2), ahead(four, -1)]
+
+    def kernel(at_ref, *refs):
+        out_ref = refs[-1]
+        for shift, ref in zip((0, 1, 2, -1), refs[:-1]):
+            for a in range(width // step):
+                out_ref[(at_ref[0] + (step * a + shift) % width) % width] = ref[a]
+
+    vmem = pl.BlockSpec(memory_space=pltpu.VMEM)
+    return pl.pallas_call(
+        kernel,
+        out_shape=jax.ShapeDtypeStruct((width, *value.shape), value.dtype),
+        in_specs=[pl.BlockSpec(memory_space=pltpu.SMEM)] + [vmem] * len(parts),
+        out_specs=vmem,
+        name="in_order",
+    )(lax.axis_index(axis).astype(jnp.int32).reshape(1), *parts)
+
+
 def on_device(
     output_gradient,
     routed_expert_index,
@@ -214,15 +240,9 @@
     pair_part = jnp.sum(hidden.astype(F32) * back, axis=1).reshape(1, total_slots)
     more = 2 * rank // z_width
     small = jnp.concatenate([summed[piece : piece + more], pair_part.astype(BF)])
-    small = small.reshape(2, -1, 128)
-    theirs = lax.dynamic_index_in_dim(small, 1 - core, axis=0, keepdims=False)
-    mine = lax.dynamic_index_in_dim(small, core, axis=0, keepdims=False).astype(F32)
-    mine = (mine + lax.ppermute(theirs, "core", swap).astype(F32)).astype(BF)
-    half = lax.all_gather(mine, "z", axis=0, tiled=False)
-    other = lax.ppermute(half, "core", swap)
-    everything = jnp.where(
-        core == 0, jnp.stack([half, other], axis=1), jnp.stack([other, half], axis=1)
-    )
+    small = small.reshape(-1, 128)
+    small = small.astype(F32) + lax.ppermute(small, "core", swap).astype(F32)
+    everything = gather_ring(small.astype(BF), "z")
     everything = everything.reshape(z_width, more + 1, total_slots)
     split = (rank, exp_local, per_expert)
     latent = everything[: z_width // 2, :more].reshape(split).astype(F32)

time: 155 us -> 165 us (1.065); the launches traced: 155 us -> 163 us
  blocking collectives: 71.2 us -> 49.4 us
  starting transfers between devices: 52 us -> 67.6 us
  waiting for transfers between devices: 4.21 us -> 15.2 us
  Pallas kernels: 8.23 us -> 10.1 us
  local copies, waits for them, and re-layouts: 10 us -> 11.7 us
    all_gather x1 -> x0, blocking collectives: 21.9 us -> none  [on_device(): half = lax.all_gather(mine, 'z', axis=0, tiled=False)]
    ppermute x2 -> x7, starting transfers between devices: 17.2 us -> 32.7 us  [the longest x6 25.1 us: ahead(): lax.ppermute(array, axis, [((i + shift) % width, i) for i in range(width)])]
    ppermute x2 -> x7, waiting for transfers between devices: 1.65 us -> 12.6 us  [the longest x6 11.9 us: ahead(): lax.ppermute(array, axis, [((i + shift) % width, i) for i in range(width)])]
    pallas_call x0 -> x1, Pallas kernels: none -> 1.88 us  [gather_ring(): pl.pallas_call(kernel, out_shape=jax.ShapeDtypeStruct((width, *value.shap...]
    unnamed x24 -> x34, local copies, waits for them, and re-layouts: 3.72 us -> 4.37 us
  transfers between devices with their start and end apart: 7 -> 12, of which waited for: 3 -> 6; matrix products, arithmetic and copies ran while one was open for 8% -> 8% of each run, Pallas kernels for 0% -> 0%
where the time goes in v6:
time: 165 us; the launch traced here: 163 us
  starting transfers between devices  67.6 us (41%)
  blocking collectives  49.4 us (30%)
  waiting for transfers between devices  15.2 us (9%)
  local copies, waits for them, and re-layouts  11.7 us (7%)
  Pallas kernels  10.1 us (6%)
  matrix products  4.77 us (3%)
  other arithmetic  2.25 us (1%)
  between operations  1.83 us (1%)
    unnamed x1, blocking collectives  49.4 us
    ppermute x6, starting transfers between devices, ahead(): lax.ppermute(array, axis, [((i + shift) % width, i) for i in range(width)])  25.1 us
    ppermute x6, waiting for transfers between devices, ahead(): lax.ppermute(array, axis, [((i + shift) % width, i) for i in range(width)])  11.9 us
    all_to_all x1, starting transfers between devices, on_device(): lax.all_to_all(send, 'exp', split_axis=0, concat_axis=0, tiled=True)  10.5 us
    ppermute x1, starting transfers between devices, on_device(): lax.ppermute(lax.dynamic_index_in_dim(weight, 1 - core, axis=2, keepdims=...  9.45 us
    ppermute x1, starting transfers between devices, on_device(): rows_peer = lax.ppermute(rows, 'core', swap)  8.16 us
    ppermute x1, starting transfers between devices, on_device(): small = small.astype(F32) + lax.ppermute(small, 'core', swap).astype(F32)  7.6 us
    pallas_call x1, Pallas kernels, partial_sums(): pl.pallas_call(kernel, out_shape=jax.ShapeDtypeStruct((z_width * chunk, e...  5.75 us
  transfers between devices with their start and end apart: 12, of which 6 were waited for; matrix products, arithmetic and copies ran while one was open for 8% of the time, Pallas kernels for 0%

profile of v6, /device:TPU:1, one launch (start us, length us, event | category | flops | bytes accessed | tf_op | source)
XLA Modules:
  0.0 162.8 jit_solution(9855028548626617584)
XLA Ops:
  0.6 0.0 copy-start.5
  0.7 2.5 %dispatch_slab.1 = bf16[32,56,128]{2,1,0:T(8,128)(2,1)} custom-call(s32[8,128]{1,0:T(8,128)} %bitcast.110, bf16[8,128]{1,0:T(8,128)(2,1)} %bitcast.121, s32[1,128]{1,0:T(1,128)} %bitcast.122, bf16[128,128]{1,0:T(8,128)(2,1)} %grad_ref.1), custom_call_target="tpu_custom_call" | custom-call | tf_op jit(solution)/shard_map/dispatch_slab/pallas_call | solution.py:115
  3.1 10.5 %all-to-all-start = ((bf16[32,56,128]{2,1,0:T(8,128)(2,1)}), bf16[32,56,128]{2,1,0:T(8,128)(2,1)S(1)}, u32[]{:S(2)}, u32[]{:S(2)}) async-start(bf16[32,56,128]{2,1,0:T(8,128)(2,1)} %dispatch_slab.1), calls=%async_computation | async-start | bytes 917504 | tf_op jit(solution)/shard_map/all_to_all | solution.py:193
  13.6 1.2 dynamic-slice_bitcast_fusion
  14.8 0.0 copy-start.12
  14.9 9.4 %collective-permute-start = (bf16[4,16,48,128]{3,2,1,0:T(8,128)(2,1)S(1)}, bf16[4,16,48,128]{3,2,1,0:T(8,128)(2,1)}, u32[]{:S(2)}, u32[]{:S(2)}) collective-permute-start(bf16[4,16,48,128]{3,2,1,0:T(8,128)(2,1)S(1)} %dynamic-slice_bitcast_fusion), channel_id=1, source_target_pairs={{0,1},{1,0},{2,3},{3,2},{4,5},{5,4},{6,7},{7,6},{8,9},{9,8},{10,11... | collective-permute-start | bytes 2359304 | tf_op jit(solution)/shard_map/ppermute | solution.py:172
  24.3 1.0 copy.65
  25.3 0.1 convert_element_type.225
  25.4 0.2 copy.63
  25.7 0.1 convert_element_type.226
  25.8 0.2 copy.64
  26.0 0.1 fusion.16
  26.1 0.8 multiply_convert_fusion.19.h_ref
  26.9 0.1 copy.66
  27.0 8.2 %collective-permute-start.1 = (bf16[4,384,128]{2,1,0:T(8,128)(2,1)S(1)}, bf16[4,384,128]{2,1,0:T(8,128)(2,1)S(1)}, u32[]{:S(2)}, u32[]{:S(2)}) collective-permute-start(bf16[4,384,128]{2,1,0:T(8,128)(2,1)S(1)} %bitcast.100), channel_id=1, source_target_pairs={{0,1},{1,0},{2,3},{3,2},{4,5},{5,4},{6,7},{7,6},{8,9},{9,8},{10,11... | collective-permute-start | bytes 1179656 | tf_op jit(solution)/shard_map/ppermute | solution.py:196
  35.2 0.1 fusion.28
  35.4 0.6 select_reduce_fusion.1
  36.0 0.7 broadcast_in_dim_reshape.3.t_ref
  36.7 0.7 copy-done.4
  37.5 5.8 %partial_sums.1 = bf16[1008,1536]{1,0:T(8,128)(2,1)} custom-call(s32[1]{0:T(128)} %bitcast.6.core_ref, f32[4,1,384]{2,1,0:T(1,128)} %broadcast_in_dim_reshape.3.t_ref, bf16[4,48,384]{2,1,0:T(8,128)(2,1)} %multiply_convert_fusion.19.h_ref, bf16[4,8,64,48]{3,2,1,0:T(8,128)(2,1)} %bitcast.99, bf16[4,8,64,128]{3,2,1,0:T(8,128)(2,1)} %b_ref.1, ...), custom_call_target="tpu_custom_call" | custom-call | tf_op jit(solution)/shard_map/partial_sums/pallas_call | solution.py:53
  43.2 49.4 %fusion = bf16[64,1536]{1,0:T(8,128)(2,1)S(1)} fusion(bf16[1008,1536]{1,0:T(8,128)(2,1)} %partial_sums.1), kind=kCustom, calls=%all-reduce-scatter | all-reduce-scatter fusion | flops 1572865 | bytes 3297280
  92.6 1.5 collective-permute-start.9
  94.1 0.1 fusion.26
  94.2 1.3 dynamic-slice.4
  96.2 0.3 concatenate.4
  96.5 0.1 constant_dynamic-slice_fusion
  96.6 0.1 fusion.19
  96.7 0.1 reshape.134
  96.7 7.6 %collective-permute-start.2 = (bf16[108,128]{1,0:T(8,128)(2,1)S(1)}, bf16[108,128]{1,0:T(8,128)(2,1)S(1)}, u32[]{:S(2)}, u32[]{:S(2)}) collective-permute-start(bf16[108,128]{1,0:T(8,128)(2,1)S(1)} %reshape.134), channel_id=1, source_target_pairs={{0,1},{1,0},{2,3},{3,2},{4,5},{5,4},{6,7},{7,6},{8,9},{9,8},{10,11... | collective-permute-start | bytes 82952 | tf_op jit(solution)/shard_map/ppermute | solution.py:244
  104.4 0.1 select_reduce_fusion.2
  104.4 0.8 collective-permute-done.2
  105.2 5.3 %collective-permute-start.5 = (bf16[108,128]{1,0:T(8,128)(2,1)S(1)}, bf16[108,128]{1,0:T(8,128)(2,1)S(1)}, u32[]{:S(2)}, u32[]{:S(2)}) collective-permute-start(bf16[108,128]{1,0:T(8,128)(2,1)S(1)} %add_convert_fusion), channel_id=1, source_target_pairs={{24,0},{26,2},{28,4},{30,6},{0,8},{2,10},{4,12},{6,14},{8,16},{10,... | collective-permute-start | bytes 82952 | tf_op jit(solution)/shard_map/ppermute | solution.py:127
  110.5 9.0 %collective-permute-start.4 = (bf16[108,128]{1,0:T(8,128)(2,1)S(1)}, bf16[108,128]{1,0:T(8,128)(2,1)S(1)}, u32[]{:S(2)}, u32[]{:S(2)}) collective-permute-start(bf16[108,128]{1,0:T(8,128)(2,1)S(1)} %add_convert_fusion), channel_id=1, source_target_pairs={{16,0},{18,2},{20,4},{22,6},{24,8},{26,10},{28,12},{30,14},{0,16},... | collective-permute-start | bytes 82952 | tf_op jit(solution)/shard_map/ppermute | solution.py:127
  119.5 2.4 %collective-permute-start.3 = (bf16[108,128]{1,0:T(8,128)(2,1)S(1)}, bf16[108,128]{1,0:T(8,128)(2,1)S(1)}, u32[]{:S(2)}, u32[]{:S(2)}) collective-permute-start(bf16[108,128]{1,0:T(8,128)(2,1)S(1)} %add_convert_fusion), channel_id=1, source_target_pairs={{8,0},{10,2},{12,4},{14,6},{16,8},{18,10},{20,12},{22,14},{24,16},... | collective-permute-start | bytes 82952 | tf_op jit(solution)/shard_map/ppermute | solution.py:127
  121.9 0.1 eq.74
  122.0 1.8 %collective-permute-done.4 = bf16[108,128]{1,0:T(8,128)(2,1)S(1)} collective-permute-done((bf16[108,128]{1,0:T(8,128)(2,1)S(1)}, bf16[108,128]{1,0:T(8,128)(2,1)S(1)}, u32[]{:S(2)}, u32[]{:S(2)}) %collective-permute-start.4) | collective-permute-done | bytes 27680 | tf_op jit(solution)/shard_map/ppermute | solution.py:127
  123.8 5.1 %collective-permute-done.3 = bf16[108,128]{1,0:T(8,128)(2,1)S(1)} collective-permute-done((bf16[108,128]{1,0:T(8,128)(2,1)S(1)}, bf16[108,128]{1,0:T(8,128)(2,1)S(1)}, u32[]{:S(2)}, u32[]{:S(2)}) %collective-permute-start.3) | collective-permute-done | bytes 27680 | tf_op jit(solution)/shard_map/ppermute | solution.py:127
  129.0 1.9 %collective-permute-start.8 = (bf16[4,108,128]{2,1,0:T(8,128)(2,1)S(1)}, bf16[4,108,128]{2,1,0:T(8,128)(2,1)S(1)}, u32[]{:S(2)}, u32[]{:S(2)}) collective-permute-start(bf16[4,108,128]{2,1,0:T(8,128)(2,1)S(1)} %pad_maximum_fusion.refs_0_), channel_id=1, source_target_pairs={{30,0},{0,2},{2,4},{4,6},{6,8},{8,10},{10,12},{12,14},{14,16},{16,... | collective-permute-start | bytes 331784 | tf_op jit(solution)/shard_map/ppermute | solution.py:127
  130.9 2.0 %collective-permute-start.7 = (bf16[4,108,128]{2,1,0:T(8,128)(2,1)S(1)}, bf16[4,108,128]{2,1,0:T(8,128)(2,1)S(1)}, u32[]{:S(2)}, u32[]{:S(2)}) collective-permute-start(bf16[4,108,128]{2,1,0:T(8,128)(2,1)S(1)} %pad_maximum_fusion.refs_0_), channel_id=1, source_target_pairs={{4,0},{6,2},{8,4},{10,6},{12,8},{14,10},{16,12},{18,14},{20,16},{2... | collective-permute-start | bytes 331784 | tf_op jit(solution)/shard_map/ppermute | solution.py:127
  132.9 4.5 %collective-permute-start.6 = (bf16[4,108,128]{2,1,0:T(8,128)(2,1)S(1)}, bf16[4,108,128]{2,1,0:T(8,128)(2,1)S(1)}, u32[]{:S(2)}, u32[]{:S(2)}) collective-permute-start(bf16[4,108,128]{2,1,0:T(8,128)(2,1)S(1)} %pad_maximum_fusion.refs_0_), channel_id=1, source_target_pairs={{2,0},{4,2},{6,4},{8,6},{10,8},{12,10},{14,12},{16,14},{18,16},{20... | collective-permute-start | bytes 331784 | tf_op jit(solution)/shard_map/ppermute | solution.py:127
  137.4 0.1 compare_convert_fusion
  137.5 0.1 mul.84
  137.6 0.1 collective-permute-done.7.refs_2_
  137.6 4.9 %collective-permute-done.6.refs_1_ = bf16[4,108,128]{2,1,0:T(8,128)(2,1)S(1)} collective-permute-done((bf16[4,108,128]{2,1,0:T(8,128)(2,1)S(1)}, bf16[4,108,128]{2,1,0:T(8,128)(2,1)S(1)}, u32[]{:S(2)}, u32[]{:S(2)}) %collective-permute-start.6) | collective-permute-done | bytes 110624 | tf_op jit(solution)/shard_map/ppermute | solution.py:127
  142.5 0.6 copy-done.11
  143.1 1.9 %in_order.1 = bf16[16,108,128]{2,1,0:T(8,128)(2,1)} custom-call(s32[1]{0:T(128)} %bitcast.19.at_ref, bf16[4,108,128]{2,1,0:T(8,128)(2,1)} %copy-done.3, bf16[4,108,128]{2,1,0:T(8,128)(2,1)} %copy-done.11, bf16[4,108,128]{2,1,0:T(8,128)(2,1)} %copy-done.10, bf16[4,108,128]{2,1,0:T(8,128)(2,1)} %copy-done.9), custom_call_target="tpu_custom_call" | custom-call | tf_op jit(solution)/shard_map/in_order/pallas_call | solution.py:139
  145.0 1.6 reshape.135
  146.6 0.1 fusion.25
  146.7 0.1 multiply_reduce_fusion
  146.8 0.1 slice_convert_fusion
  146.9 0.1 reshape.144
  147.0 0.1 convert_element_type.218
  147.1 0.7 copy.75
  147.9 5.4 %all-to-all-start.1 = ((bf16[32,4,12]{2,1,0:T(4,128)(2,1)}), bf16[32,4,12]{2,1,0:T(4,128)(2,1)S(1)}, u32[]{:S(2)}, u32[]{:S(2)}) async-start(bf16[32,4,12]{2,1,0:T(4,128)(2,1)} %copy.75), calls=%async_computation.1 | async-start | bytes 65536 | tf_op jit(solution)/shard_map/all_to_all | solution.py:253
  153.2 0.1 reshape.143
  153.4 0.1 fusion.23
  153.6 0.5 multiply_convert_fusion.17
  154.1 0.3 copy-done.1
  154.4 1.4 fusion.10
  155.7 1.9 %fusion.12 = bf16[4,8,48,64]{3,2,1,0:T(8,128)(2,1)} fusion(f32[64,4,384]{2,0,1:T(8,128)S(1)} %copy.69, f32[8,4,384]{2,0,1:T(8,128)S(1)} %compare_convert_fusion, bf16[4,48,384]{2,1,0:T(8,128)(2,1)S(1)} %copy-done.2), kind=kOutput, calls=%fused_computation.13 | convolution fusion | flops 77168640 | bytes 786432 | tf_op jit(solution)/shard_map/tres,efs->etfr/dot_general | solution.py:267
  157.6 0.9 copy.73
  158.5 0.9 copy.72
  159.4 2.5 %all-to-all-done.1 = bf16[32,4,12]{2,1,0:T(4,128)(2,1)S(1)} async-done(((bf16[32,4,12]{2,1,0:T(4,128)(2,1)}), bf16[32,4,12]{2,1,0:T(4,128)(2,1)S(1)}, u32[]{:S(2)}, u32[]{:S(2)}) %all-to-all-start.1) | async-done | bytes 3104 | tf_op jit(solution)/shard_map/all_to_all | solution.py:253
  162.0 0.8 fusion.15
  (47 shorter events, 0.3 us)
Async XLA Ops:
  0.6 23.7 %copy-start.5 = (bf16[4,8,48,64]{3,2,1,0:T(8,128)(2,1)S(1)}, bf16[4,8,48,64]{3,2,1,0:T(8,128)(2,1)}, u32[]{:S(2)}) copy-start(bf16[4,8,48,64]{3,2,1,0:T(8,128)(2,1)} %param.16) | copy-start | bytes 589828
  0.6 24.7 %copy-start.7 = (bf16[4,32,12,48]{3,1,2,0:T(8,128)(2,1)S(1)}, bf16[4,32,12,48]{3,1,2,0:T(8,128)(2,1)}, u32[]{:S(2)}) copy-start(bf16[4,32,12,48]{3,1,2,0:T(8,128)(2,1)} %param.13) | copy-start | bytes 442372
  0.7 25.0 %copy-start.8 = (bf16[4,32,12,48]{3,1,2,0:T(8,128)(2,1)S(1)}, bf16[4,32,12,48]{3,1,2,0:T(8,128)(2,1)}, u32[]{:S(2)}) copy-start(bf16[4,32,12,48]{3,1,2,0:T(8,128)(2,1)} %param.14) | copy-start | bytes 442372
  3.1 23.8 %all-to-all-start = ((bf16[32,56,128]{2,1,0:T(8,128)(2,1)}), bf16[32,56,128]{2,1,0:T(8,128)(2,1)S(1)}, u32[]{:S(2)}, u32[]{:S(2)}) async-start(bf16[32,56,128]{2,1,0:T(8,128)(2,1)} %dispatch_slab.1), calls=%async_computation | async-start | bytes 917504 | tf_op jit(solution)/shard_map/all_to_all | solution.py:193
  14.8 11.2 %copy-start.12 = (s32[128,8]{0,1:T(8,128)S(1)}, s32[128,8]{0,1:T(8,128)}, u32[]{:S(2)}) copy-start(s32[128,8]{0,1:T(8,128)} %param.10) | copy-start | bytes 12292
  14.9 21.9 %collective-permute-start = (bf16[4,16,48,128]{3,2,1,0:T(8,128)(2,1)S(1)}, bf16[4,16,48,128]{3,2,1,0:T(8,128)(2,1)}, u32[]{:S(2)}, u32[]{:S(2)}) collective-permute-start(bf16[4,16,48,128]{3,2,1,0:T(8,128)(2,1)S(1)} %dynamic-slice_bitcast_fusion), channel_id=1, source_target_pairs={{0,1},{1,0},{2,3},{3,2},{4,5},{5,4},{6,7},{7,6},{8,9},{9,8},{10,11... | collective-permute-start | bytes 2359304 | tf_op jit(solution)/shard_map/ppermute | solution.py:172
  27.0 9.7 %copy-start = (bf16[48,32,128]{2,1,0:T(8,128)(2,1)}, bf16[48,32,128]{2,1,0:T(8,128)(2,1)S(1)}, u32[]{:S(2)}) copy-start(bf16[48,32,128]{2,1,0:T(8,128)(2,1)S(1)} %copy.66) | copy-start | bytes 1179652
  27.0 9.7 %collective-permute-start.1 = (bf16[4,384,128]{2,1,0:T(8,128)(2,1)S(1)}, bf16[4,384,128]{2,1,0:T(8,128)(2,1)S(1)}, u32[]{:S(2)}, u32[]{:S(2)}) collective-permute-start(bf16[4,384,128]{2,1,0:T(8,128)(2,1)S(1)} %bitcast.100), channel_id=1, source_target_pairs={{0,1},{1,0},{2,3},{3,2},{4,5},{5,4},{6,7},{7,6},{8,9},{9,8},{10,11... | collective-permute-start | bytes 1179656 | tf_op jit(solution)/shard_map/ppermute | solution.py:196
  36.7 0.7 copy-start.4
  43.2 53.3 %copy-start.2 = (bf16[4,48,384]{2,1,0:T(8,128)(2,1)S(1)}, bf16[4,48,384]{2,1,0:T(8,128)(2,1)}, u32[]{:S(2)}) copy-start(bf16[4,48,384]{2,1,0:T(8,128)(2,1)} %multiply_convert_fusion.19.h_ref) | copy-start | bytes 442372
  43.2 61.1 %copy-start.13 = (s32[128,8]{0,1:T(8,128)S(1)}, s32[128,8]{0,1:T(8,128)}, u32[]{:S(2)}) copy-start(s32[128,8]{0,1:T(8,128)} %param.10) | copy-start | bytes 12292
  92.6 3.5 %collective-permute-start.9 = (bf16[15,1536]{1,0:T(8,128)(2,1)S(1)}, bf16[15,1536]{1,0:T(8,128)(2,1)S(1)}, u32[]{:S(2)}, u32[]{:S(2)}) collective-permute-start(bf16[15,1536]{1,0:T(8,128)(2,1)S(1)} %slice.40), channel_id=1, source_target_pairs={{0,2},{2,4},{4,6},{6,8},{8,10},{10,12},{12,14},{14,16},{16,18},{18... | collective-permute-start | bytes 138248
  96.7 8.4 %collective-permute-start.2 = (bf16[108,128]{1,0:T(8,128)(2,1)S(1)}, bf16[108,128]{1,0:T(8,128)(2,1)S(1)}, u32[]{:S(2)}, u32[]{:S(2)}) collective-permute-start(bf16[108,128]{1,0:T(8,128)(2,1)S(1)} %reshape.134), channel_id=1, source_target_pairs={{0,1},{1,0},{2,3},{3,2},{4,5},{5,4},{6,7},{7,6},{8,9},{9,8},{10,11... | collective-permute-start | bytes 82952 | tf_op jit(solution)/shard_map/ppermute | solution.py:244
  105.2 16.8 %collective-permute-start.5 = (bf16[108,128]{1,0:T(8,128)(2,1)S(1)}, bf16[108,128]{1,0:T(8,128)(2,1)S(1)}, u32[]{:S(2)}, u32[]{:S(2)}) collective-permute-start(bf16[108,128]{1,0:T(8,128)(2,1)S(1)} %add_convert_fusion), channel_id=1, source_target_pairs={{24,0},{26,2},{28,4},{30,6},{0,8},{2,10},{4,12},{6,14},{8,16},{10,... | collective-permute-start | bytes 82952 | tf_op jit(solution)/shard_map/ppermute | solution.py:127
  110.5 13.3 %collective-permute-start.4 = (bf16[108,128]{1,0:T(8,128)(2,1)S(1)}, bf16[108,128]{1,0:T(8,128)(2,1)S(1)}, u32[]{:S(2)}, u32[]{:S(2)}) collective-permute-start(bf16[108,128]{1,0:T(8,128)(2,1)S(1)} %add_convert_fusion), channel_id=1, source_target_pairs={{16,0},{18,2},{20,4},{22,6},{24,8},{26,10},{28,12},{30,14},{0,16},... | collective-permute-start | bytes 82952 | tf_op jit(solution)/shard_map/ppermute | solution.py:127
  119.5 9.4 %collective-permute-start.3 = (bf16[108,128]{1,0:T(8,128)(2,1)S(1)}, bf16[108,128]{1,0:T(8,128)(2,1)S(1)}, u32[]{:S(2)}, u32[]{:S(2)}) collective-permute-start(bf16[108,128]{1,0:T(8,128)(2,1)S(1)} %add_convert_fusion), channel_id=1, source_target_pairs={{8,0},{10,2},{12,4},{14,6},{16,8},{18,10},{20,12},{22,14},{24,16},... | collective-permute-start | bytes 82952 | tf_op jit(solution)/shard_map/ppermute | solution.py:127
  129.0 13.5 %copy-start.3 = (bf16[4,108,128]{2,1,0:T(8,128)(2,1)}, bf16[4,108,128]{2,1,0:T(8,128)(2,1)S(1)}, u32[]{:S(2)}) copy-start(bf16[4,108,128]{2,1,0:T(8,128)(2,1)S(1)} %pad_maximum_fusion.refs_0_) | copy-start | bytes 331780
  129.0 8.6 %collective-permute-start.8 = (bf16[4,108,128]{2,1,0:T(8,128)(2,1)S(1)}, bf16[4,108,128]{2,1,0:T(8,128)(2,1)S(1)}, u32[]{:S(2)}, u32[]{:S(2)}) collective-permute-start(bf16[4,108,128]{2,1,0:T(8,128)(2,1)S(1)} %pad_maximum_fusion.refs_0_), channel_id=1, source_target_pairs={{30,0},{0,2},{2,4},{4,6},{6,8},{8,10},{10,12},{12,14},{14,16},{16,... | collective-permute-start | bytes 331784 | tf_op jit(solution)/shard_map/ppermute | solution.py:127
  130.9 6.7 %collective-permute-start.7 = (bf16[4,108,128]{2,1,0:T(8,128)(2,1)S(1)}, bf16[4,108,128]{2,1,0:T(8,128)(2,1)S(1)}, u32[]{:S(2)}, u32[]{:S(2)}) collective-permute-start(bf16[4,108,128]{2,1,0:T(8,128)(2,1)S(1)} %pad_maximum_fusion.refs_0_), channel_id=1, source_target_pairs={{4,0},{6,2},{8,4},{10,6},{12,8},{14,10},{16,12},{18,14},{20,16},{2... | collective-permute-start | bytes 331784 | tf_op jit(solution)/shard_map/ppermute | solution.py:127
  132.9 9.6 %collective-permute-start.6 = (bf16[4,108,128]{2,1,0:T(8,128)(2,1)S(1)}, bf16[4,108,128]{2,1,0:T(8,128)(2,1)S(1)}, u32[]{:S(2)}, u32[]{:S(2)}) collective-permute-start(bf16[4,108,128]{2,1,0:T(8,128)(2,1)S(1)} %pad_maximum_fusion.refs_0_), channel_id=1, source_target_pairs={{2,0},{4,2},{6,4},{8,6},{10,8},{12,10},{14,12},{16,14},{18,16},{20... | collective-permute-start | bytes 331784 | tf_op jit(solution)/shard_map/ppermute | solution.py:127
  137.6 4.9 %copy-start.9 = (bf16[4,108,128]{2,1,0:T(8,128)(2,1)}, bf16[4,108,128]{2,1,0:T(8,128)(2,1)S(1)}, u32[]{:S(2)}) copy-start(bf16[4,108,128]{2,1,0:T(8,128)(2,1)S(1)} %collective-permute-done.8.refs_3_) | copy-start | bytes 331780
  137.6 4.9 %copy-start.10 = (bf16[4,108,128]{2,1,0:T(8,128)(2,1)}, bf16[4,108,128]{2,1,0:T(8,128)(2,1)S(1)}, u32[]{:S(2)}) copy-start(bf16[4,108,128]{2,1,0:T(8,128)(2,1)S(1)} %collective-permute-done.7.refs_2_) | copy-start | bytes 331780
  142.5 0.6 copy-start.11
  146.8 6.8 %copy-start.6 = (bf16[4,8,48,64]{3,2,1,0:T(8,128)(2,1)S(1)}, bf16[4,8,48,64]{3,2,1,0:T(8,128)(2,1)}, u32[]{:S(2)}) copy-start(bf16[4,8,48,64]{3,2,1,0:T(8,128)(2,1)} %param.16) | copy-start | bytes 589828
  147.9 14.1 %all-to-all-start.1 = ((bf16[32,4,12]{2,1,0:T(4,128)(2,1)}), bf16[32,4,12]{2,1,0:T(4,128)(2,1)S(1)}, u32[]{:S(2)}, u32[]{:S(2)}) async-start(bf16[32,4,12]{2,1,0:T(4,128)(2,1)} %copy.75), calls=%async_computation.1 | async-start | bytes 65536 | tf_op jit(solution)/shard_map/all_to_all | solution.py:253
  153.4 1.0 copy-start.1

commit v7 on v5

--- a/solution.py
+++ b/solution.py
@@ -8,39 +8,50 @@
 
 BF = jnp.bfloat16
 F32 = jnp.float32
-PAD = 7
-
-
-def partial_sums(core, task_row, hidden, first, second, weight, weight_peer, rows, rows_peer):
+PAD = 3
+
+
+def partial_sums(core, task_row, own_pack, peer_pack, second, weight, peer_weight, rows, rows_peer):
     exp_local, z_width, _, piece, width = weight.shape
     slots = rows.shape[1]
-    task_count, rank = first.shape[1], first.shape[2]
-    more = 2 * rank // z_width
+    task_count, half = second.shape[1], second.shape[3]
+    packed = task_count * half
+    more = 2 * half // z_width
     chunk = piece + more + PAD
-
-    def kernel(core_ref, t_ref, h_ref, a_ref, b_ref, w_ref, wp_ref, x_ref, xp_ref, out_ref, f32_ref):
+    first, hidden = own_pack
+
+    def kernel(core_ref, t_ref, a_ref, h_ref, p_ref, b_ref, w_ref, wp_ref, x_ref, xp_ref, out_ref, f32_ref):
         nums = (((1,), (1,)), ((), ()))
-        x = x_ref[0]
         own = w_ref[0, :, 0].reshape(z_width * piece, width)
-        peer = wp_ref[0].reshape(z_width * piece, width)
+        peer = wp_ref[0]
+        both = jnp.concatenate([x_ref[0], xp_ref[0]], axis=1)
         total = lax.dot_general(
-            jnp.concatenate([own, peer], axis=1),
-            jnp.concatenate([x, xp_ref[0]], axis=1),
+            jnp.concatenate([own, peer[: z_width * piece]], axis=1),
+            both,
             nums,
             preferred_element_type=F32,
         )
         ql_all = lax.dot_general(
-            b_ref[0].reshape(task_count * rank, width), x, nums, preferred_element_type=F32
+            jnp.concatenate(
+                [b_ref[0, :, 0].reshape(packed, width), peer[z_width * piece :]], axis=1
+            ),
+            both,
+            nums,
+            preferred_element_type=F32,
         )
-        lat_all = jnp.dot(
-            a_ref[0].reshape(task_count * rank, piece), h_ref[0], preferred_element_type=F32
+        theirs = p_ref[0]
+        lat_all = lax.dot_general(
+            jnp.concatenate([a_ref[0, 0], theirs[:, :packed]]),
+            jnp.concatenate([h_ref[0], theirs[:, packed:]]),
+            (((0,), (0,)), ((), ())),
+            preferred_element_type=F32,
         )
-        lat = jnp.zeros((rank, slots), F32)
-        ql = jnp.zeros((rank, slots), F32)
+        lat = jnp.zeros((half, slots), F32)
+        ql = jnp.zeros((half, slots), F32)
         for t in range(task_count):
             keep = t_ref[0] == float(t)
-            lat += jnp.where(keep, lat_all[t * rank : (t + 1) * rank], 0.0)
-            ql += jnp.where(keep, ql_all[t * rank : (t + 1) * rank], 0.0)
+            lat += jnp.where(keep, lat_all[t * half : (t + 1) * half], 0.0)
+            ql += jnp.where(keep, ql_all[t * half : (t + 1) * half], 0.0)
         small = jnp.concatenate([lat, ql])
         empty = jnp.zeros((PAD, slots), F32)
         for z in range(z_width):
@@ -58,11 +69,12 @@
             grid=(exp_local,),
             in_specs=[
                 pl.BlockSpec((1, 1, slots), lambda e, c: (e, 0, 0)),
+                pl.BlockSpec((1, 1, piece, packed), lambda e, c: (e, c[0], 0, 0)),
                 pl.BlockSpec((1, piece, slots), lambda e, c: (e, 0, 0)),
-                pl.BlockSpec((1, task_count, rank, piece), lambda e, c: (e, 0, 0, 0)),
-                pl.BlockSpec((1, task_count, rank, width), lambda e, c: (e, 0, 0, 0)),
+                pl.BlockSpec((1, piece, packed + slots), lambda e, c: (e, 0, 0)),
+                pl.BlockSpec((1, task_count, 1, half, width), lambda e, c: (e, 0, c[0], 0, 0)),
                 pl.BlockSpec((1, z_width, 1, piece, width), lambda e, c: (e, 0, c[0], 0, 0)),
-                pl.BlockSpec((1, z_width, piece, width), lambda e, c: (e, 0, 0, 0)),
+                pl.BlockSpec((1, z_width * piece + packed, width), lambda e, c: (e, 0, 0)),
                 pl.BlockSpec((1, slots, width), lambda e, c: (e, 0, 0)),
                 pl.BlockSpec((1, slots, width), lambda e, c: (e, 0, 0)),
             ],
@@ -70,7 +82,18 @@
             scratch_shapes=[pltpu.VMEM((z_width * chunk, slots), F32)],
         ),
         name="partial_sums",
-    )(core.reshape(1), task_row, hidden, first, second, weight, weight_peer, rows, rows_peer)
+    )(
+        core.reshape(1),
+        task_row,
+        first,
+        hidden,
+        peer_pack,
+        second,
+        weight,
+        peer_weight,
+        rows,
+        rows_peer,
+    )
 
 
 def dispatch_slab(ids, gates, tasks, gradient, expert_count, exp_width, most):
@@ -143,9 +166,15 @@
     swap = [(0, 1), (1, 0)]
 
     weight = down_weight.reshape(exp_local, z_width, 2, piece, width)
-    weight_peer = lax.ppermute(
-        lax.dynamic_index_in_dim(weight, 1 - core, axis=2, keepdims=False), "core", swap
-    )
+    half = rank // 2
+    second = adapter_second_factor.reshape(exp_local, task_count, 2, half, width)
+    first = adapter_first_factor.reshape(exp_local, task_count, piece, 2, half)
+    first = first.transpose(0, 3, 2, 1, 4).reshape(exp_local, 2, piece, task_count * half)
+    for_peer = [
+        lax.dynamic_index_in_dim(a, 1 - core, axis=2, keepdims=False).reshape(exp_local, -1, width)
+        for a in (weight, second)
+    ]
+    peer_weight = lax.ppermute(jnp.concatenate(for_peer, axis=1), "core", swap)
 
     ids = routed_expert_index.T
     experts = jnp.arange(expert_count, dtype=jnp.int32)
@@ -196,14 +225,17 @@
     act = gate_f * sig
     hidden = (act * up_f).astype(BF)
 
+    first_send = lax.dynamic_index_in_dim(first, 1 - core, axis=1, keepdims=False)
+    peer_pack = lax.ppermute(jnp.concatenate([first_send, hidden], axis=2), "core", swap)
+
     partial = partial_sums(
         core.astype(jnp.int32),
         task_slot[:, None],
-        hidden,
-        adapter_first_factor.swapaxes(2, 3),
-        adapter_second_factor,
+        (first, hidden),
+        peer_pack,
+        second,
         weight,
-        weight_peer,
+        peer_weight,
         rows,
         rows_peer,
     )
@@ -212,23 +244,22 @@
     back = summed[:piece].astype(F32).reshape(piece, exp_local, per_expert).transpose(1, 0, 2)
 
     pair_part = jnp.sum(hidden.astype(F32) * back, axis=1).reshape(1, total_slots)
-    more = 2 * rank // z_width
+    more = 2 * half // z_width
     small = jnp.concatenate([summed[piece : piece + more], pair_part.astype(BF)])
-    small = small.reshape(2, -1, 128)
-    theirs = lax.dynamic_index_in_dim(small, 1 - core, axis=0, keepdims=False)
-    mine = lax.dynamic_index_in_dim(small, core, axis=0, keepdims=False).astype(F32)
-    mine = (mine + lax.ppermute(theirs, "core", swap).astype(F32)).astype(BF)
-    half = lax.all_gather(mine, "z", axis=0, tiled=False)
-    other = lax.ppermute(half, "core", swap)
-    everything = jnp.where(
-        core == 0, jnp.stack([half, other], axis=1), jnp.stack([other, half], axis=1)
-    )
-    everything = everything.reshape(z_width, more + 1, total_slots)
-    split = (rank, exp_local, per_expert)
-    latent = everything[: z_width // 2, :more].reshape(split).astype(F32)
-    query = everything[z_width // 2 :, :more].reshape(split).astype(F32)
-    pair_sum = jnp.sum(everything[:, more].astype(F32), axis=0).reshape(exp_local, per_expert)
-    weight_grad = pair_sum + jnp.sum(latent * query, axis=0)
+    gathered = lax.all_gather(small.reshape(-1, 128), "z", axis=0, tiled=False)
+    sides = []
+    for side in (gathered, lax.ppermute(gathered, "core", swap)):
+        side = side.reshape(z_width, more + 1, total_slots).astype(F32)
+        lat_side = side[: z_width // 2, :more].reshape(half, exp_local, per_expert)
+        ql_side = side[z_width // 2 :, :more].reshape(half, exp_local, per_expert)
+        sums = jnp.sum(side[:, more], axis=0).reshape(exp_local, per_expert)
+        sides.append((lat_side, ql_side, sums + jnp.sum(lat_side * ql_side, axis=0)))
+    own_side, peer_side = sides
+    weight_grad = own_side[2] + peer_side[2]
+    latent, query = (
+        jnp.where(core == 0, jnp.concatenate([a, b]), jnp.concatenate([b, a]))
+        for a, b in zip(own_side[:2], peer_side[:2])
+    )
 
     returned = lax.all_to_all(
         weight_grad.astype(BF).reshape(exp_local, most, source_count).transpose(2, 0, 1),

time: 155 us -> 153 us (0.987)
  blocking collectives: 71.2 us -> 66.9 us
  other arithmetic: 2.31 us -> 5.78 us
  starting transfers between devices: 52 us -> 50.4 us
    ppermute x1, starting transfers between devices: 8.01 us -> 2.41 us  [on_device(): rows_peer = lax.ppermute(rows, 'core', swap)]
    unnamed x1, blocking collectives: 49.3 us -> 44.8 us
    all_to_all x1, starting transfers between devices: 5.42 us -> 8.6 us  [on_device(): lax.all_to_all(weight_grad.astype(BF).reshape(exp_local, most, source_cou...]
    convert_element_type x2, other arithmetic: 0.16 us -> 2.28 us  [on_device(): gate_f, up_f = (gate_f.astype(F32), up_f.astype(F32))]
    unnamed x24 -> x28, local copies, waits for them, and re-layouts: 3.72 us -> 4.27 us
  transfers between devices with their start and end apart: 7 -> 7, of which waited for: 3 -> 3; matrix products, arithmetic and copies ran while one was open for 8% -> 12% of each run, Pallas kernels for 0% -> 0%
where the time goes in v7:
time: 153 us
  blocking collectives  66.9 us (44%)
  starting transfers between devices  50.4 us (33%)
  local copies, waits for them, and re-layouts  11.3 us (7%)
  Pallas kernels  7.7 us (5%)
  other arithmetic  5.78 us (4%)
  matrix products  4.77 us (3%)
  waiting for transfers between devices  3.88 us (3%)
  between operations  1.85 us (1%)
    unnamed x1, blocking collectives  44.8 us
    all_gather x1, blocking collectives, on_device(): gathered = lax.all_gather(small.reshape(-1, 128), 'z', axis=0, tiled=False)  22.1 us
    ppermute x1, starting transfers between devices, on_device(): lax.ppermute(gathered, 'core', swap)  14.6 us
    all_to_all x1, starting transfers between devices, on_device(): lax.all_to_all(send, 'exp', split_axis=0, concat_axis=0, tiled=True)  10.5 us
    ppermute x1, starting transfers between devices, on_device(): lax.ppermute(jnp.concatenate([first_send, hidden], axis=2), 'core', swap)  9.44 us
    all_to_all x1, starting transfers between devices, on_device(): lax.all_to_all(weight_grad.astype(BF).reshape(exp_local, most, source_cou...  8.6 us
    pallas_call x1, Pallas kernels, partial_sums(): pl.pallas_call(kernel, out_shape=jax.ShapeDtypeStruct((z_width * chunk, e...  5.33 us
    unnamed x28, local copies, waits for them, and re-layouts  4.27 us
  transfers between devices with their start and end apart: 7, of which 3 were waited for; matrix products, arithmetic and copies ran while one was open for 12% of the time, Pallas kernels for 0%

profile of v7, /device:TPU:1, one launch (start us, length us, event | category | flops | bytes accessed | tf_op | source)
XLA Modules:
  0.0 152.6 jit_solution(17257138859129485427)
XLA Ops:
  0.6 2.4 %dispatch_slab.1 = bf16[32,56,128]{2,1,0:T(8,128)(2,1)} custom-call(s32[8,128]{1,0:T(8,128)} %bitcast.115, bf16[8,128]{1,0:T(8,128)(2,1)} %bitcast.123, s32[1,128]{1,0:T(1,128)} %bitcast.124, bf16[128,128]{1,0:T(8,128)(2,1)} %grad_ref.1), custom_call_target="tpu_custom_call" | custom-call | tf_op jit(solution)/shard_map/dispatch_slab/pallas_call | solution.py:138
  3.0 10.5 %all-to-all-start = ((bf16[32,56,128]{2,1,0:T(8,128)(2,1)}), bf16[32,56,128]{2,1,0:T(8,128)(2,1)S(1)}, u32[]{:S(2)}, u32[]{:S(2)}) async-start(bf16[32,56,128]{2,1,0:T(8,128)(2,1)} %dispatch_slab.1), calls=%async_computation | async-start | bytes 917504 | tf_op jit(solution)/shard_map/all_to_all | solution.py:196
  13.5 1.3 copy.62
  14.8 0.5 copy.63
  15.3 0.5 reshape.205.a_ref
  15.8 1.2 convert_element_type.192
  17.0 0.2 copy.65
  17.3 1.1 convert_element_type.193
  18.3 1.0 copy.66
  19.3 0.0 copy-start.10
  19.3 1.1 multiply_convert_fusion.17.h_ref
  20.5 0.7 pad_maximum_fusion.1
  21.2 9.4 %collective-permute-start = (bf16[4,48,640]{2,1,0:T(8,128)(2,1)}, bf16[4,48,640]{2,1,0:T(8,128)(2,1)}, u32[]{:S(2)}, u32[]{:S(2)}) collective-permute-start(bf16[4,48,640]{2,1,0:T(8,128)(2,1)} %pad_maximum_fusion.1), channel_id=1, source_target_pairs={{0,1},{1,0},{2,3},{3,2},{4,5},{5,4},{6,7},{7,6},{8,9},{9,8},{10,11... | collective-permute-start | bytes 737288 | tf_op jit(solution)/shard_map/ppermute | solution.py:229
  30.7 0.1 constant_dynamic-slice_fusion.2
  30.8 0.1 pad_maximum_fusion
  30.9 1.9 %collective-permute-start.1 = (bf16[4,1024,128]{2,1,0:T(8,128)(2,1)S(1)}, bf16[4,1024,128]{2,1,0:T(8,128)(2,1)S(1)}, u32[]{:S(2)}, u32[]{:S(2)}) collective-permute-start(bf16[4,1024,128]{2,1,0:T(8,128)(2,1)S(1)} %pad_maximum_fusion), channel_id=1, source_target_pairs={{0,1},{1,0},{2,3},{3,2},{4,5},{5,4},{6,7},{7,6},{8,9},{9,8},{10,11... | collective-permute-start | bytes 3145736 | tf_op jit(solution)/shard_map/ppermute | solution.py:177
  32.8 1.3 dynamic-slice.4
  34.7 0.1 fusion.16
  34.8 0.1 fusion.29
  35.0 0.1 select_reduce_fusion.2
  35.1 0.1 copy.67
  35.2 0.0 copy-start.3
  35.2 2.4 %collective-permute-start.2 = (bf16[4,384,128]{2,1,0:T(8,128)(2,1)S(1)}, bf16[4,384,128]{2,1,0:T(8,128)(2,1)}, u32[]{:S(2)}, u32[]{:S(2)}) collective-permute-start(bf16[4,384,128]{2,1,0:T(8,128)(2,1)S(1)} %bitcast.103), channel_id=1, source_target_pairs={{0,1},{1,0},{2,3},{3,2},{4,5},{5,4},{6,7},{7,6},{8,9},{9,8},{10,11... | collective-permute-start | bytes 1179656 | tf_op jit(solution)/shard_map/ppermute | solution.py:199
  37.7 0.1 fusion.31
  37.9 0.6 select_reduce_fusion.1
  38.5 0.1 eq.78
  38.5 0.7 broadcast_in_dim_reshape.3.t_ref
  39.3 1.0 copy-done.8
  40.2 5.3 %partial_sums.1 = bf16[880,1536]{1,0:T(8,128)(2,1)} custom-call(s32[1]{0:T(128)} %bitcast.6.core_ref, f32[4,1,384]{2,1,0:T(1,128)} %broadcast_in_dim_reshape.3.t_ref, bf16[4,2,48,256]{3,2,1,0:T(8,128)(2,1)} %copy-done.5, bf16[4,48,384]{2,1,0:T(8,128)(2,1)} %copy-done.1, bf16[4,48,640]{2,1,0:T(8,128)(2,1)} %collective-permute-done.p_ref, ...), custom_call_target="tpu_custom_call" | custom-call | tf_op jit(solution)/shard_map/partial_sums/pallas_call | solution.py:64
  45.6 44.8 %fusion = bf16[56,1536]{1,0:T(8,128)(2,1)S(1)} fusion(bf16[880,1536]{1,0:T(8,128)(2,1)} %partial_sums.1), kind=kCustom, calls=%all-reduce-scatter | all-reduce-scatter fusion | flops 1376257 | bytes 2879488
  90.4 2.9 %collective-permute-start.4 = (bf16[15,1536]{1,0:T(8,128)(2,1)S(1)}, bf16[15,1536]{1,0:T(8,128)(2,1)S(1)}, u32[]{:S(2)}, u32[]{:S(2)}) collective-permute-start(bf16[15,1536]{1,0:T(8,128)(2,1)S(1)} %slice.55), channel_id=1, source_target_pairs={{0,2},{2,4},{4,6},{6,8},{8,10},{10,12},{12,14},{14,16},{16,18},{18... | collective-permute-start | bytes 138248
  93.3 0.1 compare_convert_fusion
  93.4 0.1 mul.88
  93.5 1.0 collective-permute-done.4
  94.5 0.2 concatenate.56
  94.7 0.1 constant_dynamic-slice_fusion
  94.8 0.1 fusion.23
  95.0 22.1 %all_gather.3 = bf16[16,60,128]{2,1,0:T(8,128)(2,1)S(1)} all-gather(bf16[1,60,128]{2,1,0:T(8,128)(2,1)S(1)} %all_gather_reshape.3), channel_id=1, replica_groups=mesh['exp'=32,'z'=16,'core'=2] {'z'}, dimensions={0}, use_global_device_ids=true | all-gather | bytes 261120 | tf_op jit(solution)/shard_map/all_gather | solution.py:249
  117.1 14.6 %collective-permute-start.3 = (bf16[16,60,128]{2,1,0:T(8,128)(2,1)S(1)}, bf16[16,60,128]{2,1,0:T(8,128)(2,1)S(1)}, u32[]{:S(2)}, u32[]{:S(2)}) collective-permute-start(bf16[16,60,128]{2,1,0:T(8,128)(2,1)S(1)} %all_gather.3), channel_id=1, source_target_pairs={{0,1},{1,0},{2,3},{3,2},{4,5},{5,4},{6,7},{7,6},{8,9},{9,8},{10,11... | collective-permute-start | bytes 737288 | tf_op jit(solution)/shard_map/ppermute | solution.py:251
  131.7 0.3 reshape.219
  131.9 0.1 multiply_reduce_fusion.1
  132.0 0.1 concatenate.52
  132.2 0.1 concatenate.48
  132.3 0.1 slice_reduce_fusion.1
  132.4 0.4 collective-permute-done.3
  132.8 0.3 reshape.220
  133.1 0.0 copy-start.6
  133.1 0.1 slice_reduce_fusion
  133.2 0.1 multiply_reduce_fusion
  133.3 0.1 concatenate.53
  133.4 0.1 concatenate.49
  133.6 0.1 convert_element_type.185
  133.7 0.7 copy.76
  134.4 8.6 %all-to-all-start.1 = ((bf16[32,4,12]{2,1,0:T(4,128)(2,1)}), bf16[32,4,12]{2,1,0:T(4,128)(2,1)S(1)}, u32[]{:S(2)}, u32[]{:S(2)}) async-start(bf16[32,4,12]{2,1,0:T(4,128)(2,1)} %copy.76), calls=%async_computation.1 | async-start | bytes 65536 | tf_op jit(solution)/shard_map/all_to_all | solution.py:264
  143.0 0.2 fusion.26
  143.2 0.0 copy-start.4
  143.3 0.5 multiply_convert_fusion.15
  143.8 0.4 copy-done.4
  144.2 1.4 fusion.10
  145.6 1.9 %fusion.12 = bf16[4,8,48,64]{3,2,1,0:T(8,128)(2,1)} fusion(f32[64,4,384]{2,0,1:T(8,128)S(1)} %copy.70, f32[8,4,384]{2,0,1:T(8,128)S(1)} %compare_convert_fusion, bf16[4,48,384]{2,1,0:T(8,128)(2,1)S(1)} %copy-done.2), kind=kOutput, calls=%fused_computation.13 | convolution fusion | flops 77168640 | bytes 786432 | tf_op jit(solution)/shard_map/tres,efs->etfr/dot_general | solution.py:278
  147.4 0.9 copy.74
  148.4 0.9 copy.73
  149.3 2.5 %all-to-all-done.1 = bf16[32,4,12]{2,1,0:T(4,128)(2,1)S(1)} async-done(((bf16[32,4,12]{2,1,0:T(4,128)(2,1)}), bf16[32,4,12]{2,1,0:T(4,128)(2,1)S(1)}, u32[]{:S(2)}, u32[]{:S(2)}) %all-to-all-start.1) | async-done | bytes 3104 | tf_op jit(solution)/shard_map/all_to_all | solution.py:264
  151.8 0.8 fusion.15
  (39 shorter events, 0.4 us)
Async XLA Ops:
  3.0 32.0 %all-to-all-start = ((bf16[32,56,128]{2,1,0:T(8,128)(2,1)}), bf16[32,56,128]{2,1,0:T(8,128)(2,1)S(1)}, u32[]{:S(2)}, u32[]{:S(2)}) async-start(bf16[32,56,128]{2,1,0:T(8,128)(2,1)} %dispatch_slab.1), calls=%async_computation | async-start | bytes 917504 | tf_op jit(solution)/shard_map/all_to_all | solution.py:196
  15.8 4.7 %copy-start.5 = (bf16[4,2,48,256]{3,2,1,0:T(8,128)(2,1)}, bf16[4,2,48,256]{3,2,1,0:T(8,128)(2,1)S(1)}, u32[]{:S(2)}) copy-start(bf16[4,2,48,256]{3,2,1,0:T(8,128)(2,1)S(1)} %reshape.205.a_ref) | copy-start | bytes 589828
  15.8 14.9 %copy-start = (bf16[4,1536,128]{2,1,0:T(8,128)(2,1)S(1)}, bf16[4,1536,128]{2,1,0:T(8,128)(2,1)}, u32[]{:S(2)}) copy-start(bf16[4,1536,128]{2,1,0:T(8,128)(2,1)} %param.15) | copy-start | bytes 4718596
  19.3 11.4 %copy-start.7 = (bf16[4,8,64,128]{3,2,1,0:T(8,128)(2,1)S(1)}, bf16[4,8,64,128]{3,2,1,0:T(8,128)(2,1)}, u32[]{:S(2)}) copy-start(bf16[4,8,64,128]{3,2,1,0:T(8,128)(2,1)} %param.17) | copy-start | bytes 1572868
  19.3 15.4 %copy-start.10 = (s32[128,8]{0,1:T(8,128)S(1)}, s32[128,8]{0,1:T(8,128)}, u32[]{:S(2)}) copy-start(s32[128,8]{0,1:T(8,128)} %param.10) | copy-start | bytes 12292
  20.5 14.6 %copy-start.1 = (bf16[4,48,384]{2,1,0:T(8,128)(2,1)}, bf16[4,48,384]{2,1,0:T(8,128)(2,1)S(1)}, u32[]{:S(2)}) copy-start(bf16[4,48,384]{2,1,0:T(8,128)(2,1)S(1)} %multiply_convert_fusion.17.h_ref) | copy-start | bytes 442372
  21.2 18.0 %collective-permute-start = (bf16[4,48,640]{2,1,0:T(8,128)(2,1)}, bf16[4,48,640]{2,1,0:T(8,128)(2,1)}, u32[]{:S(2)}, u32[]{:S(2)}) collective-permute-start(bf16[4,48,640]{2,1,0:T(8,128)(2,1)} %pad_maximum_fusion.1), channel_id=1, source_target_pairs={{0,1},{1,0},{2,3},{3,2},{4,5},{5,4},{6,7},{7,6},{8,9},{9,8},{10,11... | collective-permute-start | bytes 737288 | tf_op jit(solution)/shard_map/ppermute | solution.py:229
  30.9 8.4 %collective-permute-start.1 = (bf16[4,1024,128]{2,1,0:T(8,128)(2,1)S(1)}, bf16[4,1024,128]{2,1,0:T(8,128)(2,1)S(1)}, u32[]{:S(2)}, u32[]{:S(2)}) collective-permute-start(bf16[4,1024,128]{2,1,0:T(8,128)(2,1)S(1)} %pad_maximum_fusion), channel_id=1, source_target_pairs={{0,1},{1,0},{2,3},{3,2},{4,5},{5,4},{6,7},{7,6},{8,9},{9,8},{10,11... | collective-permute-start | bytes 3145736 | tf_op jit(solution)/shard_map/ppermute | solution.py:177
  35.2 4.1 %copy-start.3 = (bf16[48,32,128]{2,1,0:T(8,128)(2,1)}, bf16[48,32,128]{2,1,0:T(8,128)(2,1)S(1)}, u32[]{:S(2)}) copy-start(bf16[48,32,128]{2,1,0:T(8,128)(2,1)S(1)} %copy.67) | copy-start | bytes 1179652
  35.2 4.0 %collective-permute-start.2 = (bf16[4,384,128]{2,1,0:T(8,128)(2,1)S(1)}, bf16[4,384,128]{2,1,0:T(8,128)(2,1)}, u32[]{:S(2)}, u32[]{:S(2)}) collective-permute-start(bf16[4,384,128]{2,1,0:T(8,128)(2,1)S(1)} %bitcast.103), channel_id=1, source_target_pairs={{0,1},{1,0},{2,3},{3,2},{4,5},{5,4},{6,7},{7,6},{8,9},{9,8},{10,11... | collective-permute-start | bytes 1179656 | tf_op jit(solution)/shard_map/ppermute | solution.py:199
  39.2 1.0 copy-start.8
  45.5 49.3 %copy-start.2 = (bf16[4,48,384]{2,1,0:T(8,128)(2,1)S(1)}, bf16[4,48,384]{2,1,0:T(8,128)(2,1)}, u32[]{:S(2)}) copy-start(bf16[4,48,384]{2,1,0:T(8,128)(2,1)} %copy-done.1) | copy-start | bytes 442372
  90.4 4.1 %collective-permute-start.4 = (bf16[15,1536]{1,0:T(8,128)(2,1)S(1)}, bf16[15,1536]{1,0:T(8,128)(2,1)S(1)}, u32[]{:S(2)}, u32[]{:S(2)}) collective-permute-start(bf16[15,1536]{1,0:T(8,128)(2,1)S(1)} %slice.55), channel_id=1, source_target_pairs={{0,2},{2,4},{4,6},{6,8},{8,10},{10,12},{12,14},{14,16},{16,18},{18... | collective-permute-start | bytes 138248
  117.1 15.7 %collective-permute-start.3 = (bf16[16,60,128]{2,1,0:T(8,128)(2,1)S(1)}, bf16[16,60,128]{2,1,0:T(8,128)(2,1)S(1)}, u32[]{:S(2)}, u32[]{:S(2)}) collective-permute-start(bf16[16,60,128]{2,1,0:T(8,128)(2,1)S(1)} %all_gather.3), channel_id=1, source_target_pairs={{0,1},{1,0},{2,3},{3,2},{4,5},{5,4},{6,7},{7,6},{8,9},{9,8},{10,11... | collective-permute-start | bytes 737288 | tf_op jit(solution)/shard_map/ppermute | solution.py:251
  133.1 10.2 %copy-start.6 = (f32[4,48,384]{2,1,0:T(8,128)S(1)}, f32[4,48,384]{2,1,0:T(8,128)}, u32[]{:S(2)}) copy-start(f32[4,48,384]{2,1,0:T(8,128)} %copy.66) | copy-start | bytes 884740
  133.1 10.2 %copy-start.9 = (bf16[4,8,48,64]{3,2,1,0:T(8,128)(2,1)S(1)}, bf16[4,8,48,64]{3,2,1,0:T(8,128)(2,1)}, u32[]{:S(2)}) copy-start(bf16[4,8,48,64]{3,2,1,0:T(8,128)(2,1)} %param.16) | copy-start | bytes 589828
  134.4 17.4 %all-to-all-start.1 = ((bf16[32,4,12]{2,1,0:T(4,128)(2,1)}), bf16[32,4,12]{2,1,0:T(4,128)(2,1)S(1)}, u32[]{:S(2)}, u32[]{:S(2)}) async-start(bf16[32,4,12]{2,1,0:T(4,128)(2,1)} %copy.76), calls=%async_computation.1 | async-start | bytes 65536 | tf_op jit(solution)/shard_map/all_to_all | solution.py:264
  143.2 1.0 copy-start.4

commit v8 on v7

--- a/solution.py
+++ b/solution.py
@@ -246,18 +246,24 @@
     pair_part = jnp.sum(hidden.astype(F32) * back, axis=1).reshape(1, total_slots)
     more = 2 * half // z_width
     small = jnp.concatenate([summed[piece : piece + more], pair_part.astype(BF)])
-    gathered = lax.all_gather(small.reshape(-1, 128), "z", axis=0, tiled=False)
+    rings = [[2 * z + (z + p) % 2 for z in range(z_width)] for p in range(2)]
+    gathered = lax.all_gather(
+        small.reshape(-1, 128), ("z", "core"), axis=0, tiled=False, axis_index_groups=rings
+    )
     sides = []
     for side in (gathered, lax.ppermute(gathered, "core", swap)):
         side = side.reshape(z_width, more + 1, total_slots).astype(F32)
-        lat_side = side[: z_width // 2, :more].reshape(half, exp_local, per_expert)
-        ql_side = side[z_width // 2 :, :more].reshape(half, exp_local, per_expert)
-        sums = jnp.sum(side[:, more], axis=0).reshape(exp_local, per_expert)
-        sides.append((lat_side, ql_side, sums + jnp.sum(lat_side * ql_side, axis=0)))
+        lat_side, ql_side = side[: z_width // 2, :more], side[z_width // 2 :, :more]
+        sums = jnp.sum(side[:, more], axis=0) + jnp.sum(lat_side * ql_side, axis=(0, 1))
+        sides.append((lat_side, ql_side, sums.reshape(exp_local, per_expert)))
     own_side, peer_side = sides
     weight_grad = own_side[2] + peer_side[2]
+    from_core = (lax.axis_index("z") + core + jnp.arange(z_width // 2, dtype=jnp.int32)) % 2
+    from_core = from_core[:, None, None]
     latent, query = (
-        jnp.where(core == 0, jnp.concatenate([a, b]), jnp.concatenate([b, a]))
+        jnp.concatenate(
+            [jnp.where(from_core == 0, a, b), jnp.where(from_core == 0, b, a)]
+        ).reshape(rank, exp_local, per_expert)
         for a, b in zip(own_side[:2], peer_side[:2])
     )
 

time: 153 us -> 148 us (0.967)
  starting transfers between devices: 50.4 us -> 35.8 us
  blocking collectives: 66.9 us -> 76.8 us
    ppermute x1, starting transfers between devices: 14.6 us -> 1.95 us  [on_device(): lax.ppermute(gathered, 'core', swap)]
    all_gather x1, blocking collectives: 22.1 us -> 30.1 us  [on_device(): lax.all_gather(small.reshape(-1, 128), ('z', 'core'), axis=0, tiled=False...]
    all_to_all x1, starting transfers between devices: 8.6 us -> 6.65 us  [on_device(): lax.all_to_all(weight_grad.astype(BF).reshape(exp_local, most, source_cou...]
    unnamed x1, blocking collectives: 44.8 us -> 46.7 us
  transfers between devices with their start and end apart: 7 -> 7, of which waited for: 3 -> 2; matrix products, arithmetic and copies ran while one was open for 12% -> 12% of each run, Pallas kernels for 0% -> 0%
where the time goes in v8:
time: 148 us; the launch traced here: 147 us
  blocking collectives  76.8 us (52%)
  starting transfers between devices  35.8 us (24%)
  local copies, waits for them, and re-layouts  11.3 us (8%)
  Pallas kernels  7.69 us (5%)
  other arithmetic  6 us (4%)
  matrix products  4.76 us (3%)
  waiting for transfers between devices  3.24 us (2%)
  between operations  1.84 us (1%)
    unnamed x1, blocking collectives  46.7 us
    all_gather x1, blocking collectives, on_device(): lax.all_gather(small.reshape(-1, 128), ('z', 'core'), axis=0, tiled=False...  30.1 us
    all_to_all x1, starting transfers between devices, on_device(): lax.all_to_all(send, 'exp', split_axis=0, concat_axis=0, tiled=True)  10.5 us
    ppermute x1, starting transfers between devices, on_device(): lax.ppermute(jnp.concatenate([first_send, hidden], axis=2), 'core', swap)  9.44 us
    all_to_all x1, starting transfers between devices, on_device(): lax.all_to_all(weight_grad.astype(BF).reshape(exp_local, most, source_cou...  6.65 us
    pallas_call x1, Pallas kernels, partial_sums(): pl.pallas_call(kernel, out_shape=jax.ShapeDtypeStruct((z_width * chunk, e...  5.32 us
    unnamed x28, local copies, waits for them, and re-layouts  4.3 us
  transfers between devices with their start and end apart: 7, of which 2 were waited for; matrix products, arithmetic and copies ran while one was open for 12% of the time, Pallas kernels for 0%

profile of v8, /device:TPU:1, one launch (start us, length us, event | category | flops | bytes accessed | tf_op | source)
XLA Modules:
  0.0 147.5 jit_solution(7857698770787744792)
XLA Ops:
  0.6 2.4 %dispatch_slab.1 = bf16[32,56,128]{2,1,0:T(8,128)(2,1)} custom-call(s32[8,128]{1,0:T(8,128)} %bitcast.115, bf16[8,128]{1,0:T(8,128)(2,1)} %bitcast.123, s32[1,128]{1,0:T(1,128)} %bitcast.124, bf16[128,128]{1,0:T(8,128)(2,1)} %grad_ref.1), custom_call_target="tpu_custom_call" | custom-call | tf_op jit(solution)/shard_map/dispatch_slab/pallas_call | solution.py:138
  3.0 10.5 %all-to-all-start = ((bf16[32,56,128]{2,1,0:T(8,128)(2,1)}), bf16[32,56,128]{2,1,0:T(8,128)(2,1)S(1)}, u32[]{:S(2)}, u32[]{:S(2)}) async-start(bf16[32,56,128]{2,1,0:T(8,128)(2,1)} %dispatch_slab.1), calls=%async_computation | async-start | bytes 917504 | tf_op jit(solution)/shard_map/all_to_all | solution.py:196
  13.5 1.3 copy.62
  14.8 0.5 copy.63
  15.3 0.5 reshape.166.a_ref
  15.8 0.0 copy-start
  15.8 1.2 convert_element_type.192
  17.0 0.2 copy.65
  17.3 1.1 convert_element_type.193
  18.3 1.0 copy.66
  19.3 0.0 copy-start.10
  19.3 1.1 multiply_convert_fusion.19.h_ref
  20.5 0.7 pad_maximum_fusion.3
  21.2 9.4 %collective-permute-start = (bf16[4,48,640]{2,1,0:T(8,128)(2,1)}, bf16[4,48,640]{2,1,0:T(8,128)(2,1)}, u32[]{:S(2)}, u32[]{:S(2)}) collective-permute-start(bf16[4,48,640]{2,1,0:T(8,128)(2,1)} %pad_maximum_fusion.3), channel_id=1, source_target_pairs={{0,1},{1,0},{2,3},{3,2},{4,5},{5,4},{6,7},{7,6},{8,9},{9,8},{10,11... | collective-permute-start | bytes 737288 | tf_op jit(solution)/shard_map/ppermute | solution.py:229
  30.7 0.1 constant_dynamic-slice_fusion.2
  30.8 0.1 pad_maximum_fusion
  30.9 1.9 %collective-permute-start.1 = (bf16[4,1024,128]{2,1,0:T(8,128)(2,1)S(1)}, bf16[4,1024,128]{2,1,0:T(8,128)(2,1)S(1)}, u32[]{:S(2)}, u32[]{:S(2)}) collective-permute-start(bf16[4,1024,128]{2,1,0:T(8,128)(2,1)S(1)} %pad_maximum_fusion), channel_id=1, source_target_pairs={{0,1},{1,0},{2,3},{3,2},{4,5},{5,4},{6,7},{7,6},{8,9},{9,8},{10,11... | collective-permute-start | bytes 3145736 | tf_op jit(solution)/shard_map/ppermute | solution.py:177
  32.8 0.1 fusion.16
  32.9 0.1 fusion.25
  33.0 0.1 select_reduce_fusion.2
  33.2 0.1 copy.67
  33.3 0.0 copy-start.3
  33.3 2.4 %collective-permute-start.2 = (bf16[4,384,128]{2,1,0:T(8,128)(2,1)S(1)}, bf16[4,384,128]{2,1,0:T(8,128)(2,1)}, u32[]{:S(2)}, u32[]{:S(2)}) collective-permute-start(bf16[4,384,128]{2,1,0:T(8,128)(2,1)S(1)} %bitcast.103), channel_id=1, source_target_pairs={{0,1},{1,0},{2,3},{3,2},{4,5},{5,4},{6,7},{7,6},{8,9},{9,8},{10,11... | collective-permute-start | bytes 1179656 | tf_op jit(solution)/shard_map/ppermute | solution.py:199
  35.7 0.1 fusion.27
  35.9 0.6 select_reduce_fusion.1
  36.5 0.7 broadcast_in_dim_reshape.3.t_ref
  37.2 0.0 collective-permute-done.p_ref
  37.2 1.0 copy-done.8
  38.2 5.3 %partial_sums.1 = bf16[880,1536]{1,0:T(8,128)(2,1)} custom-call(s32[1]{0:T(128)} %bitcast.6.core_ref, f32[4,1,384]{2,1,0:T(1,128)} %broadcast_in_dim_reshape.3.t_ref, bf16[4,2,48,256]{3,2,1,0:T(8,128)(2,1)} %copy-done.5, bf16[4,48,384]{2,1,0:T(8,128)(2,1)} %copy-done.1, bf16[4,48,640]{2,1,0:T(8,128)(2,1)} %collective-permute-done.p_ref, ...), custom_call_target="tpu_custom_call" | custom-call | tf_op jit(solution)/shard_map/partial_sums/pallas_call | solution.py:64
  43.5 46.7 %fusion = bf16[56,1536]{1,0:T(8,128)(2,1)S(1)} fusion(bf16[880,1536]{1,0:T(8,128)(2,1)} %partial_sums.1), kind=kCustom, calls=%all-reduce-scatter | all-reduce-scatter fusion | flops 1376257 | bytes 2879488
  90.3 2.9 %collective-permute-start.4 = (bf16[15,1536]{1,0:T(8,128)(2,1)S(1)}, bf16[15,1536]{1,0:T(8,128)(2,1)S(1)}, u32[]{:S(2)}, u32[]{:S(2)}) collective-permute-start(bf16[15,1536]{1,0:T(8,128)(2,1)S(1)} %slice.55), channel_id=1, source_target_pairs={{0,2},{2,4},{4,6},{6,8},{8,10},{10,12},{12,14},{14,16},{16,18},{18... | collective-permute-start | bytes 138248
  93.2 1.3 dynamic-slice.4
  95.2 0.1 eq.87
  95.3 0.3 concatenate.20
  95.5 0.1 constant_dynamic-slice_fusion
  95.6 0.1 fusion.19
  95.8 30.1 %all_gather.3 = bf16[16,60,128]{2,1,0:T(8,128)(2,1)S(1)} all-gather(bf16[1,60,128]{2,1,0:T(8,128)(2,1)S(1)} %all_gather_reshape.3), channel_id=1, replica_groups={{0,3,4,7,8,11,12,15,16,19,20,23,24,27,28,31},{1,2,5,6,9,10,13,14,17,18,..., dimensions={0}, use_global_device_ids=true | all-gather | bytes 261120 | tf_op jit(solution)/shard_map/all_gather | solution.py:250
  125.9 1.9 %collective-permute-start.3 = (bf16[16,60,128]{2,1,0:T(8,128)(2,1)S(1)}, bf16[16,60,128]{2,1,0:T(8,128)(2,1)S(1)}, u32[]{:S(2)}, u32[]{:S(2)}) collective-permute-start(bf16[16,60,128]{2,1,0:T(8,128)(2,1)S(1)} %all_gather.3), channel_id=1, source_target_pairs={{0,1},{1,0},{2,3},{3,2},{4,5},{5,4},{6,7},{7,6},{8,9},{9,8},{10,11... | collective-permute-start | bytes 737288 | tf_op jit(solution)/shard_map/ppermute | solution.py:254
  127.8 0.1 compare_convert_fusion
  127.9 0.1 mul.86
  128.0 0.3 reshape.182
  128.3 0.1 slice_reduce_fusion.1
  128.4 0.9 collective-permute-done.3
  129.3 0.3 reshape.183
  129.6 0.1 slice_reduce_fusion
  129.7 0.3 slice_select_fusion.1
  130.0 0.2 pad_maximum_fusion.1
  130.2 0.0 copy-start.6
  130.2 0.0 copy-start.9
  130.2 0.2 reshape.173
  130.5 0.1 convert_element_type.185
  130.5 0.7 copy.76
  131.3 6.7 %all-to-all-start.1 = ((bf16[32,4,12]{2,1,0:T(4,128)(2,1)}), bf16[32,4,12]{2,1,0:T(4,128)(2,1)S(1)}, u32[]{:S(2)}, u32[]{:S(2)}) async-start(bf16[32,4,12]{2,1,0:T(4,128)(2,1)} %copy.76), calls=%async_computation.1 | async-start | bytes 65536 | tf_op jit(solution)/shard_map/all_to_all | solution.py:270
  137.9 0.2 reshape.176
  138.2 0.1 fusion.23
  138.3 0.0 copy-start.4
  138.4 0.5 multiply_convert_fusion.17
  138.9 0.4 copy-done.4
  139.3 1.4 fusion.10
  140.7 1.9 %fusion.12 = bf16[4,8,48,64]{3,2,1,0:T(8,128)(2,1)} fusion(f32[64,4,384]{2,0,1:T(8,128)S(1)} %copy.70, f32[8,4,384]{2,0,1:T(8,128)S(1)} %compare_convert_fusion, bf16[4,48,384]{2,1,0:T(8,128)(2,1)S(1)} %copy-done.2), kind=kOutput, calls=%fused_computation.13 | convolution fusion | flops 77168640 | bytes 786432 | tf_op jit(solution)/shard_map/tres,efs->etfr/dot_general | solution.py:284
  142.5 0.9 copy.74
  143.5 0.9 copy.73
  144.4 2.3 %all-to-all-done.1 = bf16[32,4,12]{2,1,0:T(4,128)(2,1)S(1)} async-done(((bf16[32,4,12]{2,1,0:T(4,128)(2,1)}), bf16[32,4,12]{2,1,0:T(4,128)(2,1)S(1)}, u32[]{:S(2)}, u32[]{:S(2)}) %all-to-all-start.1) | async-done | bytes 3104 | tf_op jit(solution)/shard_map/all_to_all | solution.py:270
  146.7 0.8 fusion.15
  (38 shorter events, 0.4 us)
Async XLA Ops:
  3.0 30.1 %all-to-all-start = ((bf16[32,56,128]{2,1,0:T(8,128)(2,1)}), bf16[32,56,128]{2,1,0:T(8,128)(2,1)S(1)}, u32[]{:S(2)}, u32[]{:S(2)}) async-start(bf16[32,56,128]{2,1,0:T(8,128)(2,1)} %dispatch_slab.1), calls=%async_computation | async-start | bytes 917504 | tf_op jit(solution)/shard_map/all_to_all | solution.py:196
  15.8 4.7 %copy-start.5 = (bf16[4,2,48,256]{3,2,1,0:T(8,128)(2,1)}, bf16[4,2,48,256]{3,2,1,0:T(8,128)(2,1)S(1)}, u32[]{:S(2)}) copy-start(bf16[4,2,48,256]{3,2,1,0:T(8,128)(2,1)S(1)} %reshape.166.a_ref) | copy-start | bytes 589828
  15.8 14.9 %copy-start = (bf16[4,1536,128]{2,1,0:T(8,128)(2,1)S(1)}, bf16[4,1536,128]{2,1,0:T(8,128)(2,1)}, u32[]{:S(2)}) copy-start(bf16[4,1536,128]{2,1,0:T(8,128)(2,1)} %param.15) | copy-start | bytes 4718596
  19.3 11.4 %copy-start.7 = (bf16[4,8,64,128]{3,2,1,0:T(8,128)(2,1)S(1)}, bf16[4,8,64,128]{3,2,1,0:T(8,128)(2,1)}, u32[]{:S(2)}) copy-start(bf16[4,8,64,128]{3,2,1,0:T(8,128)(2,1)} %param.17) | copy-start | bytes 1572868
  19.3 13.5 %copy-start.10 = (s32[128,8]{0,1:T(8,128)S(1)}, s32[128,8]{0,1:T(8,128)}, u32[]{:S(2)}) copy-start(s32[128,8]{0,1:T(8,128)} %param.10) | copy-start | bytes 12292
  20.5 12.7 %copy-start.1 = (bf16[4,48,384]{2,1,0:T(8,128)(2,1)}, bf16[4,48,384]{2,1,0:T(8,128)(2,1)S(1)}, u32[]{:S(2)}) copy-start(bf16[4,48,384]{2,1,0:T(8,128)(2,1)S(1)} %multiply_convert_fusion.19.h_ref) | copy-start | bytes 442372
  21.2 16.0 %collective-permute-start = (bf16[4,48,640]{2,1,0:T(8,128)(2,1)}, bf16[4,48,640]{2,1,0:T(8,128)(2,1)}, u32[]{:S(2)}, u32[]{:S(2)}) collective-permute-start(bf16[4,48,640]{2,1,0:T(8,128)(2,1)} %pad_maximum_fusion.3), channel_id=1, source_target_pairs={{0,1},{1,0},{2,3},{3,2},{4,5},{5,4},{6,7},{7,6},{8,9},{9,8},{10,11... | collective-permute-start | bytes 737288 | tf_op jit(solution)/shard_map/ppermute | solution.py:229
  30.9 6.4 %collective-permute-start.1 = (bf16[4,1024,128]{2,1,0:T(8,128)(2,1)S(1)}, bf16[4,1024,128]{2,1,0:T(8,128)(2,1)S(1)}, u32[]{:S(2)}, u32[]{:S(2)}) collective-permute-start(bf16[4,1024,128]{2,1,0:T(8,128)(2,1)S(1)} %pad_maximum_fusion), channel_id=1, source_target_pairs={{0,1},{1,0},{2,3},{3,2},{4,5},{5,4},{6,7},{7,6},{8,9},{9,8},{10,11... | collective-permute-start | bytes 3145736 | tf_op jit(solution)/shard_map/ppermute | solution.py:177
  33.3 4.0 %copy-start.3 = (bf16[48,32,128]{2,1,0:T(8,128)(2,1)}, bf16[48,32,128]{2,1,0:T(8,128)(2,1)S(1)}, u32[]{:S(2)}) copy-start(bf16[48,32,128]{2,1,0:T(8,128)(2,1)S(1)} %copy.67) | copy-start | bytes 1179652
  33.3 3.9 %collective-permute-start.2 = (bf16[4,384,128]{2,1,0:T(8,128)(2,1)S(1)}, bf16[4,384,128]{2,1,0:T(8,128)(2,1)}, u32[]{:S(2)}, u32[]{:S(2)}) collective-permute-start(bf16[4,384,128]{2,1,0:T(8,128)(2,1)S(1)} %bitcast.103), channel_id=1, source_target_pairs={{0,1},{1,0},{2,3},{3,2},{4,5},{5,4},{6,7},{7,6},{8,9},{9,8},{10,11... | collective-permute-start | bytes 1179656 | tf_op jit(solution)/shard_map/ppermute | solution.py:199
  37.2 1.0 copy-start.8
  43.5 52.1 %copy-start.2 = (bf16[4,48,384]{2,1,0:T(8,128)(2,1)S(1)}, bf16[4,48,384]{2,1,0:T(8,128)(2,1)}, u32[]{:S(2)}) copy-start(bf16[4,48,384]{2,1,0:T(8,128)(2,1)} %copy-done.1) | copy-start | bytes 442372
  90.3 5.0 %collective-permute-start.4 = (bf16[15,1536]{1,0:T(8,128)(2,1)S(1)}, bf16[15,1536]{1,0:T(8,128)(2,1)S(1)}, u32[]{:S(2)}, u32[]{:S(2)}) collective-permute-start(bf16[15,1536]{1,0:T(8,128)(2,1)S(1)} %slice.55), channel_id=1, source_target_pairs={{0,2},{2,4},{4,6},{6,8},{8,10},{10,12},{12,14},{14,16},{16,18},{18... | collective-permute-start | bytes 138248
  125.9 3.4 %collective-permute-start.3 = (bf16[16,60,128]{2,1,0:T(8,128)(2,1)S(1)}, bf16[16,60,128]{2,1,0:T(8,128)(2,1)S(1)}, u32[]{:S(2)}, u32[]{:S(2)}) collective-permute-start(bf16[16,60,128]{2,1,0:T(8,128)(2,1)S(1)} %all_gather.3), channel_id=1, source_target_pairs={{0,1},{1,0},{2,3},{3,2},{4,5},{5,4},{6,7},{7,6},{8,9},{9,8},{10,11... | collective-permute-start | bytes 737288 | tf_op jit(solution)/shard_map/ppermute | solution.py:254
  130.2 8.2 %copy-start.6 = (f32[4,48,384]{2,1,0:T(8,128)S(1)}, f32[4,48,384]{2,1,0:T(8,128)}, u32[]{:S(2)}) copy-start(f32[4,48,384]{2,1,0:T(8,128)} %copy.66) | copy-start | bytes 884740
  130.2 8.2 %copy-start.9 = (bf16[4,8,48,64]{3,2,1,0:T(8,128)(2,1)S(1)}, bf16[4,8,48,64]{3,2,1,0:T(8,128)(2,1)}, u32[]{:S(2)}) copy-start(bf16[4,8,48,64]{3,2,1,0:T(8,128)(2,1)} %param.16) | copy-start | bytes 589828
  131.3 15.4 %all-to-all-start.1 = ((bf16[32,4,12]{2,1,0:T(4,128)(2,1)}), bf16[32,4,12]{2,1,0:T(4,128)(2,1)S(1)}, u32[]{:S(2)}, u32[]{:S(2)}) async-start(bf16[32,4,12]{2,1,0:T(4,128)(2,1)} %copy.76), calls=%async_computation.1 | async-start | bytes 65536 | tf_op jit(solution)/shard_map/all_to_all | solution.py:270
  138.3 1.0 copy-start.4

commit v9 on v8

--- a/solution.py
+++ b/solution.py
@@ -22,7 +22,7 @@
 
     def kernel(core_ref, t_ref, a_ref, h_ref, p_ref, b_ref, w_ref, wp_ref, x_ref, xp_ref, out_ref, f32_ref):
         nums = (((1,), (1,)), ((), ()))
-        own = w_ref[0, :, 0].reshape(z_width * piece, width)
+        own = jnp.concatenate([w_ref[0, z, (core_ref[0] + z) % 2] for z in range(z_width)])
         peer = wp_ref[0]
         both = jnp.concatenate([x_ref[0], xp_ref[0]], axis=1)
         total = lax.dot_general(
@@ -73,7 +73,7 @@
                 pl.BlockSpec((1, piece, slots), lambda e, c: (e, 0, 0)),
                 pl.BlockSpec((1, piece, packed + slots), lambda e, c: (e, 0, 0)),
                 pl.BlockSpec((1, task_count, 1, half, width), lambda e, c: (e, 0, c[0], 0, 0)),
-                pl.BlockSpec((1, z_width, 1, piece, width), lambda e, c: (e, 0, c[0], 0, 0)),
+                pl.BlockSpec((1, z_width, 2, piece, width), lambda e, c: (e, 0, 0, 0, 0)),
                 pl.BlockSpec((1, z_width * piece + packed, width), lambda e, c: (e, 0, 0)),
                 pl.BlockSpec((1, slots, width), lambda e, c: (e, 0, 0)),
                 pl.BlockSpec((1, slots, width), lambda e, c: (e, 0, 0)),
@@ -170,10 +170,14 @@
     second = adapter_second_factor.reshape(exp_local, task_count, 2, half, width)
     first = adapter_first_factor.reshape(exp_local, task_count, piece, 2, half)
     first = first.transpose(0, 3, 2, 1, 4).reshape(exp_local, 2, piece, task_count * half)
+    ring = (lax.axis_index("z") + core) % 2
+    rings = [[2 * z + (z + p) % 2 for z in range(z_width)] for p in range(2)]
+    to_core = (jnp.arange(z_width, dtype=jnp.int32) + ring) % 2
     for_peer = [
-        lax.dynamic_index_in_dim(a, 1 - core, axis=2, keepdims=False).reshape(exp_local, -1, width)
-        for a in (weight, second)
+        jnp.where(to_core[:, None, None] == 0, weight[:, :, 1], weight[:, :, 0]),
+        lax.dynamic_index_in_dim(second, 1 - ring, axis=2, keepdims=False),
     ]
+    for_peer = [a.reshape(exp_local, -1, width) for a in for_peer]
     peer_weight = lax.ppermute(jnp.concatenate(for_peer, axis=1), "core", swap)
 
     ids = routed_expert_index.T
@@ -225,11 +229,11 @@
     act = gate_f * sig
     hidden = (act * up_f).astype(BF)
 
-    first_send = lax.dynamic_index_in_dim(first, 1 - core, axis=1, keepdims=False)
+    first_send = lax.dynamic_index_in_dim(first, 1 - ring, axis=1, keepdims=False)
     peer_pack = lax.ppermute(jnp.concatenate([first_send, hidden], axis=2), "core", swap)
 
     partial = partial_sums(
-        core.astype(jnp.int32),
+        ring.astype(jnp.int32),
         task_slot[:, None],
         (first, hidden),
         peer_pack,
@@ -239,14 +243,15 @@
         rows,
         rows_peer,
     )
-    summed = lax.psum_scatter(partial, "z", scatter_dimension=0, tiled=True)
+    summed = lax.psum_scatter(
+        partial, ("z", "core"), scatter_dimension=0, tiled=True, axis_index_groups=rings
+    )
     summed = lax.optimization_barrier(summed)
     back = summed[:piece].astype(F32).reshape(piece, exp_local, per_expert).transpose(1, 0, 2)
 
     pair_part = jnp.sum(hidden.astype(F32) * back, axis=1).reshape(1, total_slots)
     more = 2 * half // z_width
     small = jnp.concatenate([summed[piece : piece + more], pair_part.astype(BF)])
-    rings = [[2 * z + (z + p) % 2 for z in range(z_width)] for p in range(2)]
     gathered = lax.all_gather(
         small.reshape(-1, 128), ("z", "core"), axis=0, tiled=False, axis_index_groups=rings
     )
@@ -258,12 +263,10 @@
         sides.append((lat_side, ql_side, sums.reshape(exp_local, per_expert)))
     own_side, peer_side = sides
     weight_grad = own_side[2] + peer_side[2]
-    from_core = (lax.axis_index("z") + core + jnp.arange(z_width // 2, dtype=jnp.int32)) % 2
-    from_core = from_core[:, None, None]
     latent, query = (
-        jnp.concatenate(
-            [jnp.where(from_core == 0, a, b), jnp.where(from_core == 0, b, a)]
-        ).reshape(rank, exp_local, per_expert)
+        jnp.where(ring == 0, jnp.concatenate([a, b]), jnp.concatenate([b, a])).reshape(
+            rank, exp_local, per_expert
+        )
         for a, b in zip(own_side[:2], peer_side[:2])
     )
 

time: 148 us -> 149 us (level)
  blocking collectives: 76.8 us -> 74.1 us
  starting transfers between devices: 35.8 us -> 38.3 us
    all_gather x1, blocking collectives: 30.1 us -> 26.3 us  [on_device(): lax.all_gather(small.reshape(-1, 128), ('z', 'core'), axis=0, tiled=False...]
    all_to_all x1, starting transfers between devices: 6.65 us -> 8.96 us  [on_device(): lax.all_to_all(weight_grad.astype(BF).reshape(exp_local, most, source_cou...]
    unnamed x28 -> x30, local copies, waits for them, and re-layouts: 4.3 us -> 4.7 us
  transfers between devices with their start and end apart: 7 -> 7, of which waited for: 2 -> 3; matrix products, arithmetic and copies ran while one was open for 12% -> 12% of each run, Pallas kernels for 0% -> 0%
where the time goes in v9:
time: 149 us; the launch traced here: 148 us
  blocking collectives  74.1 us (50%)
  starting transfers between devices  38.3 us (26%)
  local copies, waits for them, and re-layouts  11.9 us (8%)
  Pallas kernels  7.73 us (5%)
  other arithmetic  5.51 us (4%)
  matrix products  4.76 us (3%)
  waiting for transfers between devices  3.91 us (3%)
  between operations  1.86 us (1%)
    unnamed x1, blocking collectives  47.8 us
    all_gather x1, blocking collectives, on_device(): lax.all_gather(small.reshape(-1, 128), ('z', 'core'), axis=0, tiled=False...  26.3 us
    all_to_all x1, starting transfers between devices, on_device(): lax.all_to_all(send, 'exp', split_axis=0, concat_axis=0, tiled=True)  10.5 us
    ppermute x1, starting transfers between devices, on_device(): lax.ppermute(jnp.concatenate([first_send, hidden], axis=2), 'core', swap)  9.45 us
    all_to_all x1, starting transfers between devices, on_device(): lax.all_to_all(weight_grad.astype(BF).reshape(exp_local, most, source_cou...  8.96 us
    pallas_call x1, Pallas kernels, partial_sums(): pl.pallas_call(kernel, out_shape=jax.ShapeDtypeStruct((z_width * chunk, e...  5.36 us
    unnamed x30, local copies, waits for them, and re-layouts  4.7 us
    unnamed x1, starting transfers between devices  3.09 us
  transfers between devices with their start and end apart: 7, of which 3 were waited for; matrix products, arithmetic and copies ran while one was open for 12% of the time, Pallas kernels for 0%

profile of v9, /device:TPU:1, one launch (start us, length us, event | category | flops | bytes accessed | tf_op | source)
XLA Modules:
  0.0 148.2 jit_solution(2709639172375792430)
XLA Ops:
  0.6 2.4 %dispatch_slab.1 = bf16[32,56,128]{2,1,0:T(8,128)(2,1)} custom-call(s32[8,128]{1,0:T(8,128)} %bitcast.117, bf16[8,128]{1,0:T(8,128)(2,1)} %bitcast.125, s32[1,128]{1,0:T(1,128)} %bitcast.126, bf16[128,128]{1,0:T(8,128)(2,1)} %grad_ref.1), custom_call_target="tpu_custom_call" | custom-call | tf_op jit(solution)/shard_map/dispatch_slab/pallas_call | solution.py:138
  3.0 10.5 %all-to-all-start = ((bf16[32,56,128]{2,1,0:T(8,128)(2,1)}), bf16[32,56,128]{2,1,0:T(8,128)(2,1)S(1)}, u32[]{:S(2)}, u32[]{:S(2)}) async-start(bf16[32,56,128]{2,1,0:T(8,128)(2,1)} %dispatch_slab.1), calls=%async_computation | async-start | bytes 917504 | tf_op jit(solution)/shard_map/all_to_all | solution.py:200
  13.5 1.3 copy.62
  14.8 0.5 copy.63
  15.3 0.5 reshape.166.a_ref
  15.8 1.2 convert_element_type.192
  17.0 0.2 copy.65
  17.3 1.1 convert_element_type.193
  18.4 1.0 copy.66
  19.3 1.1 multiply_convert_fusion.19.h_ref
  20.4 9.4 %collective-permute-start = (bf16[4,48,640]{2,1,0:T(8,128)(2,1)S(1)}, bf16[4,48,640]{2,1,0:T(8,128)(2,1)S(1)}, u32[]{:S(2)}, u32[]{:S(2)}) collective-permute-start(bf16[4,48,640]{2,1,0:T(8,128)(2,1)S(1)} %pad_maximum_fusion.1), channel_id=1, source_target_pairs={{0,1},{1,0},{2,3},{3,2},{4,5},{5,4},{6,7},{7,6},{8,9},{9,8},{10,11... | collective-permute-start | bytes 737288 | tf_op jit(solution)/shard_map/ppermute | solution.py:233
  29.9 0.1 broadcast_in_dim.66
  30.0 0.1 broadcast_in_dim.67
  30.1 0.1 fusion.32
  30.2 0.4 bitcast_select_fusion
  30.6 0.5 copy-done.7
  31.1 0.1 pad_maximum_fusion
  31.2 1.9 %collective-permute-start.1 = (bf16[4,1024,128]{2,1,0:T(8,128)(2,1)S(1)}, bf16[4,1024,128]{2,1,0:T(8,128)(2,1)}, u32[]{:S(2)}, u32[]{:S(2)}) collective-permute-start(bf16[4,1024,128]{2,1,0:T(8,128)(2,1)S(1)} %pad_maximum_fusion), channel_id=1, source_target_pairs={{0,1},{1,0},{2,3},{3,2},{4,5},{5,4},{6,7},{7,6},{8,9},{9,8},{10,11... | collective-permute-start | bytes 3145736 | tf_op jit(solution)/shard_map/ppermute | solution.py:181
  33.2 1.3 dynamic-slice.4
  35.1 0.1 fusion.16
  35.2 0.1 fusion.25
  35.3 0.1 select_reduce_fusion.2
  35.4 0.1 copy.67
  35.6 2.4 %collective-permute-start.2 = (bf16[4,384,128]{2,1,0:T(8,128)(2,1)S(1)}, bf16[4,384,128]{2,1,0:T(8,128)(2,1)S(1)}, u32[]{:S(2)}, u32[]{:S(2)}) collective-permute-start(bf16[4,384,128]{2,1,0:T(8,128)(2,1)S(1)} %bitcast.105), channel_id=1, source_target_pairs={{0,1},{1,0},{2,3},{3,2},{4,5},{5,4},{6,7},{7,6},{8,9},{9,8},{10,11... | collective-permute-start | bytes 1179656 | tf_op jit(solution)/shard_map/ppermute | solution.py:203
  38.0 0.1 fusion.27
  38.2 0.6 select_reduce_fusion.1
  38.8 0.1 eq.89
  38.9 0.7 broadcast_in_dim_reshape.3.t_ref
  39.6 0.7 copy-done.10
  40.3 0.1 copy-done.9
  40.4 5.4 %partial_sums.1 = bf16[880,1536]{1,0:T(8,128)(2,1)} custom-call(s32[1]{0:T(128)} %bitcast.6.core_ref, f32[4,1,384]{2,1,0:T(1,128)} %broadcast_in_dim_reshape.3.t_ref, bf16[4,2,48,256]{3,2,1,0:T(8,128)(2,1)} %copy-done.5, bf16[4,48,384]{2,1,0:T(8,128)(2,1)} %copy-done.1, bf16[4,48,640]{2,1,0:T(8,128)(2,1)} %copy-done.10, ...), custom_call_target="tpu_custom_call" | custom-call | tf_op jit(solution)/shard_map/partial_sums/pallas_call | solution.py:64
  45.8 47.8 %fusion = bf16[56,1536]{1,0:T(8,128)(2,1)S(1)} fusion(bf16[880,1536]{1,0:T(8,128)(2,1)} %partial_sums.1), kind=kCustom, calls=%all-reduce-scatter | all-reduce-scatter fusion | flops 1376257 | bytes 2879488
  93.7 3.1 %collective-permute-start.4 = (bf16[15,1536]{1,0:T(8,128)(2,1)S(1)}, bf16[15,1536]{1,0:T(8,128)(2,1)S(1)}, u32[]{:S(2)}, u32[]{:S(2)}) collective-permute-start(bf16[15,1536]{1,0:T(8,128)(2,1)S(1)} %slice.65), channel_id=1, source_target_pairs={{0,3},{3,4},{4,7},{7,8},{8,11},{11,12},{12,15},{15,16},{16,19},{19... | collective-permute-start | bytes 138248
  96.7 0.1 compare_convert_fusion
  96.8 0.1 mul.86
  96.9 1.2 collective-permute-done.4
  98.1 0.2 concatenate.28
  98.3 0.1 constant_dynamic-slice_fusion
  98.6 26.3 %all_gather.3 = bf16[16,60,128]{2,1,0:T(8,128)(2,1)S(1)} all-gather(bf16[1,60,128]{2,1,0:T(8,128)(2,1)S(1)} %all_gather_reshape.3), channel_id=1, replica_groups={{0,3,4,7,8,11,12,15,16,19,20,23,24,27,28,31},{1,2,5,6,9,10,13,14,17,18,..., dimensions={0}, use_global_device_ids=true | all-gather | bytes 261120 | tf_op jit(solution)/shard_map/all_gather | solution.py:255
  124.9 2.0 %collective-permute-start.3 = (bf16[16,60,128]{2,1,0:T(8,128)(2,1)S(1)}, bf16[16,60,128]{2,1,0:T(8,128)(2,1)S(1)}, u32[]{:S(2)}, u32[]{:S(2)}) collective-permute-start(bf16[16,60,128]{2,1,0:T(8,128)(2,1)S(1)} %all_gather.3), channel_id=1, source_target_pairs={{0,1},{1,0},{2,3},{3,2},{4,5},{5,4},{6,7},{7,6},{8,9},{9,8},{10,11... | collective-permute-start | bytes 737288 | tf_op jit(solution)/shard_map/ppermute | solution.py:259
  126.9 0.3 reshape.179
  127.2 0.1 slice_reduce_fusion.1
  127.3 0.1 multiply_reduce_fusion.1
  127.4 0.9 collective-permute-done.3
  128.3 0.3 reshape.180
  128.6 0.1 slice_reduce_fusion
  128.7 0.1 multiply_reduce_fusion
  128.8 0.1 convert_element_type.185
  128.9 0.7 copy.76
  129.6 9.0 %all-to-all-start.1 = ((bf16[32,4,12]{2,1,0:T(4,128)(2,1)}), bf16[32,4,12]{2,1,0:T(4,128)(2,1)S(1)}, u32[]{:S(2)}, u32[]{:S(2)}) async-start(bf16[32,4,12]{2,1,0:T(4,128)(2,1)} %copy.76), calls=%async_computation.1 | async-start | bytes 65536 | tf_op jit(solution)/shard_map/all_to_all | solution.py:273
  138.6 0.2 maximum_select_fusion
  138.8 0.2 select_n.78
  139.1 0.2 select_n.80
  139.3 0.1 fusion.23
  139.5 0.2 copy-done.6
  139.8 0.1 copy-done.8
  139.9 0.5 multiply_convert_fusion.17
  140.4 0.1 copy-done.4
  140.5 1.4 fusion.10
  141.9 1.9 %fusion.12 = bf16[4,8,48,64]{3,2,1,0:T(8,128)(2,1)} fusion(f32[64,4,384]{2,0,1:T(8,128)S(1)} %copy.70, f32[8,4,384]{2,0,1:T(8,128)S(1)} %compare_convert_fusion, bf16[4,48,384]{2,1,0:T(8,128)(2,1)S(1)} %copy-done.2), kind=kOutput, calls=%fused_computation.13 | convolution fusion | flops 77168640 | bytes 786432 | tf_op jit(solution)/shard_map/tres,efs->etfr/dot_general | solution.py:287
  143.7 0.9 copy.74
  144.7 0.9 copy.73
  145.6 1.8 %all-to-all-done.1 = bf16[32,4,12]{2,1,0:T(4,128)(2,1)S(1)} async-done(((bf16[32,4,12]{2,1,0:T(4,128)(2,1)}), bf16[32,4,12]{2,1,0:T(4,128)(2,1)S(1)}, u32[]{:S(2)}, u32[]{:S(2)}) %all-to-all-start.1) | async-done | bytes 3104 | tf_op jit(solution)/shard_map/all_to_all | solution.py:273
  147.4 0.8 fusion.15
  (44 shorter events, 0.5 us)
Async XLA Ops:
  3.0 32.4 %all-to-all-start = ((bf16[32,56,128]{2,1,0:T(8,128)(2,1)}), bf16[32,56,128]{2,1,0:T(8,128)(2,1)S(1)}, u32[]{:S(2)}, u32[]{:S(2)}) async-start(bf16[32,56,128]{2,1,0:T(8,128)(2,1)} %dispatch_slab.1), calls=%async_computation | async-start | bytes 917504 | tf_op jit(solution)/shard_map/all_to_all | solution.py:200
  15.8 4.6 %copy-start.5 = (bf16[4,2,48,256]{3,2,1,0:T(8,128)(2,1)}, bf16[4,2,48,256]{3,2,1,0:T(8,128)(2,1)S(1)}, u32[]{:S(2)}) copy-start(bf16[4,2,48,256]{3,2,1,0:T(8,128)(2,1)S(1)} %reshape.166.a_ref) | copy-start | bytes 589828
  15.8 14.3 %copy-start = (bf16[4,1536,128]{2,1,0:T(8,128)(2,1)S(1)}, bf16[4,1536,128]{2,1,0:T(8,128)(2,1)}, u32[]{:S(2)}) copy-start(bf16[4,1536,128]{2,1,0:T(8,128)(2,1)} %param.15) | copy-start | bytes 4718596
  20.4 10.2 %copy-start.1 = (bf16[4,48,384]{2,1,0:T(8,128)(2,1)}, bf16[4,48,384]{2,1,0:T(8,128)(2,1)S(1)}, u32[]{:S(2)}) copy-start(bf16[4,48,384]{2,1,0:T(8,128)(2,1)S(1)} %multiply_convert_fusion.19.h_ref) | copy-start | bytes 442372
  20.4 19.2 %collective-permute-start = (bf16[4,48,640]{2,1,0:T(8,128)(2,1)S(1)}, bf16[4,48,640]{2,1,0:T(8,128)(2,1)S(1)}, u32[]{:S(2)}, u32[]{:S(2)}) collective-permute-start(bf16[4,48,640]{2,1,0:T(8,128)(2,1)S(1)} %pad_maximum_fusion.1), channel_id=1, source_target_pairs={{0,1},{1,0},{2,3},{3,2},{4,5},{5,4},{6,7},{7,6},{8,9},{9,8},{10,11... | collective-permute-start | bytes 737288 | tf_op jit(solution)/shard_map/ppermute | solution.py:233
  30.1 1.0 copy-start.7
  30.2 4.9 %copy-start.11 = (s32[128,8]{0,1:T(8,128)S(1)}, s32[128,8]{0,1:T(8,128)}, u32[]{:S(2)}) copy-start(s32[128,8]{0,1:T(8,128)} %param.10) | copy-start | bytes 12292
  31.2 8.4 %collective-permute-start.1 = (bf16[4,1024,128]{2,1,0:T(8,128)(2,1)S(1)}, bf16[4,1024,128]{2,1,0:T(8,128)(2,1)}, u32[]{:S(2)}, u32[]{:S(2)}) collective-permute-start(bf16[4,1024,128]{2,1,0:T(8,128)(2,1)S(1)} %pad_maximum_fusion), channel_id=1, source_target_pairs={{0,1},{1,0},{2,3},{3,2},{4,5},{5,4},{6,7},{7,6},{8,9},{9,8},{10,11... | collective-permute-start | bytes 3145736 | tf_op jit(solution)/shard_map/ppermute | solution.py:181
  35.6 4.1 %copy-start.3 = (bf16[48,32,128]{2,1,0:T(8,128)(2,1)}, bf16[48,32,128]{2,1,0:T(8,128)(2,1)S(1)}, u32[]{:S(2)}) copy-start(bf16[48,32,128]{2,1,0:T(8,128)(2,1)S(1)} %copy.67) | copy-start | bytes 1179652
  35.6 4.0 %collective-permute-start.2 = (bf16[4,384,128]{2,1,0:T(8,128)(2,1)S(1)}, bf16[4,384,128]{2,1,0:T(8,128)(2,1)S(1)}, u32[]{:S(2)}, u32[]{:S(2)}) collective-permute-start(bf16[4,384,128]{2,1,0:T(8,128)(2,1)S(1)} %bitcast.105), channel_id=1, source_target_pairs={{0,1},{1,0},{2,3},{3,2},{4,5},{5,4},{6,7},{7,6},{8,9},{9,8},{10,11... | collective-permute-start | bytes 1179656 | tf_op jit(solution)/shard_map/ppermute | solution.py:203
  39.6 0.7 copy-start.10
  39.6 0.8 copy-start.9
  45.8 52.7 %copy-start.2 = (bf16[4,48,384]{2,1,0:T(8,128)(2,1)S(1)}, bf16[4,48,384]{2,1,0:T(8,128)(2,1)}, u32[]{:S(2)}) copy-start(bf16[4,48,384]{2,1,0:T(8,128)(2,1)} %copy-done.1) | copy-start | bytes 442372
  93.7 4.5 %collective-permute-start.4 = (bf16[15,1536]{1,0:T(8,128)(2,1)S(1)}, bf16[15,1536]{1,0:T(8,128)(2,1)S(1)}, u32[]{:S(2)}, u32[]{:S(2)}) collective-permute-start(bf16[15,1536]{1,0:T(8,128)(2,1)S(1)} %slice.65), channel_id=1, source_target_pairs={{0,3},{3,4},{4,7},{7,8},{8,11},{11,12},{12,15},{15,16},{16,19},{19... | collective-permute-start | bytes 138248
  124.9 3.4 %collective-permute-start.3 = (bf16[16,60,128]{2,1,0:T(8,128)(2,1)S(1)}, bf16[16,60,128]{2,1,0:T(8,128)(2,1)S(1)}, u32[]{:S(2)}, u32[]{:S(2)}) collective-permute-start(bf16[16,60,128]{2,1,0:T(8,128)(2,1)S(1)} %all_gather.3), channel_id=1, source_target_pairs={{0,1},{1,0},{2,3},{3,2},{4,5},{5,4},{6,7},{7,6},{8,9},{9,8},{10,11... | collective-permute-start | bytes 737288 | tf_op jit(solution)/shard_map/ppermute | solution.py:259
  129.6 17.7 %all-to-all-start.1 = ((bf16[32,4,12]{2,1,0:T(4,128)(2,1)}), bf16[32,4,12]{2,1,0:T(4,128)(2,1)S(1)}, u32[]{:S(2)}, u32[]{:S(2)}) async-start(bf16[32,4,12]{2,1,0:T(4,128)(2,1)} %copy.76), calls=%async_computation.1 | async-start | bytes 65536 | tf_op jit(solution)/shard_map/all_to_all | solution.py:273
  138.8 1.0 copy-start.6
  138.8 1.1 copy-start.8
  139.5 1.1 copy-start.4
